TPU v7x, 32 devices: a whole 2x2x4 slice. The times are simulated.
32 devices in a mesh: outer: 4 (over y, x), inner: 2 (over core), mp: 4 (over z).
Axes of the slice: x: 2, y: 2, z: 4, core: 2. Of those that a mesh axis runs over, the one named last changes fastest.
Arguments:
- inputs: bfloat16 [16384, 4096], P(('outer', 'inner'), 'mp'), may hold values from -6 to 6
- log_decay: float32 [64, 16384], P('mp', ('outer', 'inner')), may hold values from -2.5 to 0, as said below
- write_keys: bfloat16 [16384, 128], P(('outer', 'inner')), may hold values from -6 to 6
- read_keys: bfloat16 [16384, 128], P(('outer', 'inner')), may hold values from -0.5 to 0.5
- skip_gain: float32 [64], P('mp'), may hold values from 0.5 to 1.5
- grad_out: bfloat16 [16384, 4096], P(('outer', 'inner'), 'mp'), may hold values from -0.75 to 0.75
Outputs:
- mixed_out: bfloat16 [16384, 4096], P(('outer', 'inner'), 'mp')
- grad_inputs: bfloat16 [16384, 4096], P(('outer', 'inner'), 'mp')
- grad_write: float32 [16384, 128], P(('outer', 'inner', 'mp'))
- grad_read: float32 [16384, 128], P(('outer', 'inner', 'mp'))
Inputs may be any that keep to these rules, and one draw needn't show every extreme that they name: `log_decay`: strictly negative.
All inputs are finite; a program needn't handle non-finite values.
Results may differ from a plain program's by a relative error of at most 0.0055.
Values sent between devices are 32-bit elements; how exact they have to be, the bound alone decides.
No kernel may reach another device: no remote copies, remote signals or barrier semaphores. Data moves between devices by JAX's collectives and lax.ppermute only.
A program may use at most 192 MiB of HBM per device.

v0:
```python
import jax
import jax.numpy as jnp
from jax import lax
from jax.sharding import PartitionSpec as P

Q = 256


def carried_in(x, axis, combine, identity, reverse):
    devices, here = (lax.axis_size(axis), lax.axis_index(axis))
    everything = jax.tree.map(lambda part: lax.all_gather(part, axis), x)
    start = jax.tree.map(
        lambda part, zero: jnp.broadcast_to(jnp.asarray(zero, part.dtype), part.shape), x, identity
    )

    def step(k, before):
        at = devices - 1 - k if reverse else k
        reached = at > here if reverse else at < here
        new = combine(before, jax.tree.map(lambda part: part[at], everything))
        return jax.tree.map(lambda a, b: jnp.where(reached, a, b), new, before)

    return lax.fori_loop(0, devices, step, start)


def link(earlier, later):
    first_decay, first_state = earlier
    second_decay, second_state = later
    return (first_decay * second_decay, second_decay[..., None, None] * first_state + second_state)


def chain(element, backward):
    identity = (jnp.ones_like(element[0]), jnp.zeros_like(element[1]))
    return carried_in((element[0], element[1]), ("outer", "inner"), link, identity, backward)


def within(decay, terms, backward):
    identity = (jnp.ones_like(decay[0]), jnp.zeros_like(terms[0]))

    def advance(carry, element):
        return (link(carry, element), carry)

    final, prefix = lax.scan(advance, identity, (decay, terms), reverse=backward)
    return (final, prefix)


def on_device(inputs, log_decay, write_keys, read_keys, skip_gain, grad_out):
    heads = log_decay.shape[0]
    length = log_decay.shape[1]
    width = inputs.shape[1] // heads
    states = write_keys.shape[1]
    count = length // Q
    cumulative = jnp.cumsum(log_decay.reshape(heads, count, Q), axis=2).transpose(1, 0, 2)
    gain = jnp.sqrt(-jnp.expm1(2.0 * log_decay)).reshape(heads, count, Q).transpose(1, 2, 0)
    input_blocks = inputs.reshape(count, Q, heads, width)
    grad_blocks = grad_out.reshape(count, Q, heads, width)
    scaled = (input_blocks * gain[..., None]).astype(jnp.bfloat16)
    write_blocks = write_keys.reshape(count, Q, states)
    read_blocks = read_keys.reshape(count, Q, states)
    tails = jnp.exp(cumulative[:, :, -1:] - cumulative)
    leads = jnp.exp(cumulative)
    block_decay = jnp.exp(cumulative[:, :, -1])
    weighted_write = (tails[..., None] * write_blocks.astype(jnp.float32)[:, None]).astype(
        jnp.bfloat16
    )
    weighted_read = (leads[..., None] * read_blocks.astype(jnp.float32)[:, None]).astype(
        jnp.bfloat16
    )
    lower = jnp.arange(Q)[:, None] >= jnp.arange(Q)[None, :]
    pushes = jnp.einsum(
        "chjn,cjhp->chnp", weighted_write, scaled, preferred_element_type=jnp.float32
    )
    pulls = jnp.einsum(
        "chkn,ckhp->chnp", weighted_read, grad_blocks, preferred_element_type=jnp.float32
    )
    device_total, block_prefix = within(block_decay, pushes, False)
    device_entry = chain(device_total, False)
    entries = link(device_entry, block_prefix)[1].astype(jnp.bfloat16)
    device_back, block_suffix = within(block_decay, pulls, True)
    device_after = chain(device_back, True)
    afters = link(device_after, block_suffix)[1].astype(jnp.bfloat16)

    def intra(item):
        scaled_b, grad_b, write_b, read_b, cum_b = item
        scores = jnp.dot(read_b, write_b.T, preferred_element_type=jnp.float32)
        gaps = jnp.where(lower[None], cum_b[:, :, None] - cum_b[:, None, :], -jnp.inf)
        decay = jnp.exp(gaps)
        mixing = (scores[None] * decay).astype(jnp.bfloat16)
        out_intra = jnp.einsum("hij,jhp->ihp", mixing, scaled_b, preferred_element_type=jnp.float32)
        back_intra = jnp.einsum("hki,khp->ihp", mixing, grad_b, preferred_element_type=jnp.float32)
        pairs = jnp.einsum("khp,ihp->hki", grad_b, scaled_b, preferred_element_type=jnp.float32)
        paired = (pairs * decay).astype(jnp.bfloat16)
        write_intra = jnp.einsum("hki,kn->in", paired, read_b, preferred_element_type=jnp.float32)
        read_intra = jnp.einsum("hij,jn->in", paired, write_b, preferred_element_type=jnp.float32)
        return (out_intra, back_intra, write_intra, read_intra)

    out_intra, back_intra, write_intra, read_intra = lax.map(
        intra, (scaled, grad_blocks, write_blocks, read_blocks, cumulative)
    )
    out_carry = jnp.einsum(
        "chin,chnp->cihp", weighted_read, entries, preferred_element_type=jnp.float32
    )
    back_carry = jnp.einsum(
        "chin,chnp->cihp", weighted_write, afters, preferred_element_type=jnp.float32
    )
    write_heads = jnp.einsum("cihp,chnp->chin", scaled, afters, preferred_element_type=jnp.float32)
    read_heads = jnp.einsum(
        "cihp,chnp->chin", grad_blocks, entries, preferred_element_type=jnp.float32
    )
    write_carry = jnp.sum(tails[..., None] * write_heads, axis=1)
    read_carry = jnp.sum(leads[..., None] * read_heads, axis=1)
    skip_scale = skip_gain[None, None, :, None]
    mixed = (out_intra + out_carry + skip_scale * input_blocks).astype(jnp.bfloat16)
    grad_in = (gain[..., None] * (back_intra + back_carry) + skip_scale * grad_blocks).astype(
        jnp.bfloat16
    )
    write_terms = (write_intra + write_carry).reshape(length, states)
    read_terms = (read_intra + read_carry).reshape(length, states)
    grad_write, grad_read = (
        lax.psum_scatter(write_terms, "mp", scatter_dimension=0, tiled=True),
        lax.psum_scatter(read_terms, "mp", scatter_dimension=0, tiled=True),
    )
    return (
        mixed.reshape(length, heads * width),
        grad_in.reshape(length, heads * width),
        grad_write,
        grad_read,
    )


def solution(mesh):
    placed = (
        P(("outer", "inner"), "mp"),
        P("mp", ("outer", "inner")),
        P(("outer", "inner"), None),
        P(("outer", "inner"), None),
        P("mp"),
        P(("outer", "inner"), "mp"),
    )
    return jax.shard_map(
        on_device,
        mesh=mesh,
        in_specs=placed,
        out_specs=(
            P(("outer", "inner"), "mp"),
            P(("outer", "inner"), "mp"),
            P(("outer", "inner", "mp"), None),
            P(("outer", "inner", "mp"), None),
        ),
        check_vma=False,
    )
```

profile of v0, /device:TPU:0, one launch (start us, length us, event | category | flops | bytes accessed | tf_op | source)
XLA Modules:
  0.0 399.3 jit_solution(17688622117670059925)
XLA Ops:
  8.3 9.0 %reduce-window.6 = f32[16,8,2,128]{3,1,2,0:T(8,128)S(1)} reduce-window(f32[16,8,2,128]{3,1,2,0:T(8,128)S(1)} %copy.86, f32[]{:T(128)} %constant.158.clone.1), window={size=1x1x1x128 pad=0_0x0_0x0_0x127_0}, to_apply=%region_0.0 | reduce-window | flops 4161536 | bytes 262148 | tf_op jit(solution)/shard_map/reduce-window
  17.8 11.6 %reshape.105 = bf16[8,256,16,64]{3,2,1,0:T(8,128)(2,1)} reshape(bf16[2048,1024]{1,0:T(8,128)(2,1)} %param.21) | data formatting | bytes 8388608 | tf_op jit(solution)/shard_map/reshape | solution.py:55
  29.5 10.4 %copy.91 = bf16[8,256,16,64]{1,3,2,0:T(8,128)(2,1)} copy(bf16[8,256,16,64]{3,2,1,0:T(8,128)(2,1)} %reshape.105) | data formatting | bytes 8388608
  40.2 12.5 %fusion.55 = f32[8,16,128,64]{3,2,1,0:T(8,128)} fusion(bf16[8,256,16,64]{1,3,2,0:T(8,128)(2,1)} %copy.91, f32[8,256,128]{2,1,0:T(8,128)S(1)} %convert_element_type.61, f32[8,16,256]{2,1,0:T(8,128)S(1)} %copy.98), kind=kOutput, calls=%fused_computation.81 | convolution fusion | flops 545259520 | bytes 9568256 | tf_op jit(solution)/shard_map/chkn,ckhp->chnp/dot_general | solution.py:72
  52.7 4.3 %broadcast.39.clone.1 = f32[8,16,128,64]{3,2,1,0:T(8,128)} broadcast(f32[]{:T(128)} %constant.158.clone.1), dimensions={} | broadcast | bytes 4194308 | tf_op jit(solution)/shard_map/broadcast.8
  57.0 20.5 %while.88 = (s32[]{:T(128)}, f32[16]{0:T(128)S(1)}, f32[16,128,64]{2,1,0:T(8,128)S(1)}, f32[8,16]{1,0:T(8,128)S(1)}, f32[8,16,128,64]{3,2,1,0:T(8,128)}, /*index...) while((s32[]{:T(128)}, f32[16]{0:T(128)S(1)}, ...), condition=%wide.region_10.11_spmd.clone, body=%wide.region_9.10_spmd.clone.sunk | while | flops 524324 | bytes 3146389 | solution.py:42
  79.0 12.3 %reshape.104 = f32[8,256,16,64]{3,2,1,0:T(8,128)} reshape(bf16[2048,1024]{1,0:T(8,128)(2,1)} %param.16) | data formatting | bytes 12582912 | tf_op jit(solution)/shard_map/convert_element_type | solution.py:56
  91.3 14.0 %copy.85 = f32[8,256,16,64]{1,3,2,0:T(8,128)} copy(f32[8,256,16,64]{3,2,1,0:T(8,128)} %reshape.104) | data formatting | bytes 16777216 | tf_op jit(solution)/shard_map/convert_element_type | solution.py:56
  105.5 5.1 %multiply_convert_fusion.18 = bf16[8,256,16,64]{1,3,2,0:T(8,128)(2,1)S(1)} fusion(f32[8,256,16,64]{1,3,2,0:T(8,128)} %copy.85, f32[8,256,16]{1,2,0:T(8,128)S(1)} %bitcast.179), kind=kLoop, calls=%fused_computation.100 | loop fusion | flops 4194304 | bytes 12713984 | tf_op jit(solution)/shard_map/convert_element_type | solution.py:56
  110.7 11.9 %fusion.54 = f32[8,16,128,64]{3,2,1,0:T(8,128)} fusion(bf16[8,256,16,64]{1,3,2,0:T(8,128)(2,1)S(1)} %multiply_convert_fusion.18, f32[8,256,128]{2,1,0:T(8,128)S(1)} %convert_element_type.58, f32[8,16,256]{2,1,0:T(8,128)S(1)} %copy.94), kind=kOutput, calls=%fused_computation.80 | convolution fusion | flops 545259520 | bytes 9568256 | tf_op jit(solution)/shard_map/chjn,cjhp->chnp/dot_general | solution.py:69
  122.6 4.3 %broadcast.39.clone = f32[8,16,128,64]{3,2,1,0:T(8,128)} broadcast(f32[]{:T(128)} %constant.158.clone.1), dimensions={} | broadcast | bytes 4194308 | tf_op jit(solution)/shard_map/broadcast.8
  126.9 20.6 %while.86 = (s32[]{:T(128)}, f32[16]{0:T(128)S(1)}, f32[16,128,64]{2,1,0:T(8,128)S(1)}, f32[8,16]{1,0:T(8,128)S(1)}, f32[8,16,128,64]{3,2,1,0:T(8,128)}, /*index...) while((s32[]{:T(128)}, f32[16]{0:T(128)S(1)}, ...), condition=%wide.region_6.7_spmd.clone, body=%wide.region_5.6_spmd.clone.sunk | while | flops 524323 | bytes 3146369 | solution.py:42
  148.9 87.7 %while.85 = (s32[]{:T(128)}, f32[8,256,16,64]{1,3,2,0:T(8,128)}, f32[8,256,16,64]{1,3,2,0:T(8,128)}, f32[8,256,128]{2,1,0:T(8,128)}, f32[8,256,128]{1,2,0:T(8,12...) while((s32[]{:T(128)}, f32[8,256,16,64]{1,3,2,0:T(8,128)}, ...), condition=%wide.region_4.5_spmd.clone, body=%wide.region_2.4_spmd.clone.sunk | while | flops 467664896 | bytes 6330489 | solution.py:96
  238.3 15.6 %all-reduce.2 = (f32[128]{0:T(128)S(1)}, f32[128]{0:T(128)S(1)}) all-reduce(f32[128]{0:T(128)S(1)} %dynamic-update-slice, f32[128]{0:T(128)S(1)} %dynamic-update-slice.1), channel_id=2, replica_groups=mesh['outer'=4,'inner'=2,'mp'=4] {'outer','inner'}, use_global_device_ids=true, to_apply=%add | all-reduce | flops 256 | bytes 2048
  254.1 13.8 %while.89 = (s32[]{:T(128)}, f32[16,128,64]{2,1,0:T(8,128)S(1)}, s32[]{:T(128)}, f32[8,16]{1,0:T(8,128)S(1)}, f32[8,16,128,64]{2,3,1,0:T(8,128)}, /*index=5*/s32[]{:T(128)}, s32[]{:T(128)}, s32[]{:T(128)}, s32[]{:T(128)}) while((s32[]{:T(128)}, f32[16,128,64]{2,1,0:T(8,128)S(1)}, s32[]{:T(128)}, f32[8,16]{1,0:T(8,128)S(1)}, ...), condition=%wide.region_12.13_spmd.clone, body=%wide.region_11.12_spmd.clone.sunk | while | flops 524296 | bytes 3670383 | solution.py:22
  267.9 9.8 %multiply_reduce_fusion.1 = f32[8,256,128]{2,1,0:T(8,128)S(1)} fusion(bf16[8,256,16,64]{1,3,2,0:T(8,128)(2,1)} %get-tuple-element.1163, f32[8,16,256]{2,1,0:T(8,128)S(1)} %copy.94, f32[8,16,128,64]{3,2,1,0:T(8,128)} %get-tuple-element.485, f32[16,128,64]{2,1,0:T(8,128)S(1)} %get-tuple-element.484, f32[8,16]{1,0:T(8,128)S(1)} %get-tuple-element.481), kind=kOutput, calls=%fused_computation.76 | convolution fusion | flops 548143104 | bytes 10093056 | tf_op jit(solution)/shard_map/cihp,chnp->chin/dot_general | solution.py:105
  278.9 29.9 %while.87 = (s32[]{:T(128)}, f32[16,128,64]{2,1,0:T(8,128)}, s32[]{:T(128)}, f32[8,16]{1,0:T(8,128)S(1)}, f32[8,16,128,64]{2,3,1,0:T(8,128)}, /*index=5*/s32[]{:T(128)}, s32[]{:T(128)}) while((s32[]{:T(128)}, f32[16,128,64]{2,1,0:T(8,128)}, s32[]{:T(128)}, f32[8,16]{1,0:T(8,128)S(1)}, f32[8,16,128,64]{2,3,1,0:T(8,128)}, ...), condition=%wide.region_8.9_spmd.clone, body=%wide.region_7.8_spmd.clone.sunk | while | flops 524292 | bytes 3670321 | solution.py:22
  308.8 7.5 %multiply_reduce_fusion = f32[8,128,256]{2,1,0:T(8,128)S(1)} fusion(bf16[8,256,16,64]{1,3,2,0:T(8,128)(2,1)} %get-tuple-element.1164, f32[8,16,256]{2,1,0:T(8,128)S(1)} %copy.98, f32[8,16,128,64]{3,2,1,0:T(8,128)} %get-tuple-element.479, f32[16,128,64]{2,1,0:T(8,128)} %get-tuple-element.478, f32[8,16]{1,0:T(8,128)S(1)} %get-tuple-element.475), kind=kOutput, calls=%fused_computation.75 | convolution fusion | flops 548143104 | bytes 10093056 | tf_op jit(solution)/shard_map/cihp,chnp->chin/dot_general | solution.py:106
  320.2 13.8 %fusion.61 = bf16[8,256,16,64]{1,3,2,0:T(8,128)(2,1)} fusion(f32[8,256,16,64]{1,3,2,0:T(8,128)} %get-tuple-element.474, f32[8,256,16,64]{1,3,2,0:T(8,128)} %copy.85, f32[16]{0:T(128)S(1)} %copy-done.11, f32[8,256,128]{2,1,0:T(8,128)S(1)} %copy-done.3, f32[8,16,256]{2,1,0:T(8,128)S(1)} %copy.98, f32[8,16,128,64]{3,2,1,0:T(8,128)} %get-tuple-element.479, ...), kind=kOutput, calls=%fused_computation.89 | convolution fusion | flops 556793856 | bytes 26870336 | tf_op jit(solution)/shard_map/chin,chnp->cihp/dot_general | solution.py:99
  334.0 10.9 %copy.124 = bf16[8,256,16,64]{3,2,1,0:T(8,128)(2,1)} copy(bf16[8,256,16,64]{1,3,2,0:T(8,128)(2,1)} %fusion.61) | data formatting | bytes 8388608
  344.9 12.0 %reshape.102 = bf16[2048,1024]{1,0:T(8,128)(2,1)} reshape(bf16[8,256,16,64]{3,2,1,0:T(8,128)(2,1)} %copy.124) | data formatting | bytes 8388608
  356.9 13.0 %fusion.59 = bf16[8,256,16,64]{1,3,2,0:T(8,128)(2,1)} fusion(f32[8,256,16,64]{1,3,2,0:T(8,128)} %get-tuple-element.480, bf16[8,256,16,64]{1,3,2,0:T(8,128)(2,1)} %get-tuple-element.1164, f32[16]{0:T(128)S(1)} %copy-done.11, f32[8,256,16]{1,2,0:T(8,128)S(1)} %bitcast.180, f32[8,256,128]{2,1,0:T(8,128)S(1)} %copy-done.5, f32[8,16,256]{2,1,0:T(8,128)S(1)} %copy.94, ...), kind=kOutput, calls=%fused_computation.86 | convolution fusion | flops 560988160 | bytes 22807104 | tf_op jit(solution)/shard_map/chin,chnp->cihp/dot_general | solution.py:102
  369.9 10.9 %copy.125 = bf16[8,256,16,64]{3,2,1,0:T(8,128)(2,1)} copy(bf16[8,256,16,64]{1,3,2,0:T(8,128)(2,1)} %fusion.59) | data formatting | bytes 8388608
  380.9 11.9 %reshape.103 = bf16[2048,1024]{1,0:T(8,128)(2,1)} reshape(bf16[8,256,16,64]{3,2,1,0:T(8,128)(2,1)} %copy.125) | data formatting | bytes 8388608
  (281 shorter events, 182.3 us)
Async XLA Ops:
  7.2 247.0 %all-gather.9.cloned.1.call-start = ((), (), s32[]{:S(2)}) async-start(), calls=%async_computation.5 | async-start | bytes 4718592 | tf_op jit(solution)/shard_map/all_gather | solution.py:11
  29.5 10.4 %copy-start.6 = (bf16[2048,128]{1,0:T(8,128)(2,1)S(1)}, bf16[2048,128]{1,0:T(8,128)(2,1)}, u32[]{:S(2)}) copy-start(bf16[2048,128]{1,0:T(8,128)(2,1)} %param.19) | copy-start | bytes 1572868
  39.9 17.1 %copy-start.2 = (f32[8,256,128]{2,1,0:T(8,128)}, f32[8,256,128]{2,1,0:T(8,128)S(1)}, u32[]{:S(2)}) copy-start(f32[8,256,128]{2,1,0:T(8,128)S(1)} %convert_element_type.61) | copy-start | bytes 3145732
  57.0 21.7 %copy-start.10 = (f32[16,2048]{1,0:T(8,128)S(1)}, f32[16,2048]{1,0:T(8,128)}, u32[]{:S(2)}) copy-start(f32[16,2048]{1,0:T(8,128)} %param.17) | copy-start | bytes 393220
  78.7 200.3 %all-gather.7.cloned.1.call-start = ((), (), s32[]{:S(2)}) async-start(), calls=%async_computation.4 | async-start | bytes 4718592 | tf_op jit(solution)/shard_map/all_gather | solution.py:11
  91.3 14.0 %copy-start.7 = (bf16[2048,128]{1,0:T(8,128)(2,1)S(1)}, bf16[2048,128]{1,0:T(8,128)(2,1)}, u32[]{:S(2)}) copy-start(bf16[2048,128]{1,0:T(8,128)(2,1)} %param.18) | copy-start | bytes 1572868
  105.4 17.2 %copy-start.4 = (f32[8,256,128]{2,1,0:T(8,128)}, f32[8,256,128]{2,1,0:T(8,128)S(1)}, u32[]{:S(2)}) copy-start(f32[8,256,128]{2,1,0:T(8,128)S(1)} %convert_element_type.58) | copy-start | bytes 3145732
  110.7 16.2 %copy-start.1 = (bf16[8,256,16,64]{1,3,2,0:T(8,128)(2,1)}, bf16[8,256,16,64]{1,3,2,0:T(8,128)(2,1)S(1)}, u32[]{:S(2)}) copy-start(bf16[8,256,16,64]{1,3,2,0:T(8,128)(2,1)S(1)} %multiply_convert_fusion.18) | copy-start | bytes 12582916
  148.6 244.1 %reduce-scatter.3.cloned.1.call-start = ((), (), s32[]{:S(2)}) async-start(), calls=%async_computation.2 | async-start | bytes 1310720 | tf_op jit(solution)/shard_map/reduce_scatter | solution.py:119
  148.9 87.8 %copy-start.12 = (u32[32]{0:T(128)S(1)}, u32[32]{0:T(128)}, u32[]{:S(2)}) copy-start(u32[32]{0:T(128)} %constant.167) | copy-start | bytes 388
  267.9 9.8 %copy-start.8 = (f32[8,256,128]{2,1,0:T(8,128)S(1)}, f32[8,256,128]{2,1,0:T(8,128)}, u32[]{:S(2)}) copy-start(f32[8,256,128]{2,1,0:T(8,128)} %get-tuple-element.486) | copy-start | bytes 3145732
  278.9 113.9 %reduce-scatter.5.cloned.1.call-start = ((), (), s32[]{:S(2)}) async-start(), calls=%async_computation.3 | async-start | bytes 1310720 | tf_op jit(solution)/shard_map/reduce_scatter | solution.py:120
  308.8 7.6 %copy-start.9 = (f32[8,256,128]{1,2,0:T(8,128)S(1)}, f32[8,256,128]{1,2,0:T(8,128)}, u32[]{:S(2)}) copy-start(f32[8,256,128]{1,2,0:T(8,128)} %get-tuple-element.487) | copy-start | bytes 3145732
  308.8 11.3 %copy-start = (f32[16,128,64]{2,1,0:T(8,128)S(1)}, f32[16,128,64]{2,1,0:T(8,128)}, u32[]{:S(2)}) copy-start(f32[16,128,64]{2,1,0:T(8,128)} %get-tuple-element.478) | copy-start | bytes 1572868
  308.8 11.3 %copy-start.3 = (f32[8,256,128]{2,1,0:T(8,128)S(1)}, f32[8,256,128]{2,1,0:T(8,128)}, u32[]{:S(2)}) copy-start(f32[8,256,128]{2,1,0:T(8,128)} %copy-done.2) | copy-start | bytes 3145732
  308.8 11.3 %copy-start.11 = (f32[16]{0:T(128)S(1)}, f32[16]{0:T(128)}, u32[]{:S(2)}) copy-start(f32[16]{0:T(128)} %param.20) | copy-start | bytes 196
  344.9 12.0 %copy-start.5 = (f32[8,256,128]{2,1,0:T(8,128)S(1)}, f32[8,256,128]{2,1,0:T(8,128)}, u32[]{:S(2)}) copy-start(f32[8,256,128]{2,1,0:T(8,128)} %copy-done.4) | copy-start | bytes 3145732
Sparse Core Ops, SparseCore 0:
  78.8 39.4 all-gather.8
  148.7 39.6 all-gather.6
  279.0 26.7 reduce-scatter.2
  320.2 26.7 reduce-scatter.4
where the time goes:
time: 404 us; the launch traced here: 399 us
  matrix products  156 us (39%)
  local copies, waits for them, and re-layouts  134 us (33%)
  other arithmetic  77.4 us (19%)
  blocking collectives  15.6 us (4%)
  between operations  14.8 us (4%)
    unnamed x36, local copies, waits for them, and re-layouts  57.2 us
    convert_element_type x2, local copies, waits for them, and re-layouts, on_device(): scaled = (input_blocks * gain[..., None]).astype(jnp.bfloat16)  26.3 us
    dot_general x8, matrix products, intra(): jnp.einsum('hij,jhp->ihp', mixing, scaled_b, preferred_element_type=jnp.f...  26.2 us
    dot_general x8, matrix products, intra(): jnp.einsum('hki,khp->ihp', mixing, grad_b, preferred_element_type=jnp.flo...  25 us
    dynamic_slice x32, local copies, waits for them, and re-layouts, step(): new = combine(before, jax.tree.map(lambda part: part[at], everything))  22.7 us
    add x16, other arithmetic, link(): second_decay[..., None, None] * first_state + second_state  22.6 us
    dot_general x8, matrix products, intra(): jnp.einsum('khp,ihp->hki', grad_b, scaled_b, preferred_element_type=jnp.f...  20.2 us
    select_n x16, other arithmetic, step(): return jax.tree.map(lambda a, b: jnp.where(reached, a, b), new, before)  20.2 us
  transfers between devices with their start and end apart: 4, of which 0 were waited for; matrix products, arithmetic and copies ran while one was open for 74% of the time, Pallas kernels for 0%

commit v1 on v0

v1 whole, which is shorter than its diff:
```python
import functools

import jax
import jax.numpy as jnp
from jax import lax
from jax.experimental import pallas as pl
from jax.experimental.pallas import tpu as pltpu
from jax.sharding import PartitionSpec as P

WIDTH = 64
BLOCK = 128
TOTALS_BLOCK = 256
GRADS_BLOCK = 256
FAR = -1e30
VMEM_BYTES = 48 * 1024 * 1024
F32 = jnp.float32
BF16 = jnp.bfloat16


def dot(a, b, over_a, over_b):
    return lax.dot_general(a, b, (((over_a,), (over_b,)), ((), ())), preferred_element_type=F32)


def minus_expm1(y):
    series = 1.0 + y * (1.0 / 9.0)
    for k in (8.0, 7.0, 6.0, 5.0, 4.0, 3.0, 2.0):
        series = 1.0 + y * (1.0 / k) * series
    return jnp.where(y > -0.4, -y * series, 1.0 - jnp.exp(y))


def spread_matrix(heads):
    row = lax.broadcasted_iota(jnp.int32, (2 * heads, heads * WIDTH), 0)
    lane = lax.broadcasted_iota(jnp.int32, (2 * heads, heads * WIDTH), 1)
    return jnp.where(lax.rem(row, heads) == lane // WIDTH, 1.0, 0.0).astype(BF16)


def spread(factor, matrix):
    heads = factor.shape[0] // 2
    high = factor.astype(BF16).astype(F32)
    row = lax.broadcasted_iota(jnp.int32, factor.shape, 0)
    parts = jnp.where(row < heads, high, factor - high).astype(BF16)
    return dot(parts, matrix, 0, 0)


def sums(log_decay):
    rows, size = log_decay.shape
    high = log_decay.astype(BF16)
    rest = log_decay - high.astype(F32)
    middle = rest.astype(BF16)
    low = (rest - middle.astype(F32)).astype(BF16)
    source = lax.broadcasted_iota(jnp.int32, (size, 2 * size), 0)
    target = lax.broadcasted_iota(jnp.int32, (size, 2 * size), 1)
    within = jnp.where(
        target < size, jnp.where(source <= target, 1.0, 0.0), jnp.where(source > target - size, 1.0, 0.0)
    ).astype(BF16)
    both = dot(high, within, 1, 0) + dot(middle, within, 1, 0) + dot(low, within, 1, 0)
    return both[:, :size], both[:, size:]


def factors(ld_ref):
    ld = ld_ref[...]
    ld = jnp.concatenate([ld, ld], axis=0)
    gain = jnp.sqrt(minus_expm1(2.0 * ld))
    before, after = sums(ld)
    total = before[:, -1:]
    return gain, before, after, total


def totals_kernel(inputs_ref, grad_ref, ld_ref, write_ref, read_ref, out_ref, push, pull, base):
    step = pl.program_id(0)
    heads = ld_ref.shape[0]
    states = write_ref.shape[1]

    @pl.when(step == 0)
    def _():
        push[...] = jnp.zeros_like(push)
        pull[...] = jnp.zeros_like(pull)
        base[...] = jnp.zeros_like(base)

    matrix = spread_matrix(heads)
    gain, before, after, total = factors(ld_ref)
    start = base[:, :1]
    lead = spread(jnp.exp(start + before), matrix)
    tail = spread(gain * jnp.exp(after), matrix)
    decay = spread(jnp.broadcast_to(jnp.exp(total), (2 * heads, states)), matrix)
    weighted = (lead * grad_ref[...].astype(F32)).astype(BF16)
    pull[...] += dot(read_ref[...], weighted, 0, 0)
    weighted = (tail * inputs_ref[...].astype(F32)).astype(BF16)
    push[...] = push[...] * decay + dot(write_ref[...], weighted, 0, 0)
    base[...] += jnp.broadcast_to(total, base.shape)

    @pl.when(step == pl.num_programs(0) - 1)
    def _():
        out_ref[0:states] = push[...]
        out_ref[states : 2 * states] = pull[...]
        whole = jnp.broadcast_to(jnp.exp(base[:, :1]), (2 * heads, 128))
        out_ref[2 * states :] = spread(whole, matrix)[0:8]


def totals(inputs, grad_out, log_decay, write_keys, read_keys):
    length, lanes = inputs.shape
    heads = log_decay.shape[0]
    states = write_keys.shape[1]
    size = TOTALS_BLOCK
    return pl.pallas_call(
        totals_kernel,
        out_shape=jax.ShapeDtypeStruct((2 * states + 8, lanes), F32),
        grid=(length // size,),
        in_specs=[
            pl.BlockSpec((size, lanes), lambda c: (c, 0)),
            pl.BlockSpec((size, lanes), lambda c: (c, 0)),
            pl.BlockSpec((heads, size), lambda c: (0, c)),
            pl.BlockSpec((size, states), lambda c: (c, 0)),
            pl.BlockSpec((size, states), lambda c: (c, 0)),
        ],
        out_specs=pl.BlockSpec((2 * states + 8, lanes), lambda c: (0, 0)),
        scratch_shapes=[
            pltpu.VMEM((states, lanes), F32),
            pltpu.VMEM((states, lanes), F32),
            pltpu.VMEM((2 * heads, 128), F32),
        ],
        compiler_params=pltpu.CompilerParams(vmem_limit_bytes=VMEM_BYTES),
        cost_estimate=pl.CostEstimate(
            flops=6 * length * lanes * states, bytes_accessed=4 * length * lanes, transcendentals=0
        ),
        name="totals",
    )(inputs, grad_out, log_decay, write_keys, read_keys)


def halves(pair):
    first = lax.broadcasted_iota(jnp.int32, pair.shape, 1) < WIDTH
    zero = jnp.zeros_like(pair)
    return jnp.concatenate([jnp.where(first, pair, zero), jnp.where(first, zero, pair)], axis=0)


def local_kernel(
    inputs_ref,
    grad_ref,
    ld_ref,
    write_ref,
    read_ref,
    inputs_back_ref,
    grad_back_ref,
    ld_back_ref,
    write_back_ref,
    read_back_ref,
    read_terms_ref,
    write_terms_ref,
    lead_ref,
    tail_ref,
    entry,
    after,
    since,
    until,
):
    step = pl.program_id(0)
    count = pl.num_programs(0)
    heads = ld_ref.shape[0]
    states = write_ref.shape[1]

    @pl.when(step == 0)
    def _():
        entry[...] = jnp.zeros_like(entry)
        after[...] = jnp.zeros_like(after)
        since[...] = jnp.ones_like(since)
        until[...] = jnp.ones_like(until)
        write_terms_ref[...] = jnp.zeros_like(write_terms_ref)

    matrix = spread_matrix(heads)
    gain, before, behind, total = factors(ld_ref)
    grad = grad_ref[...]
    inputs = inputs_ref[...].astype(F32)
    led = spread(jnp.exp(before), matrix) * grad.astype(F32)
    lead_ref[...] = (led * since[0:1]).astype(BF16)
    read_terms = dot(led.astype(BF16), entry[...].astype(BF16), 1, 1)
    tailed = (spread(gain * jnp.exp(behind), matrix) * inputs).astype(BF16)
    scaled = (spread(gain, matrix) * inputs).astype(BF16)
    decay = spread(jnp.broadcast_to(jnp.exp(total), (2 * heads, states)), matrix)
    since[...] *= decay[0:8]
    entry[...] = entry[...] * decay + dot(write_ref[...], tailed, 0, 0)
    columns = before.T
    lower = lax.broadcasted_iota(jnp.int32, (BLOCK, BLOCK), 0) >= lax.broadcasted_iota(
        jnp.int32, (BLOCK, BLOCK), 1
    )
    gathered = jnp.zeros((BLOCK, BLOCK), F32)
    for pair in range(heads // 2):
        lanes = slice(pair * 128, pair * 128 + 128)
        products = dot(grad[:, lanes], halves(scaled[:, lanes]), 1, 1)
        for k in range(2):
            head = 2 * pair + k
            gap = columns[:, head : head + 1] - before[head : head + 1, :]
            gathered += products[:, k * BLOCK : k * BLOCK + BLOCK] * jnp.exp(jnp.where(lower, gap, FAR))
    high = gathered.astype(BF16)
    low = (gathered - high.astype(F32)).astype(BF16)
    read_terms_ref[...] = read_terms + dot(high, write_ref[...], 1, 0) + dot(low, write_ref[...], 1, 0)
    at = pl.ds(pl.multiple_of(step * BLOCK, BLOCK), BLOCK)
    write_terms_ref[at, :] += dot(high, read_ref[...], 0, 0) + dot(low, read_ref[...], 0, 0)

    gain, before, behind, total = factors(ld_back_ref)
    tailed = spread(gain * jnp.exp(behind), matrix) * inputs_back_ref[...].astype(F32)
    tail_ref[...] = (tailed * until[0:1]).astype(BF16)
    at = pl.ds(pl.multiple_of((count - 1 - step) * BLOCK, BLOCK), BLOCK)
    write_terms_ref[at, :] += dot(tailed.astype(BF16), after[...].astype(BF16), 1, 1)
    led = (spread(jnp.exp(before), matrix) * grad_back_ref[...].astype(F32)).astype(BF16)
    decay = spread(jnp.broadcast_to(jnp.exp(total), (2 * heads, states)), matrix)
    until[...] *= decay[0:8]
    after[...] = after[...] * decay + dot(read_back_ref[...], led, 0, 0)


def local(inputs, grad_out, log_decay, write_keys, read_keys):
    length, lanes = inputs.shape
    heads = log_decay.shape[0]
    states = write_keys.shape[1]
    count = length // BLOCK

    def specs(at):
        return [
            pl.BlockSpec((BLOCK, lanes), lambda c: (at(c), 0)),
            pl.BlockSpec((BLOCK, lanes), lambda c: (at(c), 0)),
            pl.BlockSpec((heads, BLOCK), lambda c: (0, at(c))),
            pl.BlockSpec((BLOCK, states), lambda c: (at(c), 0)),
            pl.BlockSpec((BLOCK, states), lambda c: (at(c), 0)),
        ]

    operands = (inputs, grad_out, log_decay, write_keys, read_keys)
    return pl.pallas_call(
        local_kernel,
        out_shape=(
            jax.ShapeDtypeStruct((length, states), F32),
            jax.ShapeDtypeStruct((length, states), F32),
            jax.ShapeDtypeStruct((length, lanes), BF16),
            jax.ShapeDtypeStruct((length, lanes), BF16),
        ),
        grid=(count,),
        in_specs=specs(lambda c: c) + specs(lambda c: count - 1 - c),
        out_specs=(
            pl.BlockSpec((BLOCK, states), lambda c: (c, 0)),
            pl.BlockSpec((length, states), lambda c: (0, 0)),
            pl.BlockSpec((BLOCK, lanes), lambda c: (c, 0)),
            pl.BlockSpec((BLOCK, lanes), lambda c: (count - 1 - c, 0)),
        ),
        scratch_shapes=[
            pltpu.VMEM((states, lanes), F32),
            pltpu.VMEM((states, lanes), F32),
            pltpu.VMEM((8, lanes), F32),
            pltpu.VMEM((8, lanes), F32),
        ],
        compiler_params=pltpu.CompilerParams(vmem_limit_bytes=VMEM_BYTES),
        cost_estimate=pl.CostEstimate(
            flops=24 * length * lanes * states, bytes_accessed=12 * length * lanes, transcendentals=0
        ),
        name="local",
    )(*operands, *operands)


def grads_kernel(
    lead_ref, tail_ref, read_terms_ref, write_terms_ref, entry_ref, after_ref, read_ref, write_ref
):
    entry = entry_ref[...].astype(BF16)
    after = after_ref[...].astype(BF16)
    read_ref[...] = read_terms_ref[...] + dot(lead_ref[...], entry, 1, 1)
    write_ref[...] = write_terms_ref[...] + dot(tail_ref[...], after, 1, 1)


def grads(lead, tail, read_terms, write_terms, entry, after):
    length, lanes = lead.shape
    states = entry.shape[0]
    size = GRADS_BLOCK
    wide = pl.BlockSpec((size, lanes), lambda c: (c, 0))
    thin = pl.BlockSpec((size, states), lambda c: (c, 0))
    state = pl.BlockSpec((states, lanes), lambda c: (0, 0))
    shape = jax.ShapeDtypeStruct((length, states), F32)
    return pl.pallas_call(
        grads_kernel,
        out_shape=(shape, shape),
        grid=(length // size,),
        in_specs=[wide, wide, thin, thin, state, state],
        out_specs=(thin, thin),
        compiler_params=pltpu.CompilerParams(vmem_limit_bytes=VMEM_BYTES),
        cost_estimate=pl.CostEstimate(
            flops=4 * length * lanes * states, bytes_accessed=4 * length * lanes, transcendentals=0
        ),
        name="grads",
    )(lead, tail, read_terms, write_terms, entry, after)


def forward_kernel(inputs_ref, ld_ref, write_ref, read_ref, entry_ref, skip_ref, out_ref, entry):
    step = pl.program_id(0)
    heads = ld_ref.shape[0]
    states = write_ref.shape[1]

    @pl.when(step == 0)
    def _():
        entry[...] = entry_ref[...]

    matrix = spread_matrix(heads)
    gain, before, behind, total = factors(ld_ref)
    inputs = inputs_ref[...].astype(F32)
    scaled = (spread(gain, matrix) * inputs).astype(BF16)
    tailed = (spread(gain * jnp.exp(behind), matrix) * inputs).astype(BF16)
    decay = spread(jnp.broadcast_to(jnp.exp(total), (2 * heads, states)), matrix)
    carried = dot(read_ref[...], entry[...].astype(BF16), 1, 0)
    rest = spread(jnp.exp(before), matrix) * carried + skip_ref[0:1] * inputs
    entry[...] = entry[...] * decay + dot(write_ref[...], tailed, 0, 0)
    scores = dot(read_ref[...], write_ref[...], 1, 1)
    columns = before.T
    lower = lax.broadcasted_iota(jnp.int32, (BLOCK, BLOCK), 0) >= lax.broadcasted_iota(
        jnp.int32, (BLOCK, BLOCK), 1
    )
    for pair in range(heads // 2):
        lanes = slice(pair * 128, pair * 128 + 128)
        mixing = []
        for k in range(2):
            head = 2 * pair + k
            gap = columns[:, head : head + 1] - before[head : head + 1, :]
            mixing.append((scores * jnp.exp(jnp.where(lower, gap, FAR))).astype(BF16))
        mixed = dot(jnp.concatenate(mixing, axis=1), halves(scaled[:, lanes]), 1, 0)
        out_ref[:, lanes] = (mixed + rest[:, lanes]).astype(BF16)


def backward_kernel(inputs_ref, ld_ref, write_ref, read_ref, after_ref, skip_ref, out_ref, after):
    step = pl.program_id(0)
    heads = ld_ref.shape[0]
    states = write_ref.shape[1]

    @pl.when(step == 0)
    def _():
        after[...] = after_ref[...]

    matrix = spread_matrix(heads)
    gain, before, behind, total = factors(ld_ref)
    grad = inputs_ref[...]
    grad_wide = grad.astype(F32)
    led = (spread(jnp.exp(before), matrix) * grad_wide).astype(BF16)
    decay = spread(jnp.broadcast_to(jnp.exp(total), (2 * heads, states)), matrix)
    gains = spread(gain, matrix)
    carried = dot(write_ref[...], after[...].astype(BF16), 1, 0)
    rest = spread(gain * jnp.exp(behind), matrix) * carried + skip_ref[0:1] * grad_wide
    after[...] = after[...] * decay + dot(read_ref[...], led, 0, 0)
    scores = dot(write_ref[...], read_ref[...], 1, 1)
    columns = before.T
    upper = lax.broadcasted_iota(jnp.int32, (BLOCK, BLOCK), 0) <= lax.broadcasted_iota(
        jnp.int32, (BLOCK, BLOCK), 1
    )
    for pair in range(heads // 2):
        lanes = slice(pair * 128, pair * 128 + 128)
        mixing = []
        for k in range(2):
            head = 2 * pair + k
            gap = before[head : head + 1, :] - columns[:, head : head + 1]
            mixing.append((scores * jnp.exp(jnp.where(upper, gap, FAR))).astype(BF16))
        mixed = dot(jnp.concatenate(mixing, axis=1), halves(grad[:, lanes]), 1, 0)
        out_ref[:, lanes] = (gains[:, lanes] * mixed + rest[:, lanes]).astype(BF16)


def sweep(kernel, name, reverse, values, log_decay, write_keys, read_keys, state, skip):
    length, lanes = values.shape
    heads = log_decay.shape[0]
    states = write_keys.shape[1]
    count = length // BLOCK

    def at(c):
        return count - 1 - c if reverse else c

    return pl.pallas_call(
        kernel,
        out_shape=jax.ShapeDtypeStruct((length, lanes), BF16),
        grid=(count,),
        in_specs=[
            pl.BlockSpec((BLOCK, lanes), lambda c: (at(c), 0)),
            pl.BlockSpec((heads, BLOCK), lambda c: (0, at(c))),
            pl.BlockSpec((BLOCK, states), lambda c: (at(c), 0)),
            pl.BlockSpec((BLOCK, states), lambda c: (at(c), 0)),
            pl.BlockSpec((states, lanes), lambda c: (0, 0)),
            pl.BlockSpec((8, lanes), lambda c: (0, 0)),
        ],
        out_specs=pl.BlockSpec((BLOCK, lanes), lambda c: (at(c), 0)),
        scratch_shapes=[pltpu.VMEM((states, lanes), F32)],
        compiler_params=pltpu.CompilerParams(vmem_limit_bytes=VMEM_BYTES),
        cost_estimate=pl.CostEstimate(
            flops=16 * length * lanes * states, bytes_accessed=4 * length * lanes, transcendentals=0
        ),
        name=name,
    )(values, log_decay, write_keys, read_keys, state, skip)


def carried_states(summed, states):
    axes = ("outer", "inner")
    devices = lax.axis_size(axes)
    here = lax.axis_index(axes)
    first = lax.rem(here, 2) == 0
    place = here // 2
    part = states // 2
    other = lax.ppermute(summed, axes, [(d, d ^ 1) for d in range(devices)])
    early = jnp.where(first, summed, other)
    late = jnp.where(first, other, summed)
    early_decay = early[2 * states : 2 * states + 1]
    late_decay = late[2 * states : 2 * states + 1]
    row = jnp.where(first, 0, part)

    def mine(x, start):
        return lax.dynamic_slice_in_dim(x, start + row, part, 0)

    push = mine(late, 0) + late_decay * mine(early, 0)
    pull = mine(early, states) + early_decay * mine(late, states)
    decay = jnp.broadcast_to(early_decay * late_decay, (8, summed.shape[1]))
    forth = jnp.concatenate([push, decay], axis=0)
    back = jnp.concatenate([pull, decay], axis=0)
    got = {}
    for m in range(1, devices // 2):
        sent = jnp.where(place < (place ^ m), forth, back)
        got[m] = lax.ppermute(sent, axes, [(d, d ^ (2 * m)) for d in range(devices)])
    entry = jnp.zeros((part, summed.shape[1]), F32)
    after = jnp.zeros((part, summed.shape[1]), F32)
    for m, value in got.items():
        source = place ^ m
        weight = jnp.ones((1, summed.shape[1]), F32)
        for k, between in got.items():
            middle = place ^ k
            inside = ((source < middle) & (middle < place)) | ((place < middle) & (middle < source))
            weight = weight * jnp.where(inside, between[part : part + 1], 1.0)
        term = weight * value[:part]
        entry = entry + jnp.where(source < place, term, 0.0)
        after = after + jnp.where(source > place, term, 0.0)
    own = jnp.concatenate([entry, after], axis=0)
    others = lax.ppermute(own, axes, [(d, d ^ 1) for d in range(devices)])
    top = jnp.where(first, own, others)
    bottom = jnp.where(first, others, own)
    entry = jnp.concatenate([top[:part], bottom[:part]], axis=0)
    after = jnp.concatenate([top[part:], bottom[part:]], axis=0)
    entry = jnp.where(first, entry, early[:states] + early_decay * entry)
    after = jnp.where(first, late[states : 2 * states] + late_decay * after, after)
    return entry, after


def on_device(inputs, log_decay, write_keys, read_keys, skip_gain, grad_out):
    states = write_keys.shape[1]
    skip = jnp.broadcast_to(jnp.repeat(skip_gain, WIDTH)[None], (8, inputs.shape[1]))
    summed = totals(inputs, grad_out, log_decay, write_keys, read_keys)
    read_terms, write_terms, lead, tail = local(inputs, grad_out, log_decay, write_keys, read_keys)
    entry, after = carried_states(summed, states)
    read_terms, write_terms = grads(lead, tail, read_terms, write_terms, entry, after)
    grad_write = lax.psum_scatter(write_terms, "mp", scatter_dimension=0, tiled=True)
    grad_read = lax.psum_scatter(read_terms, "mp", scatter_dimension=0, tiled=True)
    mixed = sweep(
        forward_kernel, "forward", False, inputs, log_decay, write_keys, read_keys, entry, skip
    )
    grad_in = sweep(
        backward_kernel, "backward", True, grad_out, log_decay, write_keys, read_keys, after, skip
    )
    return mixed, grad_in, grad_write, grad_read


def solution(mesh):
    tokens = ("outer", "inner")
    return jax.shard_map(
        on_device,
        mesh=mesh,
        in_specs=(
            P(tokens, "mp"),
            P("mp", tokens),
            P(tokens, None),
            P(tokens, None),
            P("mp"),
            P(tokens, "mp"),
        ),
        out_specs=(
            P(tokens, "mp"),
            P(tokens, "mp"),
            P(("outer", "inner", "mp"), None),
            P(("outer", "inner", "mp"), None),
        ),
        check_vma=False,
    )
```

time: 404 us -> 153 us (0.38)
  matrix products: 156 us -> 0 us
  local copies, waits for them, and re-layouts: 134 us -> 7.15 us
  Pallas kernels: 0 us -> 92.2 us
  other arithmetic: 77.4 us -> 3.14 us
  waiting for transfers between devices: 0.09 us -> 30.5 us
  blocking collectives: 15.6 us -> 0 us
  starting transfers between devices: 0.34 us -> 5.04 us
    dot_general x54 -> x0, matrix products: 156 us -> none  [the longest x8 26.2 us: intra(): jnp.einsum('hij,jhp->ihp', mixing, scaled_b, preferred_element_type=jnp.f...]
    pallas_call x0 -> x5, Pallas kernels: none -> 92.2 us  [the longest x2 40.6 us: sweep(): pl.pallas_call(kernel, out_shape=jax.ShapeDtypeStruct((length, lanes), BF...]
    unnamed x36 -> x20, local copies, waits for them, and re-layouts: 57.2 us -> 6.91 us
    convert_element_type x2 -> x0, local copies, waits for them, and re-layouts: 26.3 us -> none  [on_device(): scaled = (input_blocks * gain[..., None]).astype(jnp.bfloat16)]
    add x18 -> x2, other arithmetic: 24.9 us -> 0.21 us  [the longest x1 0.12 us: carried_states(): entry = entry + jnp.where(source < place, term, 0.0)]
    dynamic_slice x48 -> x0, local copies, waits for them, and re-layouts: 22.8 us -> none  [the longest x32 22.7 us: step(): new = combine(before, jax.tree.map(lambda part: part[at], everything))]
    select_n x16 -> x4, other arithmetic: 20.2 us -> 2.87 us  [the longest x1 1.43 us: carried_states(): late = jnp.where(first, other, summed)]
    dynamic_update_slice x16 -> x0, other arithmetic: 17.3 us -> none  [within(): lax.scan(advance, identity, (decay, terms), reverse=backward)]
  transfers between devices with their start and end apart: 4 -> 7, of which waited for: 0 -> 4; matrix products, arithmetic and copies ran while one was open for 74% -> 0% of each run, Pallas kernels for 0% -> 49%
where the time goes in v1:
time: 153 us; the launch traced here: 152 us
  Pallas kernels  92.2 us (60%)
  waiting for transfers between devices  30.5 us (20%)
  between operations  14.2 us (9%)
  local copies, waits for them, and re-layouts  7.15 us (5%)
  starting transfers between devices  5.04 us (3%)
  other arithmetic  3.14 us (2%)
    pallas_call x2, Pallas kernels, sweep(): pl.pallas_call(kernel, out_shape=jax.ShapeDtypeStruct((length, lanes), BF...  40.6 us
    pallas_call x1, Pallas kernels, local(): pl.pallas_call(local_kernel, out_shape=(jax.ShapeDtypeStruct((length, sta...  33.4 us
    reduce_scatter x1, waiting for transfers between devices, on_device(): lax.psum_scatter(read_terms, 'mp', scatter_dimension=0, tiled=True)  13.9 us
    ppermute x3, waiting for transfers between devices, carried_states(): got[m] = lax.ppermute(sent, axes, [(d, d ^ 2 * m) for d in range(devices)])  13.4 us
    pallas_call x1, Pallas kernels, totals(): pl.pallas_call(totals_kernel, out_shape=jax.ShapeDtypeStruct((2 * states...  10 us
    pallas_call x1, Pallas kernels, grads(): pl.pallas_call(grads_kernel, out_shape=(shape, shape), grid=(length // si...  8.22 us
    unnamed x20, local copies, waits for them, and re-layouts  6.91 us
    ppermute x3, starting transfers between devices, carried_states(): got[m] = lax.ppermute(sent, axes, [(d, d ^ 2 * m) for d in range(devices)])  4.37 us
  transfers between devices with their start and end apart: 7, of which 4 were waited for; matrix products, arithmetic and copies ran while one was open for 0% of the time, Pallas kernels for 49%

profile of v1, /device:TPU:0, one launch (start us, length us, event | category | flops | bytes accessed | tf_op | source)
XLA Modules:
  0.0 152.2 jit_solution(6241225457192469109)
XLA Ops:
  7.2 1.0 copy-done.2
  8.3 1.0 copy-done.4
  9.3 0.9 copy-done.6
  10.2 10.0 %totals.1 = f32[264,1024]{1,0:T(8,128)S(1)} custom-call(bf16[2048,1024]{1,0:T(8,128)(2,1)} %inputs_back_ref.1, bf16[2048,1024]{1,0:T(8,128)(2,1)} %grad_back_ref.1, f32[16,2048]{1,0:T(8,128)S(1)} %copy-done.6, bf16[2048,128]{1,0:T(8,128)(2,1)S(1)} %copy-done.2, bf16[2048,128]{1,0:T(8,128)(2,1)S(1)} %copy-done.4), custom_call_target="tpu_custom_call" | custom-call | flops 1610612736 | bytes 8388608 | tf_op jit(solution)/shard_map/totals/pallas_call | solution.py:105
  20.2 0.5 collective-permute-start
  20.8 2.5 %collective-permute-done = f32[264,1024]{1,0:T(8,128)} collective-permute-done((f32[264,1024]{1,0:T(8,128)S(1)}, f32[264,1024]{1,0:T(8,128)}, u32[]{:S(2)}, u32[]{:S(2)}) %collective-permute-start) | collective-permute-done | bytes 1081376 | tf_op jit(solution)/shard_map/ppermute | solution.py:394
  23.2 1.4 broadcast_select_fusion.1
  24.9 0.8 copy-done.8
  25.7 2.9 %collective-permute-start.1 = (f32[72,1024]{1,0:T(8,128)S(1)}, f32[72,1024]{1,0:T(8,128)S(1)}, u32[]{:S(2)}, u32[]{:S(2)}) collective-permute-start(f32[72,1024]{1,0:T(8,128)S(1)} %get-tuple-element.29), channel_id=1, source_target_pairs={{0,16},{4,20},{8,24},{12,28},{16,0},{20,4},{24,8},{28,12},{1,17},{... | collective-permute-start | bytes 884744 | tf_op jit(solution)/shard_map/ppermute | solution.py:412
  28.6 1.4 collective-permute-start.2
  30.0 12.1 %collective-permute-done.1 = f32[72,1024]{1,0:T(8,128)S(1)} collective-permute-done((f32[72,1024]{1,0:T(8,128)S(1)}, f32[72,1024]{1,0:T(8,128)S(1)}, u32[]{:S(2)}, u32[]{:S(2)}) %collective-permute-start.1) | collective-permute-done | bytes 294944 | tf_op jit(solution)/shard_map/ppermute | solution.py:412
  42.2 1.2 collective-permute-done.3
  43.5 0.1 select_add_fusion.1
  43.7 0.8 copy-done.3
  44.5 0.2 copy-done.5
  44.7 33.4 %local.1 = (f32[2048,128]{1,0:T(8,128)S(1)}, f32[2048,128]{1,0:T(8,128)S(1)}, bf16[2048,1024]{1,0:T(8,128)(2,1)}, bf16[2048,1024]{1,0:T(8,128)(2,1)}) custom-call(bf16[2048,1024]{1,0:T(8,128)(2,1)} %inputs_back_ref.1, bf16[2048,1024]{1,0:T(8,128)(2,1)} %grad_back_ref.1, f32[16,2048]{1,0:T(8,128)S(1)} %copy-done.7, bf16[2048,128]{1,0:T(8,128)(2,1)S(1)} %copy-done.3, ...), custom_call_target="tpu_custom_call" | custom-call | flops 6442450944 | bytes 25165824 | tf_op jit(solution)/shard_map/local/pallas_call | solution.py:226
  78.0 0.1 broadcast_select_fusion.3
  78.3 1.2 fusion
  79.5 8.2 %grads.1 = (f32[2048,128]{1,0:T(8,128)}, f32[2048,128]{1,0:T(8,128)}) custom-call(bf16[2048,1024]{1,0:T(8,128)(2,1)} %get-tuple-element.10.lead_ref, bf16[2048,1024]{1,0:T(8,128)(2,1)} %get-tuple-element.11.tail_ref, f32[2048,128]{1,0:T(8,128)S(1)} %get-tuple-element.12.read_terms_ref, f32[2048,128]{1,0:T(8,128)S(1)} %get-tuple-element.13.write_terms_ref, ...), custom_call_target="tpu_custom_call" | custom-call | flops 1073741824 | bytes 8388608 | tf_op jit(solution)/shard_map/grads/pallas_call | solution.py:273
  87.8 0.7 reduce-scatter.5.cloned.1.call-update
  88.7 2.2 %copy-done = bf16[2048,1024]{1,0:T(8,128)(2,1)S(1)} copy-done((bf16[2048,1024]{1,0:T(8,128)(2,1)S(1)}, bf16[2048,1024]{1,0:T(8,128)(2,1)}, u32[]{:S(2)}) %copy-start) | copy-done | bytes 4194328
  90.9 19.8 %forward.1 = bf16[2048,1024]{1,0:T(8,128)(2,1)} custom-call(bf16[2048,1024]{1,0:T(8,128)(2,1)S(1)} %copy-done, f32[16,2048]{1,0:T(8,128)S(1)} %copy-done.7, bf16[2048,128]{1,0:T(8,128)(2,1)S(1)} %copy-done.3, bf16[2048,128]{1,0:T(8,128)(2,1)S(1)} %copy-done.5, f32[128,1024]{1,0:T(8,128)S(1)} %get-tuple-element.38.entry_ref, ...), custom_call_target="tpu_custom_call" | custom-call | flops 4294967296 | bytes 8388608 | tf_op jit(solution)/shard_map/forward/pallas_call | solution.py:365
  110.7 20.8 %backward.1 = bf16[2048,1024]{1,0:T(8,128)(2,1)} custom-call(bf16[2048,1024]{1,0:T(8,128)(2,1)S(1)} %copy-done.1, f32[16,2048]{1,0:T(8,128)S(1)} %copy-done.7, bf16[2048,128]{1,0:T(8,128)(2,1)S(1)} %copy-done.3, bf16[2048,128]{1,0:T(8,128)(2,1)S(1)} %copy-done.5, f32[128,1024]{1,0:T(8,128)S(1)} %get-tuple-element.37.after_ref, ...), custom_call_target="tpu_custom_call" | custom-call | flops 4294967296 | bytes 8388608 | tf_op jit(solution)/shard_map/backward/pallas_call | solution.py:365
  131.5 13.9 %reduce-scatter.5.cloned.1.call-done = f32[512,128]{1,0:T(8,128)} async-done(((f32[2048,128]{1,0:T(8,128)}), f32[512,128]{1,0:T(8,128)}) %reduce-scatter.5.cloned.1.call-update) | async-done | bytes 262160 | tf_op jit(solution)/shard_map/reduce_scatter | solution.py:444
  (32 shorter events, 0.8 us)
Async XLA Ops:
  7.2 124.3 %reduce-scatter.3.cloned.1.call-start = ((), (), s32[]{:S(2)}) async-start(), calls=%async_computation.2 | async-start | bytes 1310720 | tf_op jit(solution)/shard_map/reduce_scatter | solution.py:443
  7.2 1.0 copy-start.2
  8.3 1.0 copy-start.4
  9.3 0.9 copy-start.6
  20.2 3.0 %collective-permute-start = (f32[264,1024]{1,0:T(8,128)S(1)}, f32[264,1024]{1,0:T(8,128)}, u32[]{:S(2)}, u32[]{:S(2)}) collective-permute-start(f32[264,1024]{1,0:T(8,128)S(1)} %totals.1), channel_id=1, source_target_pairs={{0,4},{4,0},{8,12},{12,8},{16,20},{20,16},{24,28},{28,24},{1,5},{5... | collective-permute-start | bytes 3244040 | tf_op jit(solution)/shard_map/ppermute | solution.py:394
  24.7 1.0 copy-start.8
  25.7 16.5 %collective-permute-start.1 = (f32[72,1024]{1,0:T(8,128)S(1)}, f32[72,1024]{1,0:T(8,128)S(1)}, u32[]{:S(2)}, u32[]{:S(2)}) collective-permute-start(f32[72,1024]{1,0:T(8,128)S(1)} %get-tuple-element.29), channel_id=1, source_target_pairs={{0,16},{4,20},{8,24},{12,28},{16,0},{20,4},{24,8},{28,12},{1,17},{... | collective-permute-start | bytes 884744 | tf_op jit(solution)/shard_map/ppermute | solution.py:412
  28.6 13.6 %collective-permute-start.2 = (f32[72,1024]{1,0:T(8,128)S(1)}, f32[72,1024]{1,0:T(8,128)S(1)}, u32[]{:S(2)}, u32[]{:S(2)}) collective-permute-start(f32[72,1024]{1,0:T(8,128)S(1)} %get-tuple-element.27), channel_id=1, source_target_pairs={{0,24},{4,28},{8,16},{12,20},{16,8},{20,12},{24,0},{28,4},{1,25},{... | collective-permute-start | bytes 884744 | tf_op jit(solution)/shard_map/ppermute | solution.py:412
  30.0 13.4 %collective-permute-start.3 = (f32[72,1024]{1,0:T(8,128)S(1)}, f32[72,1024]{1,0:T(8,128)S(1)}, u32[]{:S(2)}, u32[]{:S(2)}) collective-permute-start(f32[72,1024]{1,0:T(8,128)S(1)} %get-tuple-element.28), channel_id=1, source_target_pairs={{0,8},{4,12},{8,0},{12,4},{16,24},{20,28},{24,16},{28,20},{1,9},{5... | collective-permute-start | bytes 884744 | tf_op jit(solution)/shard_map/ppermute | solution.py:412
  43.5 1.0 copy-start.3
  43.5 1.2 copy-start.5
  43.5 1.2 copy-start.7
  43.7 34.4 %collective-permute-start.4 = (f32[128,1024]{1,0:T(8,128)S(1)}, f32[128,1024]{1,0:T(8,128)S(1)}, u32[]{:S(2)}, u32[]{:S(2)}) collective-permute-start(f32[128,1024]{1,0:T(8,128)S(1)} %pad_maximum_fusion), channel_id=1, source_target_pairs={{0,4},{4,0},{8,12},{12,8},{16,20},{20,16},{24,28},{28,24},{1,5},{5... | collective-permute-start | bytes 1572872 | tf_op jit(solution)/shard_map/ppermute | solution.py:426
  87.7 0.8 copy-start.9
  87.8 57.6 %reduce-scatter.5.cloned.1.call-start = ((), (), s32[]{:S(2)}) async-start(), calls=%async_computation.3 | async-start | bytes 1310720 | tf_op jit(solution)/shard_map/reduce_scatter | solution.py:444
  88.7 2.2 %copy-start = (bf16[2048,1024]{1,0:T(8,128)(2,1)S(1)}, bf16[2048,1024]{1,0:T(8,128)(2,1)}, u32[]{:S(2)}) copy-start(bf16[2048,1024]{1,0:T(8,128)(2,1)} %inputs_back_ref.1) | copy-start | bytes 12582916
  90.9 19.8 %copy-start.1 = (bf16[2048,1024]{1,0:T(8,128)(2,1)S(1)}, bf16[2048,1024]{1,0:T(8,128)(2,1)}, u32[]{:S(2)}) copy-start(bf16[2048,1024]{1,0:T(8,128)(2,1)} %grad_back_ref.1) | copy-start | bytes 12582916
Sparse Core Ops, SparseCore 0:
  87.9 28.6 reduce-scatter.2
  119.5 25.8 reduce-scatter.4

commit v2 on v1

v2 whole, which is shorter than its diff:
```python
import functools

import jax
import jax.numpy as jnp
from jax import lax
from jax.experimental import pallas as pl
from jax.experimental.pallas import tpu as pltpu
from jax.sharding import PartitionSpec as P

WIDTH = 64
BLOCK = 128
STEP = 512
GRADS_STEP = 1024
FAR = -1e30
LOG2E = 1.4426950408889634
VMEM_BYTES = 60 * 1024 * 1024
F32 = jnp.float32
BF16 = jnp.bfloat16


def dot(a, b, over_a, over_b):
    return lax.dot_general(a, b, (((over_a,), (over_b,)), ((), ())), preferred_element_type=F32)


def minus_expm1(y):
    series = 1.0 + y * (1.0 / 9.0)
    for k in (8.0, 7.0, 6.0, 5.0, 4.0, 3.0, 2.0):
        series = 1.0 + y * (1.0 / k) * series
    return jnp.where(y > -0.4, -y * series, 1.0 - jnp.exp(y))


def iota(shape, dimension):
    return lax.broadcasted_iota(jnp.int32, shape, dimension)


def spread_matrix(heads, group):
    shape = (128, heads * WIDTH)
    row = iota(shape, 0) - 2 * heads * group
    gap = iota(shape, 1) - WIDTH * jnp.where(row < heads, row, row - heads)
    inside = (row >= 0) & (row < 2 * heads) & (gap >= 0) & (gap < WIDTH)
    return jnp.where(inside, 1.0, 0.0).astype(BF16)


def row_spread_matrix(heads):
    shape = (heads, heads * WIDTH)
    gap = iota(shape, 1) - WIDTH * iota(shape, 0)
    one = jnp.where((gap >= 0) & (gap < WIDTH), 1.0, 0.0)
    return jnp.concatenate([one, one, one], axis=0).astype(BF16)


def three(x):
    high = x.astype(BF16).astype(F32)
    middle = (x - high).astype(BF16).astype(F32)
    return high, middle, x - high - middle


def block_sums(rows):
    shape = (BLOCK, 2 * BLOCK)
    source, target = iota(shape, 0), iota(shape, 1)
    upto = jnp.where(source <= target, 1.0, 0.0)
    beyond = jnp.where(source > target - BLOCK, 1.0, 0.0)
    within = jnp.where(target < BLOCK, upto, beyond).astype(BF16)
    count = rows.shape[0]
    both = dot(jnp.concatenate(three(rows), axis=0).astype(BF16), within, 1, 0)
    both = both[:count] + both[count : 2 * count] + both[2 * count :]
    return both[:, :BLOCK], both[:, BLOCK:]


def stacked(x):
    return jnp.concatenate(
        [x[:, at : at + BLOCK] for at in range(0, x.shape[1], BLOCK)], axis=0
    )


def block_factors(ld_ref):
    ld = ld_ref[...]
    gain = stacked(jnp.sqrt(minus_expm1(2.0 * ld)))
    before, behind = block_sums(stacked(ld))
    return gain, before, behind


def in_columns(groups, heads, block):
    parts = []
    for factor in groups:
        rows = factor[block * heads : block * heads + heads]
        high = rows.astype(BF16).astype(F32)
        parts += [high, rows - high]
    parts.append(jnp.zeros((128 - 2 * heads * len(groups), BLOCK), F32))
    rows = jnp.concatenate(parts, axis=0).astype(BF16)
    eye = jnp.where(iota((BLOCK, BLOCK), 0) == iota((BLOCK, BLOCK), 1), 1.0, 0.0).astype(BF16)
    return dot(eye, rows, 1, 1).astype(BF16)


def totals_kernel(
    inputs_ref, grad_ref, ld_ref, write_ref, read_ref, out_ref, lead_ref, tail_ref, parts, lanes_of
):
    step = pl.program_id(0)
    heads = ld_ref.shape[0]
    states = write_ref.shape[1]
    count = ld_ref.shape[1] // BLOCK

    @pl.when(step == 0)
    def _():
        lanes_of[0] = spread_matrix(heads, 0)
        lanes_of[1] = spread_matrix(heads, 1)
        gain, before, behind = block_factors(ld_ref)
        totals = [before[c * heads : c * heads + heads, BLOCK - 1 :] for c in range(count)]
        start = [jnp.zeros((heads, 1), F32)]
        for total in totals:
            start.append(start[-1] + total)
        end = [jnp.zeros((heads, 1), F32)]
        for total in totals[::-1]:
            end.append(end[-1] + total)
        since = jnp.concatenate(start[:count], axis=0)
        until = jnp.concatenate(end[:count][::-1], axis=0)
        lead = jnp.exp(since + before)
        tail = gain * jnp.exp(until + behind)
        for c in range(count):
            parts[c * BLOCK : c * BLOCK + BLOCK] = in_columns((lead, tail), heads, c)
        out_ref[...] = jnp.zeros_like(out_ref)
        whole = jnp.concatenate(three(jnp.exp(start[count])), axis=0)
        whole = jnp.broadcast_to(whole, (3 * heads, 128)).astype(BF16)
        out_ref[2 * states :] = dot(whole, row_spread_matrix(heads), 0, 0)[0:8]

    at = pl.ds(pl.multiple_of(step * STEP, STEP), STEP)
    here = parts[at, :]
    lead = (dot(here, lanes_of[0], 1, 0) * grad_ref[...].astype(F32)).astype(BF16)
    lead_ref[...] = lead
    out_ref[states : 2 * states] += dot(read_ref[at, :], lead, 0, 0)
    tail = (dot(here, lanes_of[1], 1, 0) * inputs_ref[...].astype(F32)).astype(BF16)
    tail_ref[...] = tail
    out_ref[0:states] += dot(write_ref[at, :], tail, 0, 0)


def totals(inputs, grad_out, log_decay, write_keys, read_keys):
    length, lanes = inputs.shape
    heads = log_decay.shape[0]
    states = write_keys.shape[1]
    wide = pl.BlockSpec((STEP, lanes), lambda c: (c, 0))
    keys = pl.BlockSpec((length, states), lambda c: (0, 0))
    return pl.pallas_call(
        totals_kernel,
        out_shape=(
            jax.ShapeDtypeStruct((2 * states + 8, lanes), F32),
            jax.ShapeDtypeStruct((length, lanes), BF16),
            jax.ShapeDtypeStruct((length, lanes), BF16),
        ),
        grid=(length // STEP,),
        in_specs=[wide, wide, pl.BlockSpec((heads, length), lambda c: (0, 0)), keys, keys],
        out_specs=(pl.BlockSpec((2 * states + 8, lanes), lambda c: (0, 0)), wide, wide),
        scratch_shapes=[
            pltpu.VMEM((length, 128), BF16),
            pltpu.VMEM((2, 128, lanes), BF16),
        ],
        compiler_params=pltpu.CompilerParams(vmem_limit_bytes=VMEM_BYTES),
        cost_estimate=pl.CostEstimate(
            flops=6 * length * lanes * states, bytes_accessed=8 * length * lanes, transcendentals=0
        ),
        name="totals",
    )(inputs, grad_out, log_decay, write_keys, read_keys)


def halves(pair):
    first = iota(pair.shape, 1) < WIDTH
    zero = jnp.zeros_like(pair)
    return jnp.concatenate([jnp.where(first, pair, zero), jnp.where(first, zero, pair)], axis=0)


def lower_block():
    return iota((BLOCK, BLOCK), 0) >= iota((BLOCK, BLOCK), 1)


def local_kernel(
    inputs_ref,
    grad_ref,
    ld_ref,
    write_ref,
    read_ref,
    read_terms_ref,
    write_terms_ref,
    entries_ref,
    afters_ref,
    parts_ref,
    rows_ref,
    columns_ref,
    ranges_ref,
    entry,
    after,
    decays,
    leads,
    tails,
    lanes_of,
):
    step = pl.program_id(0)
    heads = ld_ref.shape[0]
    length = ld_ref.shape[1]
    states = write_ref.shape[1]
    count = length // BLOCK
    steps = length // STEP
    inner = STEP // BLOCK

    @pl.when(step == 0)
    def _():
        for k in range(3):
            lanes_of[k] = spread_matrix(heads, k)
        gain, before, behind = block_factors(ld_ref)
        lead = jnp.exp(before)
        tail = gain * jnp.exp(behind)
        matrix = row_spread_matrix(heads)
        powers = before * LOG2E
        rows_ref[...] = powers
        lasts = []
        for c in range(count):
            at = slice(c * BLOCK, c * BLOCK + BLOCK)
            mine = slice(c * heads, c * heads + heads)
            parts_ref[at] = in_columns((lead, tail, gain), heads, c)
            columns_ref[at] = powers[mine].T
            lasts.append(lead[mine, BLOCK - 1 :])
        last = jnp.concatenate(lasts, axis=1)
        decays[...] = dot(jnp.concatenate(three(last), axis=0).astype(BF16), matrix, 0, 0)
        ones = jnp.ones((1, heads * WIDTH), F32)
        since, until = [ones], [ones]
        for c in range(count - 1):
            since.append(since[-1] * decays[c : c + 1])
            until.append(until[-1] * decays[count - 1 - c : count - c])
        ranges_ref[:count] = jnp.concatenate(since, axis=0)
        ranges_ref[count:] = jnp.concatenate(until[::-1], axis=0)
        entry[...] = jnp.zeros_like(entry)
        after[...] = jnp.zeros_like(after)

    @pl.when(step < steps)
    def _():
        for k in range(inner):
            inside = slice(k * BLOCK, k * BLOCK + BLOCK)
            block = step * inner + k
            at = pl.ds(pl.multiple_of(block * BLOCK, BLOCK), BLOCK)
            here = parts_ref[at, :]
            write, read = write_ref[at, :], read_ref[at, :]
            grad = grad_ref[inside]
            inputs = inputs_ref[inside].astype(F32)
            lead = (dot(here, lanes_of[0], 1, 0) * grad.astype(F32)).astype(BF16)
            tail = (dot(here, lanes_of[1], 1, 0) * inputs).astype(BF16)
            scaled = (dot(here, lanes_of[2], 1, 0) * inputs).astype(BF16)
            leads[at, :] = lead
            tails[at, :] = tail
            state = entry[...]
            held = state.astype(BF16)
            entries_ref[inside] = held
            entry[...] = state * decays[pl.ds(block, 1), :] + dot(write, tail, 0, 0)
            rows = rows_ref[pl.ds(pl.multiple_of(block * heads, heads), heads), :]
            columns = columns_ref[at, :]
            lower = lower_block()
            gathered = jnp.zeros((BLOCK, BLOCK), F32)
            for pair in range(heads // 2):
                lanes = slice(pair * 128, pair * 128 + 128)
                products = dot(grad[:, lanes], halves(scaled[:, lanes]), 1, 1)
                for j in range(2):
                    head = 2 * pair + j
                    gap = columns[:, head : head + 1] - rows[head : head + 1, :]
                    gathered += products[:, j * BLOCK : j * BLOCK + BLOCK] * jnp.exp2(
                        jnp.where(lower, gap, FAR)
                    )
            high = gathered.astype(BF16)
            low = (gathered - high.astype(F32)).astype(BF16)
            read_terms_ref[inside] = dot(lead, held, 1, 1) + dot(high, write, 1, 0) + dot(low, write, 1, 0)
            write_terms_ref[at, :] = dot(high, read, 0, 0) + dot(low, read, 0, 0)

    @pl.when(step >= steps)
    def _():
        for k in reversed(range(inner)):
            inside = slice(k * BLOCK, k * BLOCK + BLOCK)
            block = (2 * steps - 1 - step) * inner + k
            at = pl.ds(pl.multiple_of(block * BLOCK, BLOCK), BLOCK)
            state = after[...]
            held = state.astype(BF16)
            afters_ref[inside] = held
            after[...] = state * decays[pl.ds(block, 1), :] + dot(read_ref[at, :], leads[at, :], 0, 0)
            write_terms_ref[at, :] += dot(tails[at, :], held, 1, 1)


def local(inputs, grad_out, log_decay, write_keys, read_keys):
    length, lanes = inputs.shape
    heads = log_decay.shape[0]
    states = write_keys.shape[1]
    assert states == BLOCK and 6 * heads <= 128
    count = length // BLOCK
    steps = length // STEP

    def forth(c):
        return jnp.minimum(c, steps - 1)

    def back(c):
        return jnp.minimum(2 * steps - 1 - c, steps - 1)

    def whole(*shape):
        return pl.BlockSpec(shape, lambda c: (0, 0))

    return pl.pallas_call(
        local_kernel,
        out_shape=(
            jax.ShapeDtypeStruct((length, states), F32),
            jax.ShapeDtypeStruct((length, states), F32),
            jax.ShapeDtypeStruct((length, lanes), BF16),
            jax.ShapeDtypeStruct((length, lanes), BF16),
            jax.ShapeDtypeStruct((length, 128), BF16),
            jax.ShapeDtypeStruct((count * heads, BLOCK), F32),
            jax.ShapeDtypeStruct((length, heads), F32),
            jax.ShapeDtypeStruct((2 * count, lanes), F32),
        ),
        grid=(2 * steps,),
        in_specs=[
            pl.BlockSpec((STEP, lanes), lambda c: (forth(c), 0)),
            pl.BlockSpec((STEP, lanes), lambda c: (forth(c), 0)),
            whole(heads, length),
            whole(length, states),
            whole(length, states),
        ],
        out_specs=(
            pl.BlockSpec((STEP, states), lambda c: (forth(c), 0)),
            whole(length, states),
            pl.BlockSpec((STEP, lanes), lambda c: (forth(c), 0)),
            pl.BlockSpec((STEP, lanes), lambda c: (back(c), 0)),
            whole(length, 128),
            whole(count * heads, BLOCK),
            whole(length, heads),
            whole(2 * count, lanes),
        ),
        scratch_shapes=[
            pltpu.VMEM((states, lanes), F32),
            pltpu.VMEM((states, lanes), F32),
            pltpu.VMEM((count, lanes), F32),
            pltpu.VMEM((length, lanes), BF16),
            pltpu.VMEM((length, lanes), BF16),
            pltpu.VMEM((3, 128, lanes), BF16),
        ],
        compiler_params=pltpu.CompilerParams(vmem_limit_bytes=VMEM_BYTES),
        cost_estimate=pl.CostEstimate(
            flops=24 * length * lanes * states, bytes_accessed=8 * length * lanes, transcendentals=0
        ),
        name="local",
    )(inputs, grad_out, log_decay, write_keys, read_keys)


def grads_kernel(
    lead_ref, tail_ref, read_terms_ref, write_terms_ref, entry_ref, after_ref, out_ref
):
    states = entry_ref.shape[0]
    entry = entry_ref[...].astype(BF16)
    after = after_ref[...].astype(BF16)
    out_ref[:, :states] = read_terms_ref[...] + dot(lead_ref[...], entry, 1, 1)
    out_ref[:, states:] = write_terms_ref[...] + dot(tail_ref[...], after, 1, 1)


def grads(lead, tail, read_terms, write_terms, entry, after):
    length, lanes = lead.shape
    states = entry.shape[0]
    size = GRADS_STEP
    wide = pl.BlockSpec((size, lanes), lambda c: (c, 0))
    thin = pl.BlockSpec((size, states), lambda c: (c, 0))
    state = pl.BlockSpec((states, lanes), lambda c: (0, 0))
    return pl.pallas_call(
        grads_kernel,
        out_shape=jax.ShapeDtypeStruct((length, 2 * states), F32),
        grid=(length // size,),
        in_specs=[wide, wide, thin, thin, state, state],
        out_specs=pl.BlockSpec((size, 2 * states), lambda c: (c, 0)),
        compiler_params=pltpu.CompilerParams(vmem_limit_bytes=VMEM_BYTES),
        cost_estimate=pl.CostEstimate(
            flops=4 * length * lanes * states, bytes_accessed=4 * length * lanes, transcendentals=0
        ),
        name="grads",
    )(lead, tail, read_terms, write_terms, entry, after)


def outputs_kernel(
    first,
    inputs_ref,
    grad_ref,
    write_ref,
    read_ref,
    entries_ref,
    afters_ref,
    parts_ref,
    rows_ref,
    columns_ref,
    ranges_ref,
    entry_ref,
    after_ref,
    skip_ref,
    *rest,
):
    mixed_ref, grad_in_ref, lanes_of = rest[-3:]
    step = pl.program_id(0)
    heads = skip_ref.shape[1] // WIDTH
    count = ranges_ref.shape[0] // 2
    inner = STEP // BLOCK

    @pl.when(step == 0)
    def _():
        for k in range(3):
            lanes_of[k] = spread_matrix(heads, k)

    for k in range(inner):
        at = slice(k * BLOCK, k * BLOCK + BLOCK)
        block = (first + step) * inner + k
        here = parts_ref[at, :]
        write, read = write_ref[at, :], read_ref[at, :]
        grad = grad_ref[at]
        inputs = inputs_ref[at].astype(F32)
        gains = dot(here, lanes_of[2], 1, 0)
        scaled = (gains * inputs).astype(BF16)
        entry = entries_ref[at].astype(F32) + ranges_ref[pl.ds(block, 1), :] * entry_ref[...]
        after = afters_ref[at].astype(F32) + ranges_ref[pl.ds(count + block, 1), :] * after_ref[...]
        skip = skip_ref[0:1]
        out_rest = dot(here, lanes_of[0], 1, 0) * dot(read, entry.astype(BF16), 1, 0) + skip * inputs
        back_rest = dot(here, lanes_of[1], 1, 0) * dot(write, after.astype(BF16), 1, 0)
        back_rest = back_rest + skip * grad.astype(F32)
        scores = dot(read, write, 1, 1)
        rows = rows_ref[k * heads : k * heads + heads, :]
        columns = columns_ref[at, :]
        lower = lower_block()
        for pair in range(heads // 2):
            lanes = slice(pair * 128, pair * 128 + 128)
            mixing = []
            for j in range(2):
                head = 2 * pair + j
                gap = columns[:, head : head + 1] - rows[head : head + 1, :]
                mixing.append((scores * jnp.exp2(jnp.where(lower, gap, FAR))).astype(BF16))
            mixed = dot(jnp.concatenate(mixing, axis=1), halves(scaled[:, lanes]), 1, 0)
            mixed_ref[at, lanes] = (mixed + out_rest[:, lanes]).astype(BF16)
            back = dot(jnp.concatenate(mixing, axis=0), halves(grad[:, lanes]), 0, 0)
            grad_in_ref[at, lanes] = (gains[:, lanes] * back + back_rest[:, lanes]).astype(BF16)


def outputs(first, steps, earlier, inputs, grad_out, write_keys, read_keys, made, entry, after, skip):
    length, lanes = inputs.shape
    states = write_keys.shape[1]
    entries, afters, parts, rows, columns, ranges = made
    heads = columns.shape[1]

    def tokens(size, width):
        return pl.BlockSpec((size, width), lambda c: (first + c, 0))

    def whole(x):
        return pl.BlockSpec(x.shape, lambda c: (0, 0))

    wide = tokens(STEP, lanes)
    shape = jax.ShapeDtypeStruct((length, lanes), BF16)
    return pl.pallas_call(
        functools.partial(outputs_kernel, first),
        out_shape=(shape, shape),
        grid=(steps,),
        in_specs=[
            wide,
            wide,
            tokens(STEP, states),
            tokens(STEP, states),
            wide,
            wide,
            tokens(STEP, 128),
            tokens(STEP // BLOCK * heads, BLOCK),
            tokens(STEP, heads),
            whole(ranges),
            whole(entry),
            whole(after),
            whole(skip),
            *[pl.BlockSpec(memory_space=pl.ANY) for _ in earlier],
        ],
        out_specs=(wide, wide),
        input_output_aliases={13 + k: k for k in range(len(earlier))},
        scratch_shapes=[pltpu.VMEM((3, 128, lanes), BF16)],
        compiler_params=pltpu.CompilerParams(vmem_limit_bytes=VMEM_BYTES),
        cost_estimate=pl.CostEstimate(
            flops=16 * steps * STEP * lanes * states,
            bytes_accessed=12 * steps * STEP * lanes,
            transcendentals=0,
        ),
        name="outputs",
    )(
        inputs, grad_out, write_keys, read_keys, entries, afters, parts, rows, columns, ranges,
        entry, after, skip, *earlier,
    )


def carried_states(summed, states, beside):
    axes = ("outer", "inner")
    devices = lax.axis_size(axes)
    here = lax.axis_index(axes)
    first = lax.rem(here, 2) == 0
    place = here // 2
    part = states // 2
    other = lax.ppermute(summed, axes, [(d, d ^ 1) for d in range(devices)])
    early = jnp.where(first, summed, other)
    late = jnp.where(first, other, summed)
    early_decay = early[2 * states : 2 * states + 1]
    late_decay = late[2 * states : 2 * states + 1]
    row = jnp.where(first, 0, part)

    def mine(x, start):
        return lax.dynamic_slice_in_dim(x, start + row, part, 0)

    push = mine(late, 0) + late_decay * mine(early, 0)
    pull = mine(early, states) + early_decay * mine(late, states)
    decay = jnp.broadcast_to(early_decay * late_decay, (8, summed.shape[1]))
    forth = jnp.concatenate([push, decay], axis=0)
    back = jnp.concatenate([pull, decay], axis=0)
    got = {}
    for m in range(1, devices // 2):
        sent = jnp.where(place < (place ^ m), forth, back)
        got[m] = lax.ppermute(sent, axes, [(d, d ^ (2 * m)) for d in range(devices)])
    got, made = beside(got)
    entry = jnp.zeros((part, summed.shape[1]), F32)
    after = jnp.zeros((part, summed.shape[1]), F32)
    for m, value in got.items():
        source = place ^ m
        weight = jnp.ones((1, summed.shape[1]), F32)
        for k, between in got.items():
            middle = place ^ k
            inside = ((source < middle) & (middle < place)) | ((place < middle) & (middle < source))
            weight = weight * jnp.where(inside, between[part : part + 1], 1.0)
        term = weight * value[:part]
        entry = entry + jnp.where(source < place, term, 0.0)
        after = after + jnp.where(source > place, term, 0.0)
    own = jnp.concatenate([entry, after], axis=0)
    others = lax.ppermute(own, axes, [(d, d ^ 1) for d in range(devices)])
    top = jnp.where(first, own, others)
    bottom = jnp.where(first, others, own)
    entry = jnp.concatenate([top[:part], bottom[:part]], axis=0)
    after = jnp.concatenate([top[part:], bottom[part:]], axis=0)
    entry = jnp.where(first, entry, early[:states] + early_decay * entry)
    after = jnp.where(first, late[states : 2 * states] + late_decay * after, after)
    return entry, after, made


def head_sum(terms, between):
    rows = terms.shape[0] // 4
    at = lax.axis_index("mp")

    def quarter(k):
        return lax.dynamic_slice_in_dim(terms, k * rows, rows, 0)

    def pick(even_half):
        return jnp.where(at < 2, even_half[0], even_half[1])

    to_far = jnp.where(lax.rem(at, 2) == 0, 3, 0)
    far = lax.ppermute(quarter(to_far), "mp", [(0, 1), (1, 0), (2, 3), (3, 2)])
    crossed = lax.ppermute(quarter(pick((2, 1))), "mp", [(1, 2), (2, 1)])
    done, (far, crossed, terms) = between(far, crossed, terms)
    onward = quarter(pick((3, 0))) + far
    last = lax.ppermute(onward, "mp", [(1, 3), (2, 0)])
    two_away = lax.ppermute(quarter(pick((2, 1))), "mp", [(0, 2), (3, 1)])
    near = lax.ppermute(quarter(pick((1, 2))), "mp", [(0, 1), (3, 2)])
    end = (at == 0) | (at == 3)
    own = quarter(at) + jnp.where(end, far, 0.0)
    return done, own, (crossed, two_away, near, last)


def on_device(inputs, log_decay, write_keys, read_keys, skip_gain, grad_out):
    states = write_keys.shape[1]
    steps = inputs.shape[0] // STEP
    skip = jnp.broadcast_to(jnp.repeat(skip_gain, WIDTH)[None], (8, inputs.shape[1]))
    summed, lead, tail = totals(inputs, grad_out, log_decay, write_keys, read_keys)

    def beside(got):
        made = local(inputs, grad_out, log_decay, write_keys, read_keys)
        return lax.optimization_barrier((got, made))

    entry, after, made = carried_states(summed, states, beside)
    read_terms, write_terms, *made = made
    terms = grads(lead, tail, read_terms, write_terms, entry, after)

    def part(first, count, earlier):
        return outputs(
            first, count, earlier, inputs, grad_out, write_keys, read_keys, made, entry, after, skip
        )

    if lax.axis_size("mp") == 4:
        early = steps // 2
        results, own, parts = head_sum(
            terms, lambda *held: lax.optimization_barrier((part(0, early, ()), held))
        )
        results, parts = lax.optimization_barrier((part(early, steps - early, results), parts))
        for term in parts:
            own = own + term
    else:
        own = lax.psum_scatter(terms, "mp", scatter_dimension=0, tiled=True)
        results = part(0, steps, ())
    return *results, own[:, states:], own[:, :states]


def solution(mesh):
    tokens = ("outer", "inner")
    return jax.shard_map(
        on_device,
        mesh=mesh,
        in_specs=(
            P(tokens, "mp"),
            P("mp", tokens),
            P(tokens, None),
            P(tokens, None),
            P("mp"),
            P(tokens, "mp"),
        ),
        out_specs=(
            P(tokens, "mp"),
            P(tokens, "mp"),
            P(("outer", "inner", "mp"), None),
            P(("outer", "inner", "mp"), None),
        ),
        check_vma=False,
    )
```

time: 153 us -> 109 us (0.71)
  Pallas kernels: 92.2 us -> 62.8 us
  waiting for transfers between devices: 30.5 us -> 11.9 us
  starting transfers between devices: 5.04 us -> 20.4 us
  between operations: 14.2 us -> 0.88 us
  other arithmetic: 3.14 us -> 8.59 us
  local copies, waits for them, and re-layouts: 7.15 us -> 3.95 us
    pallas_call x4, Pallas kernels: 58.9 us -> 41.2 us  [the longest x2 23.8 us: outputs(): pl.pallas_call(functools.partial(outputs_kernel, first), out_shape=(shape...]
    ppermute x0 -> x5, starting transfers between devices: none -> 15.3 us  [the longest x1 6.03 us: head_sum(): near = lax.ppermute(quarter(pick((1, 2))), 'mp', [(0, 1), (3, 2)])]
    reduce_scatter x2 -> x0, waiting for transfers between devices: 13.9 us -> none  [the longest x1 13.9 us: on_device(): lax.psum_scatter(read_terms, 'mp', scatter_dimension=0, tiled=True)]
    ppermute x3, waiting for transfers between devices: 13.4 us -> 0.01 us  [carried_states(): got[m] = lax.ppermute(sent, axes, [(d, d ^ 2 * m) for d in range(devices)])]
    pallas_call x1, Pallas kernels: 33.4 us -> 21.6 us  [local(): pl.pallas_call(local_kernel, out_shape=(jax.ShapeDtypeStruct((length, sta...]
    ppermute x0 -> x5, waiting for transfers between devices: none -> 7.21 us  [the longest x1 7.2 us: head_sum(): two_away = lax.ppermute(quarter(pick((2, 1))), 'mp', [(0, 2), (3, 1)])]
    unnamed x20 -> x4, local copies, waits for them, and re-layouts: 6.91 us -> 0.01 us
    add x0 -> x2, other arithmetic: none -> 2.82 us  [the longest x1 1.56 us: on_device(): own = own + term]
  transfers between devices with their start and end apart: 7 -> 10, of which waited for: 4 -> 3; matrix products, arithmetic and copies ran while one was open for 0% -> 1% of each run, Pallas kernels for 49% -> 42%
where the time goes in v2:
time: 109 us; the launch traced here: 108 us
  Pallas kernels  62.8 us (58%)
  starting transfers between devices  20.4 us (19%)
  waiting for transfers between devices  11.9 us (11%)
  other arithmetic  8.59 us (8%)
  local copies, waits for them, and re-layouts  3.95 us (4%)
    pallas_call x2, Pallas kernels, outputs(): pl.pallas_call(functools.partial(outputs_kernel, first), out_shape=(shape...  23.8 us
    pallas_call x1, Pallas kernels, local(): pl.pallas_call(local_kernel, out_shape=(jax.ShapeDtypeStruct((length, sta...  21.6 us
    pallas_call x1, Pallas kernels, totals(): pl.pallas_call(totals_kernel, out_shape=(jax.ShapeDtypeStruct((2 * states...  10.5 us
    ppermute x1, waiting for transfers between devices, head_sum(): two_away = lax.ppermute(quarter(pick((2, 1))), 'mp', [(0, 2), (3, 1)])  7.2 us
    pallas_call x1, Pallas kernels, grads(): pl.pallas_call(grads_kernel, out_shape=jax.ShapeDtypeStruct((length, 2 *...  6.92 us
    ppermute x1, starting transfers between devices, head_sum(): near = lax.ppermute(quarter(pick((1, 2))), 'mp', [(0, 1), (3, 2)])  6.03 us
    ppermute x1, starting transfers between devices, head_sum(): far = lax.ppermute(quarter(to_far), 'mp', [(0, 1), (1, 0), (2, 3), (3, 2)])  4.83 us
    ppermute x3, starting transfers between devices, carried_states(): got[m] = lax.ppermute(sent, axes, [(d, d ^ 2 * m) for d in range(devices)])  4.52 us
  transfers between devices with their start and end apart: 10, of which 3 were waited for; matrix products, arithmetic and copies ran while one was open for 1% of the time, Pallas kernels for 42%

profile of v2, /device:TPU:0, one launch (start us, length us, event | category | flops | bytes accessed | tf_op | source)
XLA Modules:
  0.0 108.5 jit_solution(6375279423145776818)
XLA Ops:
  0.6 10.5 %totals.1 = (f32[264,1024]{1,0:T(8,128)}, bf16[2048,1024]{1,0:T(8,128)(2,1)}, bf16[2048,1024]{1,0:T(8,128)(2,1)}) custom-call(bf16[2048,1024]{1,0:T(8,128)(2,1)} %inputs_ref.7, bf16[2048,1024]{1,0:T(8,128)(2,1)} %grad_ref.7, f32[16,2048]{1,0:T(8,128)} %ld_ref.3, bf16[2048,128]{1,0:T(8,128)(2,1)} %write_ref.7, bf16[2048,128]{1,0:T(8,128)(2,1)} %read_ref.7), custom_call_target="tpu_custom_call" | custom-call | flops 1610612736 | bytes 16777216 | tf_op jit(solution)/shard_map/totals/pallas_call | solution.py:141
  11.6 2.5 %collective-permute-done = f32[264,1024]{1,0:T(8,128)S(1)} collective-permute-done((f32[264,1024]{1,0:T(8,128)}, f32[264,1024]{1,0:T(8,128)S(1)}, u32[]{:S(2)}, u32[]{:S(2)}) %collective-permute-start) | collective-permute-done | bytes 1081376 | tf_op jit(solution)/shard_map/ppermute | solution.py:492
  14.2 1.5 %broadcast_select_fusion.1 = (f32[264,1024]{1,0:T(8,128)S(1)}, f32[264,1024]{1,0:T(8,128)S(1)}) fusion(f32[264,1024]{1,0:T(8,128)S(1)} %collective-permute-done, f32[264,1024]{1,0:T(8,128)} %get-tuple-element.41, pred[]{:T(512)S(6)} %eq.12), kind=kLoop, calls=%fused_computation.1 | loop fusion | flops 540672 | bytes 4325377 | tf_op jit(solution)/shard_map/jit(_where)/select_n | solution.py:494
  15.8 3.9 %collective-permute-start.3 = (f32[72,1024]{1,0:T(8,128)S(1)}, f32[72,1024]{1,0:T(8,128)S(1)}, u32[]{:S(2)}, u32[]{:S(2)}) collective-permute-start(f32[72,1024]{1,0:T(8,128)S(1)} %get-tuple-element.94), channel_id=1, source_target_pairs={{0,24},{4,28},{8,16},{12,20},{16,8},{20,12},{24,0},{28,4},{1,25},{... | collective-permute-start | bytes 884744 | tf_op jit(solution)/shard_map/ppermute | solution.py:510
  20.4 21.6 %local.1 = (f32[2048,128]{1,0:T(8,128)}, f32[2048,128]{1,0:T(8,128)}, bf16[2048,1024]{1,0:T(8,128)(2,1)}, bf16[2048,1024]{1,0:T(8,128)(2,1)}, bf16[2048,128]{1,0...) custom-call(bf16[2048,1024]{1,0:T(8,128)(2,1)} %inputs_ref.7, ...), custom_call_target="tpu_custom_call" | custom-call | flops 6442450944 | bytes 16777216 | tf_op jit(solution)/shard_map/local/pallas_call | solution.py:298
  42.1 0.8 fusion.5
  42.9 1.2 %select_add_fusion.1 = (f32[64,1024]{1,0:T(8,128)S(1)}, f32[64,1024]{1,0:T(8,128)S(1)}) fusion(f32[72,1024]{1,0:T(8,128)} %collective-permute-done.1, f32[72,1024]{1,0:T(8,128)} %collective-permute-done.2, f32[72,1024]{1,0:T(8,128)S(1)} %collective-permute-done.3, f32[1024]{0:T(1024)S(1)} %bitcast.11, f32[1024]{0:T(1024)S(1)} %bitcast.12, ...), kind=kLoop, calls=%fused_computation.14 | loop fusion | flops 851968 | bytes 1323014 | tf_op jit(solution)/shard_map/add | solution.py:522
  44.1 0.9 pad_maximum_fusion
  45.0 2.1 %collective-permute-done.4 = f32[128,1024]{1,0:T(8,128)S(1)} collective-permute-done((f32[128,1024]{1,0:T(8,128)}, f32[128,1024]{1,0:T(8,128)S(1)}, u32[]{:S(2)}, u32[]{:S(2)}) %collective-permute-start.4) | collective-permute-done | bytes 524320 | tf_op jit(solution)/shard_map/ppermute | solution.py:525
  47.3 1.2 %fusion = (f32[128,1024]{1,0:T(8,128)}, f32[128,1024]{1,0:T(8,128)}) fusion(f32[264,1024]{1,0:T(8,128)S(1)} %get-tuple-element.80, f32[64,1024]{1,0:T(8,128)S(1)} %get-tuple-element.101, f32[64,1024]{1,0:T(8,128)S(1)} %get-tuple-element.99, f32[1024]{0:T(1024)S(1)} %bitcast.9, pred[]{:T(512)S(6)} %eq.12, f32[1024]{0:T(1024)S(1)} %bitcast.7, ...), kind=kLoop, calls=%fused_computation.3 | loop fusion | flops 1048576 | bytes 3153921 | tf_op jit(solution)/shard_map/jit(_where)/select_n | solution.py:531
  48.5 6.9 %grads.1 = f32[2048,256]{1,0:T(8,128)} custom-call(bf16[2048,1024]{1,0:T(8,128)(2,1)} %get-tuple-element.61.lead_ref, bf16[2048,1024]{1,0:T(8,128)(2,1)} %get-tuple-element.62.tail_ref, f32[2048,128]{1,0:T(8,128)} %get-tuple-element.63.read_terms_ref, f32[2048,128]{1,0:T(8,128)} %get-tuple-element.64.write_terms_ref, ...), custom_call_target="tpu_custom_call" | custom-call | flops 1073741824 | bytes 8388608 | tf_op jit(solution)/shard_map/grads/pallas_call | solution.py:361
  55.4 2.3 %constant_dynamic-slice_fusion.2 = (f32[512,256]{1,0:T(8,128)}, f32[512,256]{1,0:T(8,128)}) fusion(f32[2048,256]{1,0:T(8,128)} %grads.1, s32[]{:T(128)S(6)} %select_n.230, s32[]{:T(128)S(6)} %select_n.228), kind=kLoop, calls=%fused_computation.36 | loop fusion | bytes 2097160 | tf_op jit(solution)/shard_map/dynamic_slice | solution.py:540
  57.7 0.9 collective-permute-start.6
  58.6 4.8 %collective-permute-start.5 = (f32[512,256]{1,0:T(8,128)}, f32[512,256]{1,0:T(8,128)S(1)}, u32[]{:S(2)}, u32[]{:S(2)}) collective-permute-start(f32[512,256]{1,0:T(8,128)} %get-tuple-element.86), channel_id=1, source_target_pairs={{0,1},{1,0},{2,3},{3,2},{4,5},{5,4},{6,7},{7,6},{8,9},{9,8},{10,11... | collective-permute-start | bytes 1572872 | tf_op jit(solution)/shard_map/ppermute | solution.py:546
  63.5 0.6 broadcast_in_dim.48.skip_ref
  64.1 11.9 %outputs.2 = (bf16[2048,1024]{1,0:T(8,128)(2,1)}, bf16[2048,1024]{1,0:T(8,128)(2,1)}) custom-call(bf16[2048,1024]{1,0:T(8,128)(2,1)} %inputs_ref.7, bf16[2048,1024]{1,0:T(8,128)(2,1)} %grad_ref.7, bf16[2048,128]{1,0:T(8,128)(2,1)} %write_ref.7, bf16[2048,128]{1,0:T(8,128)(2,1)} %read_ref.7, bf16[2048,1024]{1,0:T(8,128)(2,1)} %get-tuple-element.50.entries_ref, ...), custom_call_target="tpu_custom_call" | custom-call | flops 2147483648 | bytes 12582912 | tf_op jit(solution)/shard_map/outputs/pallas_call | solution.py:449
  76.1 1.3 %dynamic-slice_add_fusion = (f32[512,256]{1,0:T(8,128)}, f32[512,256]{1,0:T(8,128)}, f32[512,256]{1,0:T(8,128)}) fusion(f32[512,256]{1,0:T(8,128)S(1)} %collective-permute-done.5, f32[2048,256]{1,0:T(8,128)S(1)} %copy-done, s32[]{:T(128)S(6)} %select_n.234, s32[]{:T(128)S(6)} %select_n.232, s32[]{:T(128)S(6)} %select_n.230), kind=kLoop, calls=%fused_computation.10 | loop fusion | flops 131072 | bytes 3670028 | tf_op jit(solution)/shard_map/add | solution.py:549
  77.4 1.3 %collective-permute-start.9 = (f32[512,256]{1,0:T(8,128)}, f32[512,256]{1,0:T(8,128)}, u32[]{:S(2)}, u32[]{:S(2)}) collective-permute-start(f32[512,256]{1,0:T(8,128)} %get-tuple-element.82), channel_id=1, source_target_pairs={{1,3},{2,0},{5,7},{6,4},{9,11},{10,8},{13,15},{14,12},{17,19},{18,... | collective-permute-start | bytes 1572872 | tf_op jit(solution)/shard_map/ppermute | solution.py:550
  78.7 6.0 %collective-permute-start.8 = (f32[512,256]{1,0:T(8,128)}, f32[512,256]{1,0:T(8,128)}, u32[]{:S(2)}, u32[]{:S(2)}) collective-permute-start(f32[512,256]{1,0:T(8,128)} %get-tuple-element.83), channel_id=1, source_target_pairs={{0,1},{3,2},{4,5},{7,6},{8,9},{11,10},{12,13},{15,14},{16,17},{19,... | collective-permute-start | bytes 1572872 | tf_op jit(solution)/shard_map/ppermute | solution.py:552
  84.7 2.3 %collective-permute-start.7 = (f32[512,256]{1,0:T(8,128)}, f32[512,256]{1,0:T(8,128)}, u32[]{:S(2)}, u32[]{:S(2)}) collective-permute-start(f32[512,256]{1,0:T(8,128)} %get-tuple-element.84), channel_id=1, source_target_pairs={{0,2},{3,1},{4,6},{7,5},{8,10},{11,9},{12,14},{15,13},{16,18},{19,... | collective-permute-start | bytes 1572872 | tf_op jit(solution)/shard_map/ppermute | solution.py:551
  87.0 11.8 %outputs.3 = (bf16[2048,1024]{1,0:T(8,128)(2,1)}, bf16[2048,1024]{1,0:T(8,128)(2,1)}) custom-call(bf16[2048,1024]{1,0:T(8,128)(2,1)} %inputs_ref.7, bf16[2048,1024]{1,0:T(8,128)(2,1)} %grad_ref.7, bf16[2048,128]{1,0:T(8,128)(2,1)} %write_ref.7, bf16[2048,128]{1,0:T(8,128)(2,1)} %read_ref.7, ...), custom_call_target="tpu_custom_call", output_to_operand_aliasing={{0}: (13, {}), {1}: (14, {})} | custom-call | flops 2147483648 | bytes 12582912 | tf_op jit(solution)/shard_map/outputs/pallas_call | solution.py:449
  98.9 7.2 %collective-permute-done.7 = f32[512,256]{1,0:T(8,128)} collective-permute-done((f32[512,256]{1,0:T(8,128)}, f32[512,256]{1,0:T(8,128)}, u32[]{:S(2)}, u32[]{:S(2)}) %collective-permute-start.7) | collective-permute-done | bytes 524320 | tf_op jit(solution)/shard_map/ppermute | solution.py:551
  106.1 1.6 %add_add_fusion = f32[512,256]{1,0:T(8,128)S(1)} fusion(f32[512,256]{1,0:T(8,128)} %collective-permute-done.9, f32[512,256]{1,0:T(8,128)} %collective-permute-done.8, f32[512,256]{1,0:T(8,128)} %collective-permute-done.7, f32[512,256]{1,0:T(8,128)S(1)} %collective-permute-done.6, f32[512,256]{1,0:T(8,128)S(1)} %collective-permute-done.5, ...), kind=kLoop, calls=%fused_computation.9 | loop fusion | flops 786432 | bytes 3670021 | tf_op jit(solution)/shard_map/add | solution.py:584
  107.6 0.8 fusion.9
  (24 shorter events, 1.7 us)
Async XLA Ops:
  11.1 3.1 %collective-permute-start = (f32[264,1024]{1,0:T(8,128)}, f32[264,1024]{1,0:T(8,128)S(1)}, u32[]{:S(2)}, u32[]{:S(2)}) collective-permute-start(f32[264,1024]{1,0:T(8,128)} %get-tuple-element.41), channel_id=1, source_target_pairs={{0,4},{4,0},{8,12},{12,8},{16,20},{20,16},{24,28},{28,24},{1,5},{5... | collective-permute-start | bytes 3244040 | tf_op jit(solution)/shard_map/ppermute | solution.py:492
  15.8 26.2 %collective-permute-start.3 = (f32[72,1024]{1,0:T(8,128)S(1)}, f32[72,1024]{1,0:T(8,128)S(1)}, u32[]{:S(2)}, u32[]{:S(2)}) collective-permute-start(f32[72,1024]{1,0:T(8,128)S(1)} %get-tuple-element.94), channel_id=1, source_target_pairs={{0,24},{4,28},{8,16},{12,20},{16,8},{20,12},{24,0},{28,4},{1,25},{... | collective-permute-start | bytes 884744 | tf_op jit(solution)/shard_map/ppermute | solution.py:510
  19.7 22.4 %collective-permute-start.2 = (f32[72,1024]{1,0:T(8,128)S(1)}, f32[72,1024]{1,0:T(8,128)}, u32[]{:S(2)}, u32[]{:S(2)}) collective-permute-start(f32[72,1024]{1,0:T(8,128)S(1)} %get-tuple-element.95), channel_id=1, source_target_pairs={{0,16},{4,20},{8,24},{12,28},{16,0},{20,4},{24,8},{28,12},{1,17},{... | collective-permute-start | bytes 884744 | tf_op jit(solution)/shard_map/ppermute | solution.py:510
  20.2 21.9 %collective-permute-start.1 = (f32[72,1024]{1,0:T(8,128)S(1)}, f32[72,1024]{1,0:T(8,128)}, u32[]{:S(2)}, u32[]{:S(2)}) collective-permute-start(f32[72,1024]{1,0:T(8,128)S(1)} %get-tuple-element.96), channel_id=1, source_target_pairs={{0,8},{4,12},{8,0},{12,4},{16,24},{20,28},{24,16},{28,20},{1,9},{5... | collective-permute-start | bytes 884744 | tf_op jit(solution)/shard_map/ppermute | solution.py:510
  45.0 2.1 %collective-permute-start.4 = (f32[128,1024]{1,0:T(8,128)}, f32[128,1024]{1,0:T(8,128)S(1)}, u32[]{:S(2)}, u32[]{:S(2)}) collective-permute-start(f32[128,1024]{1,0:T(8,128)} %pad_maximum_fusion), channel_id=1, source_target_pairs={{0,4},{4,0},{8,12},{12,8},{16,20},{20,16},{24,28},{28,24},{1,5},{5... | collective-permute-start | bytes 1572872 | tf_op jit(solution)/shard_map/ppermute | solution.py:525
  55.4 8.0 %copy-start.1 = (f32[16]{0:T(128)S(1)}, f32[16]{0:T(128)}, u32[]{:S(2)}) copy-start(f32[16]{0:T(128)} %param.10) | copy-start | bytes 196
  57.7 18.4 %collective-permute-start.6 = (f32[512,256]{1,0:T(8,128)}, f32[512,256]{1,0:T(8,128)S(1)}, u32[]{:S(2)}, u32[]{:S(2)}) collective-permute-start(f32[512,256]{1,0:T(8,128)} %get-tuple-element.85), channel_id=1, source_target_pairs={{1,2},{2,1},{5,6},{6,5},{9,10},{10,9},{13,14},{14,13},{17,18},{18,... | collective-permute-start | bytes 1572872 | tf_op jit(solution)/shard_map/ppermute | solution.py:547
  58.6 17.6 %collective-permute-start.5 = (f32[512,256]{1,0:T(8,128)}, f32[512,256]{1,0:T(8,128)S(1)}, u32[]{:S(2)}, u32[]{:S(2)}) collective-permute-start(f32[512,256]{1,0:T(8,128)} %get-tuple-element.86), channel_id=1, source_target_pairs={{0,1},{1,0},{2,3},{3,2},{4,5},{5,4},{6,7},{7,6},{8,9},{9,8},{10,11... | collective-permute-start | bytes 1572872 | tf_op jit(solution)/shard_map/ppermute | solution.py:546
  64.1 12.0 %copy-start = (f32[2048,256]{1,0:T(8,128)S(1)}, f32[2048,256]{1,0:T(8,128)}, u32[]{:S(2)}) copy-start(f32[2048,256]{1,0:T(8,128)} %grads.1) | copy-start | bytes 6291460
  77.4 21.5 %collective-permute-start.9 = (f32[512,256]{1,0:T(8,128)}, f32[512,256]{1,0:T(8,128)}, u32[]{:S(2)}, u32[]{:S(2)}) collective-permute-start(f32[512,256]{1,0:T(8,128)} %get-tuple-element.82), channel_id=1, source_target_pairs={{1,3},{2,0},{5,7},{6,4},{9,11},{10,8},{13,15},{14,12},{17,19},{18,... | collective-permute-start | bytes 1572872 | tf_op jit(solution)/shard_map/ppermute | solution.py:550
  78.7 20.2 %collective-permute-start.8 = (f32[512,256]{1,0:T(8,128)}, f32[512,256]{1,0:T(8,128)}, u32[]{:S(2)}, u32[]{:S(2)}) collective-permute-start(f32[512,256]{1,0:T(8,128)} %get-tuple-element.83), channel_id=1, source_target_pairs={{0,1},{3,2},{4,5},{7,6},{8,9},{11,10},{12,13},{15,14},{16,17},{19,... | collective-permute-start | bytes 1572872 | tf_op jit(solution)/shard_map/ppermute | solution.py:552
  84.7 21.4 %collective-permute-start.7 = (f32[512,256]{1,0:T(8,128)}, f32[512,256]{1,0:T(8,128)}, u32[]{:S(2)}, u32[]{:S(2)}) collective-permute-start(f32[512,256]{1,0:T(8,128)} %get-tuple-element.84), channel_id=1, source_target_pairs={{0,2},{3,1},{4,6},{7,5},{8,10},{11,9},{12,14},{15,13},{16,18},{19,... | collective-permute-start | bytes 1572872 | tf_op jit(solution)/shard_map/ppermute | solution.py:551

commit v3 on v2

v3 whole, which is shorter than its diff:
```python
import functools

import jax
import jax.numpy as jnp
from jax import lax
from jax.experimental import pallas as pl
from jax.experimental.pallas import tpu as pltpu
from jax.sharding import PartitionSpec as P

WIDTH = 64
BLOCK = 128
STEP = 512
FAR = -1e30
LOG2E = 1.4426950408889634
VMEM_BYTES = 60 * 1024 * 1024
F32 = jnp.float32
BF16 = jnp.bfloat16


def dot(a, b, over_a, over_b):
    return lax.dot_general(a, b, (((over_a,), (over_b,)), ((), ())), preferred_element_type=F32)


def minus_expm1(y):
    series = 1.0 + y * (1.0 / 9.0)
    for k in (8.0, 7.0, 6.0, 5.0, 4.0, 3.0, 2.0):
        series = 1.0 + y * (1.0 / k) * series
    return jnp.where(y > -0.4, -y * series, 1.0 - jnp.exp(y))


def iota(shape, dimension):
    return lax.broadcasted_iota(jnp.int32, shape, dimension)


def spread_matrix(heads, group):
    shape = (128, heads * WIDTH)
    row = iota(shape, 0) - 2 * heads * group
    gap = iota(shape, 1) - WIDTH * jnp.where(row < heads, row, row - heads)
    inside = (row >= 0) & (row < 2 * heads) & (gap >= 0) & (gap < WIDTH)
    return jnp.where(inside, 1.0, 0.0).astype(BF16)


def row_spread_matrix(heads):
    shape = (heads, heads * WIDTH)
    gap = iota(shape, 1) - WIDTH * iota(shape, 0)
    one = jnp.where((gap >= 0) & (gap < WIDTH), 1.0, 0.0)
    return jnp.concatenate([one, one, one], axis=0).astype(BF16)


def three(x):
    high = x.astype(BF16).astype(F32)
    middle = (x - high).astype(BF16).astype(F32)
    return high, middle, x - high - middle


def block_sums(rows):
    shape = (BLOCK, 2 * BLOCK)
    source, target = iota(shape, 0), iota(shape, 1)
    upto = jnp.where(source <= target, 1.0, 0.0)
    beyond = jnp.where(source > target - BLOCK, 1.0, 0.0)
    within = jnp.where(target < BLOCK, upto, beyond).astype(BF16)
    count = rows.shape[0]
    both = dot(jnp.concatenate(three(rows), axis=0).astype(BF16), within, 1, 0)
    both = both[:count] + both[count : 2 * count] + both[2 * count :]
    return both[:, :BLOCK], both[:, BLOCK:]


def stacked(x):
    return jnp.concatenate(
        [x[:, at : at + BLOCK] for at in range(0, x.shape[1], BLOCK)], axis=0
    )


def block_factors(ld_ref):
    ld = ld_ref[...]
    gain = stacked(jnp.sqrt(minus_expm1(2.0 * ld)))
    before, behind = block_sums(stacked(ld))
    return gain, before, behind


def in_columns(groups, heads, block):
    parts = []
    for factor in groups:
        rows = factor[block * heads : block * heads + heads]
        high = rows.astype(BF16).astype(F32)
        parts += [high, rows - high]
    parts.append(jnp.zeros((128 - 2 * heads * len(groups), BLOCK), F32))
    rows = jnp.concatenate(parts, axis=0).astype(BF16)
    eye = jnp.where(iota((BLOCK, BLOCK), 0) == iota((BLOCK, BLOCK), 1), 1.0, 0.0).astype(BF16)
    return dot(eye, rows, 1, 1).astype(BF16)


def starts_and_ends(before, heads, count):
    totals = [before[c * heads : c * heads + heads, BLOCK - 1 :] for c in range(count)]
    start = [jnp.zeros((heads, 1), F32)]
    for total in totals:
        start.append(start[-1] + total)
    end = [jnp.zeros((heads, 1), F32)]
    for total in totals[::-1]:
        end.append(end[-1] + total)
    since = jnp.concatenate(start[:count], axis=0)
    until = jnp.concatenate(end[:count][::-1], axis=0)
    return since, until, start[count]


def totals_kernel(
    inputs_ref, grad_ref, ld_ref, write_ref, read_ref, out_ref, parts, lanes_of
):
    step = pl.program_id(0)
    heads = ld_ref.shape[0]
    states = write_ref.shape[1]
    count = ld_ref.shape[1] // BLOCK

    @pl.when(step == 0)
    def _():
        lanes_of[0] = spread_matrix(heads, 0)
        lanes_of[1] = spread_matrix(heads, 1)
        gain, before, behind = block_factors(ld_ref)
        since, until, whole = starts_and_ends(before, heads, count)
        lead = jnp.exp(since + before)
        tail = gain * jnp.exp(until + behind)
        for c in range(count):
            parts[c * BLOCK : c * BLOCK + BLOCK] = in_columns((lead, tail), heads, c)
        out_ref[...] = jnp.zeros_like(out_ref)
        whole = jnp.concatenate(three(jnp.exp(whole)), axis=0)
        whole = jnp.broadcast_to(whole, (3 * heads, 128)).astype(BF16)
        out_ref[2 * states :] = dot(whole, row_spread_matrix(heads), 0, 0)[0:8]

    at = pl.ds(pl.multiple_of(step * STEP, STEP), STEP)
    here = parts[at, :]
    lead = (dot(here, lanes_of[0], 1, 0) * grad_ref[...].astype(F32)).astype(BF16)
    out_ref[states : 2 * states] += dot(read_ref[...], lead, 0, 0)
    tail = (dot(here, lanes_of[1], 1, 0) * inputs_ref[...].astype(F32)).astype(BF16)
    out_ref[0:states] += dot(write_ref[...], tail, 0, 0)


def totals(inputs, grad_out, log_decay, write_keys, read_keys):
    length, lanes = inputs.shape
    heads = log_decay.shape[0]
    states = write_keys.shape[1]
    wide = pl.BlockSpec((STEP, lanes), lambda c: (c, 0))
    keys = pl.BlockSpec((STEP, states), lambda c: (c, 0))
    return pl.pallas_call(
        totals_kernel,
        out_shape=jax.ShapeDtypeStruct((2 * states + 8, lanes), F32),
        grid=(length // STEP,),
        in_specs=[wide, wide, pl.BlockSpec((heads, length), lambda c: (0, 0)), keys, keys],
        out_specs=pl.BlockSpec((2 * states + 8, lanes), lambda c: (0, 0)),
        scratch_shapes=[
            pltpu.VMEM((length, 128), BF16),
            pltpu.VMEM((2, 128, lanes), BF16),
        ],
        compiler_params=pltpu.CompilerParams(vmem_limit_bytes=VMEM_BYTES),
        cost_estimate=pl.CostEstimate(
            flops=6 * length * lanes * states, bytes_accessed=4 * length * lanes, transcendentals=0
        ),
        name="totals",
    )(inputs, grad_out, log_decay, write_keys, read_keys)


def factors_kernel(ld_ref, near_ref, rows_ref, decays_ref, ranges_ref):
    heads, length = ld_ref.shape
    count = length // BLOCK
    gain, before, behind = block_factors(ld_ref)
    lead = jnp.exp(before)
    tail = gain * jnp.exp(behind)
    rows_ref[...] = before * LOG2E
    lasts = []
    for c in range(count):
        at = slice(c * BLOCK, c * BLOCK + BLOCK)
        near_ref[at] = in_columns((lead, tail, gain), heads, c)
        lasts.append(lead[c * heads : c * heads + heads, BLOCK - 1 :])
    last = jnp.concatenate(lasts, axis=1)
    decays = dot(jnp.concatenate(three(last), axis=0).astype(BF16), row_spread_matrix(heads), 0, 0)
    decays_ref[...] = decays
    ones = jnp.ones((1, heads * WIDTH), F32)
    after, before = [ones], [ones]
    for c in range(count - 1):
        after.append(after[-1] * decays[c : c + 1])
        before.append(before[-1] * decays[count - 1 - c : count - c])
    ranges_ref[:count] = jnp.concatenate(after, axis=0)
    ranges_ref[count:] = jnp.concatenate(before[::-1], axis=0)


def factors(log_decay):
    heads, length = log_decay.shape
    count = length // BLOCK
    lanes = heads * WIDTH
    return pl.pallas_call(
        factors_kernel,
        out_shape=(
            jax.ShapeDtypeStruct((length, 128), BF16),
            jax.ShapeDtypeStruct((count * heads, BLOCK), F32),
            jax.ShapeDtypeStruct((count, lanes), F32),
            jax.ShapeDtypeStruct((2 * count, lanes), F32),
        ),
        compiler_params=pltpu.CompilerParams(vmem_limit_bytes=VMEM_BYTES),
        cost_estimate=pl.CostEstimate(
            flops=heads * length * 6000, bytes_accessed=1000 * length, transcendentals=0
        ),
        name="factors",
    )(log_decay)


def halves(pair):
    first = iota(pair.shape, 1) < WIDTH
    zero = jnp.zeros_like(pair)
    return jnp.concatenate([jnp.where(first, pair, zero), jnp.where(first, zero, pair)], axis=0)


def lower_block():
    return iota((BLOCK, BLOCK), 0) >= iota((BLOCK, BLOCK), 1)


def key_block(scaled, grad, rows):
    heads = rows.shape[0]
    columns = rows.T
    lower = lower_block()
    gathered = jnp.zeros((BLOCK, BLOCK), F32)
    for pair in range(heads // 2):
        lanes = slice(pair * 128, pair * 128 + 128)
        products = dot(grad[:, lanes], halves(scaled[:, lanes]), 1, 1)
        for j in range(2):
            head = 2 * pair + j
            gap = columns[:, head : head + 1] - rows[head : head + 1, :]
            decay = jnp.exp2(jnp.where(lower, gap, FAR))
            gathered += products[:, j * BLOCK : j * BLOCK + BLOCK] * decay
    return gathered


def two_parts(x):
    high = x.astype(BF16)
    return high, (x - high.astype(F32)).astype(BF16)


def local_kernel(
    plan_ref,
    inputs_ref,
    grad_ref,
    write_ref,
    read_ref,
    parts_ref,
    rows_ref,
    decays_ref,
    ranges_ref,
    entries_ref,
    afters_ref,
    read_terms_ref,
    write_terms_ref,
    far_lead_ref,
    far_tail_ref,
    entry,
    leads,
    tails,
    states_in,
    states_out,
    write_terms,
    lanes_of,
):
    step = pl.program_id(0)
    states, lanes = entry.shape
    heads = lanes // WIDTH
    count = decays_ref.shape[0]
    steps = decays_ref.shape[0] * BLOCK // STEP
    inner = STEP // BLOCK

    @pl.when(step == 0)
    def _():
        for k in range(3):
            lanes_of[k] = spread_matrix(heads, k)
        entry[...] = jnp.zeros_like(entry)

    @pl.when(step < steps)
    def _():
        here = parts_ref[...]
        whole = pl.ds(pl.multiple_of(step * STEP, STEP), STEP)
        leads[whole, :] = (dot(here, lanes_of[0], 1, 0) * grad_ref[...].astype(F32)).astype(BF16)
        tails[whole, :] = (dot(here, lanes_of[1], 1, 0) * inputs_ref[...].astype(F32)).astype(BF16)
        entries_ref[...] = entry[...].astype(BF16)
        for k in range(inner):
            block = step * inner + k
            at = pl.ds(pl.multiple_of(block * BLOCK, BLOCK), BLOCK)
            state = entry[...]
            states_in[k * BLOCK : k * BLOCK + BLOCK] = state.astype(BF16)
            entry[...] = state * decays_ref[pl.ds(block, 1), :] + dot(
                write_ref[at, :], tails[at, :], 0, 0
            )

    @pl.when((step == plan_ref[0]) | (step == plan_ref[1]))
    def _():
        scaled = (dot(parts_ref[...], lanes_of[2], 1, 0) * inputs_ref[...].astype(F32)).astype(BF16)
        for k in range(inner):
            inside = slice(k * BLOCK, k * BLOCK + BLOCK)
            block = step * inner + k
            at = pl.ds(pl.multiple_of(block * BLOCK, BLOCK), BLOCK)
            write, read = write_ref[at, :], read_ref[at, :]
            lead, tail = leads[at, :], tails[at, :]
            far_lead_ref[inside] = (lead.astype(F32) * ranges_ref[pl.ds(block, 1), :]).astype(BF16)
            far_tail_ref[inside] = (
                tail.astype(F32) * ranges_ref[pl.ds(count + block, 1), :]
            ).astype(BF16)
            high, low = two_parts(
                key_block(scaled[inside], grad_ref[inside], rows_ref[k * heads : k * heads + heads, :])
            )
            read_terms_ref[inside] = (
                dot(lead, states_in[inside], 1, 1) + dot(high, write, 1, 0) + dot(low, write, 1, 0)
            )
            write_terms[at, :] = dot(high, read, 0, 0) + dot(low, read, 0, 0)

    @pl.when(step == steps)
    def _():
        state = jnp.zeros_like(entry)
        for block in reversed(range(count)):
            at = slice(block * BLOCK, block * BLOCK + BLOCK)
            states_out[at] = state.astype(BF16)
            state = state * decays_ref[block : block + 1] + dot(read_ref[at, :], leads[at], 0, 0)
        for quarter in range(steps):
            last = quarter * STEP + STEP - BLOCK
            afters_ref[quarter * states : quarter * states + states] = states_out[last : last + BLOCK]
        for slot in range(2):
            for k in range(inner):
                place = slot * STEP + k * BLOCK
                at = pl.ds(pl.multiple_of(plan_ref[slot] * STEP + k * BLOCK, BLOCK), BLOCK)
                write_terms_ref[place : place + BLOCK] = write_terms[at, :] + dot(
                    tails[at, :], states_out[at, :], 1, 1
                )


def local(plan, inputs, grad_out, write_keys, read_keys, parts, rows, decays, ranges):
    length, lanes = inputs.shape
    heads = lanes // WIDTH
    states = write_keys.shape[1]
    assert states == BLOCK and 6 * heads <= 128
    steps = length // STEP

    def forth(c, plan):
        return jnp.minimum(c, steps - 1)

    def slot_forth(c, plan):
        return jnp.where(c > plan[0], 1, 0)

    def all_of(c, plan):
        return 0

    def whole(x):
        return pl.BlockSpec(x.shape, lambda c, plan: (0, 0))

    def tokens(at, size, width):
        return pl.BlockSpec((size, width), lambda c, plan: (at(c, plan), 0))

    return pl.pallas_call(
        local_kernel,
        out_shape=(
            jax.ShapeDtypeStruct((steps * states, lanes), BF16),
            jax.ShapeDtypeStruct((steps * states, lanes), BF16),
            jax.ShapeDtypeStruct((2 * STEP, states), F32),
            jax.ShapeDtypeStruct((2 * STEP, states), F32),
            jax.ShapeDtypeStruct((2 * STEP, lanes), BF16),
            jax.ShapeDtypeStruct((2 * STEP, lanes), BF16),
        ),
        grid_spec=pltpu.PrefetchScalarGridSpec(
            num_scalar_prefetch=1,
            grid=(steps + 1,),
            in_specs=[
                tokens(forth, STEP, lanes),
                tokens(forth, STEP, lanes),
                whole(write_keys),
                whole(read_keys),
                tokens(forth, STEP, 128),
                tokens(forth, STEP // BLOCK * heads, BLOCK),
                whole(decays),
                whole(ranges),
            ],
            out_specs=(
                tokens(forth, states, lanes),
                tokens(all_of, steps * states, lanes),
                tokens(slot_forth, STEP, states),
                tokens(all_of, 2 * STEP, states),
                tokens(slot_forth, STEP, lanes),
                tokens(slot_forth, STEP, lanes),
            ),
            scratch_shapes=[
                pltpu.VMEM((states, lanes), F32),
                pltpu.VMEM((length, lanes), BF16),
                pltpu.VMEM((length, lanes), BF16),
                pltpu.VMEM((STEP, lanes), BF16),
                pltpu.VMEM((length, lanes), BF16),
                pltpu.VMEM((length, states), F32),
                pltpu.VMEM((3, 128, lanes), BF16),
            ],
        ),
        compiler_params=pltpu.CompilerParams(vmem_limit_bytes=VMEM_BYTES),
        cost_estimate=pl.CostEstimate(
            flops=24 * length * lanes * states, bytes_accessed=8 * length * lanes, transcendentals=0
        ),
        name="local",
    )(plan, inputs, grad_out, write_keys, read_keys, parts, rows, decays, ranges)


def early_grads_kernel(
    plan_ref,
    lead_ref,
    tail_ref,
    read_terms_ref,
    write_terms_ref,
    own_ref,
    others_ref,
    other_ref,
    entry_ref,
    after_ref,
    far_ref,
    crossed_ref,
    halved,
):
    step = pl.program_id(0)
    states, lanes = entry_ref.shape
    part = states // 2

    @pl.when(step == 0)
    def _():
        first = plan_ref[4] == 1
        own, others = own_ref[...], others_ref[...]
        top, bottom = jnp.where(first, own, others), jnp.where(first, others, own)
        entry = jnp.concatenate([top[:part], bottom[:part]], axis=0)
        after = jnp.concatenate([top[part:], bottom[part:]], axis=0)
        decay = other_ref[2 * states : 2 * states + 1]
        entry = jnp.where(first, entry, other_ref[:states] + decay * entry)
        after = jnp.where(first, other_ref[states : 2 * states] + decay * after, after)
        entry_ref[...] = entry
        after_ref[...] = after
        halved[0] = entry.astype(BF16)
        halved[1] = after.astype(BF16)

    read = read_terms_ref[...] + dot(lead_ref[...], halved[0], 1, 1)
    write = write_terms_ref[...] + dot(tail_ref[...], halved[1], 1, 1)
    for at, out in ((plan_ref[5], far_ref), (1 - plan_ref[5], crossed_ref)):

        @pl.when(step == at)
        def _():
            out[:, :states] = read
            out[:, states:] = write


def early_grads(plan, lead, tail, read_terms, write_terms, own, others, other):
    lanes = lead.shape[1]
    states = read_terms.shape[1]

    def tokens(width):
        return pl.BlockSpec((STEP, width), lambda c, plan: (c, 0))

    def whole(x):
        return pl.BlockSpec(x.shape, lambda c, plan: (0, 0))

    state = jax.ShapeDtypeStruct((states, lanes), F32)
    terms = jax.ShapeDtypeStruct((STEP, 2 * states), F32)
    shapes = (state, state, terms, terms)
    return pl.pallas_call(
        early_grads_kernel,
        out_shape=shapes,
        grid_spec=pltpu.PrefetchScalarGridSpec(
            num_scalar_prefetch=1,
            grid=(2,),
            in_specs=[
                tokens(lanes),
                tokens(lanes),
                tokens(states),
                tokens(states),
                whole(own),
                whole(others),
                whole(other),
            ],
            out_specs=tuple(whole(x) for x in shapes),
            scratch_shapes=[pltpu.VMEM((2, states, lanes), BF16)],
        ),
        compiler_params=pltpu.CompilerParams(vmem_limit_bytes=VMEM_BYTES),
        cost_estimate=pl.CostEstimate(
            flops=8 * STEP * lanes * states, bytes_accessed=8 * STEP * lanes, transcendentals=0
        ),
        name="early_grads",
    )(plan, lead, tail, read_terms, write_terms, own, others, other)


def combine_kernel(place_ref, *refs):
    *got, out_ref = refs
    place = place_ref[0]
    part, lanes = got[0].shape[0] - 8, got[0].shape[1]
    entry = jnp.zeros((part, lanes), F32)
    after = jnp.zeros((part, lanes), F32)
    for m, value in enumerate(got, 1):
        source = place ^ m
        weight = jnp.ones((1, lanes), F32)
        for k, between in enumerate(got, 1):
            middle = place ^ k
            inside = ((source < middle) & (middle < place)) | ((place < middle) & (middle < source))
            weight = weight * jnp.where(inside, between[part : part + 1], 1.0)
        term = weight * value[:part]
        entry = entry + jnp.where(source < place, term, 0.0)
        after = after + jnp.where(source > place, term, 0.0)
    out_ref[:part] = entry
    out_ref[part:] = after


def combine(place, got):
    rows, lanes = got[0].shape
    return pl.pallas_call(
        combine_kernel,
        out_shape=jax.ShapeDtypeStruct((2 * (rows - 8), lanes), F32),
        in_specs=[pl.BlockSpec(memory_space=pltpu.SMEM)]
        + [pl.BlockSpec(memory_space=pltpu.VMEM)] * len(got),
        out_specs=pl.BlockSpec(memory_space=pltpu.VMEM),
        compiler_params=pltpu.CompilerParams(vmem_limit_bytes=VMEM_BYTES),
        cost_estimate=pl.CostEstimate(
            flops=4 * len(got) * rows * lanes,
            bytes_accessed=4 * (len(got) + 2) * rows * lanes,
            transcendentals=0,
        ),
        name="combine",
    )(place.reshape(1), *got)


def outputs_kernel(
    offset,
    with_terms,
    aliased,
    plan_ref,
    inputs_ref,
    grad_ref,
    write_ref,
    read_ref,
    entries_ref,
    afters_ref,
    parts_ref,
    rows_ref,
    decays_ref,
    ranges_ref,
    entry_ref,
    after_ref,
    skip_ref,
    *rest,
):
    mixed_ref, grad_in_ref, *terms, lanes_of, states_in, states_out, skip_row = rest[aliased:]
    step = pl.program_id(0)
    states = write_ref.shape[1]
    heads = skip_ref.shape[1]
    count = ranges_ref.shape[0] // 2
    inner = STEP // BLOCK

    @pl.when(step == 0)
    def _():
        for k in range(3):
            lanes_of[k] = spread_matrix(heads, k)
        gains = jnp.concatenate(three(jnp.broadcast_to(skip_ref[...], (8, heads))), axis=1)
        skip_row[...] = dot(gains.astype(BF16), row_spread_matrix(heads), 1, 0)

    leads, tails, gains = [dot(parts_ref[...], lanes_of[k], 1, 0) for k in range(3)]
    scaled = (gains * inputs_ref[...].astype(F32)).astype(BF16)
    lead = (leads * grad_ref[...].astype(F32)).astype(BF16)
    tail = (tails * inputs_ref[...].astype(F32)).astype(BF16)
    start = plan_ref[offset + step] * inner
    state = entries_ref[...].astype(F32) + ranges_ref[pl.ds(start, 1), :] * entry_ref[...]
    for k in range(inner):
        at = slice(k * BLOCK, k * BLOCK + BLOCK)
        states_in[at] = state.astype(BF16)
        if k < inner - 1:
            state = state * decays_ref[pl.ds(start + k, 1), :] + dot(write_ref[at, :], tail[at], 0, 0)
    end = start + inner - 1
    state = afters_ref[...].astype(F32) + ranges_ref[pl.ds(count + end, 1), :] * after_ref[...]
    for k in reversed(range(inner)):
        at = slice(k * BLOCK, k * BLOCK + BLOCK)
        states_out[at] = state.astype(BF16)
        if k > 0:
            state = state * decays_ref[pl.ds(start + k, 1), :] + dot(read_ref[at, :], lead[at], 0, 0)
    found = []
    for k in range(inner):
        at = slice(k * BLOCK, k * BLOCK + BLOCK)
        write, read = write_ref[at, :], read_ref[at, :]
        grad = grad_ref[at]
        entry, after = states_in[at], states_out[at]
        skip = skip_row[0:1]
        out_rest = leads[at] * dot(read, entry, 1, 0) + skip * inputs_ref[at].astype(F32)
        back_rest = tails[at] * dot(write, after, 1, 0) + skip * grad.astype(F32)
        scores = dot(read, write, 1, 1)
        rows = rows_ref[k * heads : k * heads + heads, :]
        columns = rows.T
        lower = lower_block()
        gathered = jnp.zeros((BLOCK, BLOCK), F32)
        for pair in range(heads // 2):
            lanes = slice(pair * 128, pair * 128 + 128)
            scaled_pair = halves(scaled[at, lanes])
            if with_terms:
                products = dot(grad[:, lanes], scaled_pair, 1, 1)
            mixing = []
            for j in range(2):
                head = 2 * pair + j
                gap = columns[:, head : head + 1] - rows[head : head + 1, :]
                decay = jnp.exp2(jnp.where(lower, gap, FAR))
                mixing.append((scores * decay).astype(BF16))
                if with_terms:
                    gathered += products[:, j * BLOCK : j * BLOCK + BLOCK] * decay
            mixed = dot(jnp.concatenate(mixing, axis=1), scaled_pair, 1, 0)
            mixed_ref[at, lanes] = (mixed + out_rest[:, lanes]).astype(BF16)
            back = dot(jnp.concatenate(mixing, axis=0), halves(grad[:, lanes]), 0, 0)
            grad_in_ref[at, lanes] = (gains[at, lanes] * back + back_rest[:, lanes]).astype(BF16)
        if with_terms:
            high, low = two_parts(gathered)
            found.append(
                (
                    dot(lead[at], entry, 1, 1) + dot(high, write, 1, 0) + dot(low, write, 1, 0),
                    dot(tail[at], after, 1, 1) + dot(high, read, 0, 0) + dot(low, read, 0, 0),
                )
            )
    for k, (for_read, for_write) in enumerate(found):
        terms[0][k * BLOCK : k * BLOCK + BLOCK, :states] = for_read
        terms[0][k * BLOCK : k * BLOCK + BLOCK, states:] = for_write


def outputs(
    plan, offset, steps, with_terms, earlier, inputs, grad_out, write_keys, read_keys, made, entry, after, skip
):
    assert steps == 1 or not with_terms
    length, lanes = inputs.shape
    states = write_keys.shape[1]
    entries, afters, parts, rows, decays, ranges = made
    heads = lanes // WIDTH

    def tokens(size, width):
        return pl.BlockSpec((size, width), lambda c, plan: (plan[offset + c], 0))

    def whole(x):
        return pl.BlockSpec(x.shape, lambda c, plan: (0, 0))

    wide = tokens(STEP, lanes)
    shape = jax.ShapeDtypeStruct((length, lanes), BF16)
    terms = (jax.ShapeDtypeStruct((STEP, 2 * states), F32),) * with_terms
    return pl.pallas_call(
        functools.partial(outputs_kernel, offset, with_terms, len(earlier)),
        out_shape=(shape, shape, *terms),
        grid_spec=pltpu.PrefetchScalarGridSpec(
            num_scalar_prefetch=1,
            grid=(steps,),
            in_specs=[
                wide,
                wide,
                tokens(STEP, states),
                tokens(STEP, states),
                tokens(states, lanes),
                tokens(states, lanes),
                tokens(STEP, 128),
                tokens(STEP // BLOCK * heads, BLOCK),
                whole(decays),
                whole(ranges),
                whole(entry),
                whole(after),
                whole(skip),
                *[pl.BlockSpec(memory_space=pl.ANY) for _ in earlier],
            ],
            out_specs=(wide, wide, *[whole(x) for x in terms]),
            scratch_shapes=[
                pltpu.VMEM((3, 128, lanes), BF16),
                pltpu.VMEM((STEP, lanes), BF16),
                pltpu.VMEM((STEP, lanes), BF16),
                pltpu.VMEM((8, lanes), F32),
            ],
        ),
        input_output_aliases={14 + k: k for k in range(len(earlier))},
        compiler_params=pltpu.CompilerParams(vmem_limit_bytes=VMEM_BYTES),
        cost_estimate=pl.CostEstimate(
            flops=16 * steps * STEP * lanes * states, bytes_accessed=12 * steps * STEP * lanes, transcendentals=0
        ),
        name="outputs_and_terms" if with_terms else "outputs",
    )(
        plan, inputs, grad_out, write_keys, read_keys, entries, afters, parts, rows, decays, ranges,
        entry, after, skip, *earlier,
    )


def carried_states(summed, states, first_window, second_window):
    axes = ("outer", "inner")
    devices = lax.axis_size(axes)
    here = lax.axis_index(axes)
    first = lax.rem(here, 2) == 0
    place = here // 2
    part = states // 2
    other = lax.ppermute(summed, axes, [(d, d ^ 1) for d in range(devices)])
    other, made = first_window(other)
    early_decay = jnp.where(first, summed, other)[2 * states : 2 * states + 1]
    late_decay = jnp.where(first, other, summed)[2 * states : 2 * states + 1]
    row = jnp.where(first, 0, part)

    def mine(x, start):
        return lax.dynamic_slice_in_dim(x, start + row, part, 0)

    early_push = jnp.where(first, mine(summed, 0), mine(other, 0))
    late_push = jnp.where(first, mine(other, 0), mine(summed, 0))
    early_pull = jnp.where(first, mine(summed, states), mine(other, states))
    late_pull = jnp.where(first, mine(other, states), mine(summed, states))
    push = late_push + late_decay * early_push
    pull = early_pull + early_decay * late_pull
    decay = jnp.broadcast_to(early_decay * late_decay, (8, summed.shape[1]))
    got = []
    for m in range(1, devices // 2):
        sent = jnp.concatenate([jnp.where(place < (place ^ m), push, pull), decay], axis=0)
        got.append(lax.ppermute(sent, axes, [(d, d ^ (2 * m)) for d in range(devices)]))
    got, made = second_window(got, made)
    own = combine(place, got)
    others = lax.ppermute(own, axes, [(d, d ^ 1) for d in range(devices)])
    return (own, others, other), made


def on_device(inputs, log_decay, write_keys, read_keys, skip_gain, grad_out):
    states = write_keys.shape[1]
    line = lax.axis_size("mp") == 4
    assert inputs.shape[0] == 4 * STEP

    at = lax.axis_index("mp")
    ends = (at == 0) | (at == 3)

    def of(*values):
        if not line:
            return jnp.int32(values[0])
        return sum(jnp.where(at == k, v, 0) for k, v in enumerate(values)).astype(jnp.int32)

    even = (lax.rem(lax.axis_index(("outer", "inner")), 2) == 0).astype(jnp.int32)
    plan = jnp.stack(
        [
            of(2, 0, 1, 0),
            of(3, 2, 3, 1),
            of(1, 3, 0, 2),
            of(0, 1, 2, 3),
            even,
            of(1, 0, 1, 0),
        ]
    )
    summed = totals(inputs, grad_out, log_decay, write_keys, read_keys)

    def first_window(other):
        ordered, _ = lax.optimization_barrier((log_decay, summed))
        return lax.optimization_barrier((other, factors(ordered)))

    def second_window(got, made):
        parts, rows, decays, ranges = made
        found = local(plan, inputs, grad_out, write_keys, read_keys, parts, rows, decays, ranges)
        return lax.optimization_barrier((got, (found, made)))

    given, made = carried_states(summed, states, first_window, second_window)
    (entries, afters, read_terms, write_terms, lead, tail), made = made
    entry, after, far, crossed = early_grads(plan, lead, tail, read_terms, write_terms, *given)

    def part(offset, steps, with_terms, earlier):
        return outputs(
            plan, offset, steps, with_terms, earlier, inputs, grad_out, write_keys, read_keys,
            (entries, afters, *made), entry, after, skip_gain[None],
        )

    if not line:
        *results, third = part(2, 1, True, ())
        *results, own = part(3, 1, True, results)
        results = part(0, 2, False, results)
        terms = jnp.concatenate([own, third, crossed, far], axis=0)
        own = lax.psum_scatter(terms, "mp", scatter_dimension=0, tiled=True)
        return *results, own[:, states:], own[:, :states]

    far_sum = lax.ppermute(far, "mp", [(0, 1), (1, 0), (2, 3), (3, 2)])
    middle = lax.ppermute(crossed, "mp", [(1, 2), (2, 1)])
    (*results, third), crossed = lax.optimization_barrier((part(2, 1, True, ()), crossed))
    two_away = lax.ppermute(crossed, "mp", [(0, 2), (3, 1)])
    (*results, own), far_sum, third = lax.optimization_barrier(
        (part(3, 1, True, results), far_sum, third)
    )
    last = lax.ppermute(third + far_sum, "mp", [(1, 3), (2, 0)])
    near_terms = lax.ppermute(third, "mp", [(0, 1), (3, 2)])
    results, middle, last, two_away, near_terms = lax.optimization_barrier(
        (part(0, 2, False, results), middle, last, two_away, near_terms)
    )

    def summed_up(lanes):
        came = jnp.where(ends, far_sum[:, lanes], near_terms[:, lanes])
        return own[:, lanes] + came + (middle[:, lanes] + two_away[:, lanes] + last[:, lanes])

    return *results, summed_up(slice(states, None)), summed_up(slice(0, states))


def solution(mesh):
    tokens = ("outer", "inner")
    return jax.shard_map(
        on_device,
        mesh=mesh,
        in_specs=(
            P(tokens, "mp"),
            P("mp", tokens),
            P(tokens, None),
            P(tokens, None),
            P("mp"),
            P(tokens, "mp"),
        ),
        out_specs=(
            P(tokens, "mp"),
            P(tokens, "mp"),
            P(("outer", "inner", "mp"), None),
            P(("outer", "inner", "mp"), None),
        ),
        check_vma=False,
    )
```

time: 109 us -> 104 us (0.954)
  waiting for transfers between devices: 11.9 us -> 2.14 us
  Pallas kernels: 62.8 us -> 72.2 us
  other arithmetic: 8.59 us -> 4.1 us
  local copies, waits for them, and re-layouts: 3.95 us -> 2.34 us
  starting transfers between devices: 20.4 us -> 21.7 us
    pallas_call x5 -> x8, Pallas kernels: 62.8 us -> 72.2 us  [the longest x3 34.5 us: outputs(): pl.pallas_call(functools.partial(outputs_kernel, offset, with_terms, len(...]
    ppermute x8, waiting for transfers between devices: 7.22 us -> 0.02 us  [the longest x3 0.01 us: carried_states(): lax.ppermute(sent, axes, [(d, d ^ 2 * m) for d in range(devices)])]
    ppermute x1, waiting for transfers between devices: 2.54 us -> 0.01 us  [carried_states(): other = lax.ppermute(summed, axes, [(d, d ^ 1) for d in range(devices)])]
    dynamic_slice x1 -> x0, local copies, waits for them, and re-layouts: 2.28 us -> none  [quarter(): return lax.dynamic_slice_in_dim(terms, k * rows, rows, 0)]
    add x4 -> x2, other arithmetic: 4.05 us -> 2.03 us  [the longest x1 1.96 us: summed_up(): own[:, lanes] + came]
    unnamed x4 -> x14, local copies, waits for them, and re-layouts: 0.01 us -> 1.73 us
    select_n x4 -> x2, other arithmetic: 2.83 us -> 1.2 us  [carried_states(): jnp.where(place < place ^ m, push, pull)]
    ppermute x8, starting transfers between devices: 19.9 us -> 21.3 us  [the longest x1 6.85 us: on_device(): near_terms = lax.ppermute(third, 'mp', [(0, 1), (3, 2)])]
  transfers between devices with their start and end apart: 10 -> 10, of which waited for: 3 -> 1; matrix products, arithmetic and copies ran while one was open for 1% -> 1% of each run, Pallas kernels for 42% -> 53%
where the time goes in v3:
time: 104 us; the launch traced here: 103 us
  Pallas kernels  72.2 us (69%)
  starting transfers between devices  21.7 us (21%)
  other arithmetic  4.1 us (4%)
  local copies, waits for them, and re-layouts  2.34 us (2%)
  waiting for transfers between devices  2.14 us (2%)
    pallas_call x3, Pallas kernels, outputs(): pl.pallas_call(functools.partial(outputs_kernel, offset, with_terms, len(...  34.5 us
    pallas_call x1, Pallas kernels, local(): pl.pallas_call(local_kernel, out_shape=(jax.ShapeDtypeStruct((steps * sta...  17.9 us
    pallas_call x1, Pallas kernels, totals(): pl.pallas_call(totals_kernel, out_shape=jax.ShapeDtypeStruct((2 * states...  8.78 us
    ppermute x1, starting transfers between devices, on_device(): near_terms = lax.ppermute(third, 'mp', [(0, 1), (3, 2)])  6.85 us
    pallas_call x1, Pallas kernels, early_grads(): pl.pallas_call(early_grads_kernel, out_shape=shapes, grid_spec=pltpu.Pref...  6.44 us
    ppermute x1, starting transfers between devices, on_device(): two_away = lax.ppermute(crossed, 'mp', [(0, 2), (3, 1)])  5.17 us
    ppermute x3, starting transfers between devices, carried_states(): lax.ppermute(sent, axes, [(d, d ^ 2 * m) for d in range(devices)])  4.09 us
    ppermute x1, starting transfers between devices, on_device(): far_sum = lax.ppermute(far, 'mp', [(0, 1), (1, 0), (2, 3), (3, 2)])  3 us
  transfers between devices with their start and end apart: 10, of which 1 were waited for; matrix products, arithmetic and copies ran while one was open for 1% of the time, Pallas kernels for 53%

profile of v3, /device:TPU:0, one launch (start us, length us, event | category | flops | bytes accessed | tf_op | source)
XLA Modules:
  0.0 103.4 jit_solution(13828323216009222513)
XLA Ops:
  0.6 8.8 %totals.1 = f32[264,1024]{1,0:T(8,128)} custom-call(bf16[2048,1024]{1,0:T(8,128)(2,1)} %inputs_ref.9, bf16[2048,1024]{1,0:T(8,128)(2,1)} %grad_ref.9, f32[16,2048]{1,0:T(8,128)} %ld_ref.2, bf16[2048,128]{1,0:T(8,128)(2,1)} %write_ref.9, bf16[2048,128]{1,0:T(8,128)(2,1)} %read_ref.9), custom_call_target="tpu_custom_call" | custom-call | flops 1610612736 | bytes 8388608 | tf_op jit(solution)/shard_map/totals/pallas_call | solution.py:143
  9.4 0.5 collective-permute-start
  9.9 0.6 stack.31.plan_ref
  10.5 2.5 %factors.1 = (bf16[2048,128]{1,0:T(8,128)(2,1)}, f32[256,128]{1,0:T(8,128)}, f32[16,1024]{1,0:T(8,128)}, f32[32,1024]{1,0:T(8,128)}) custom-call(f32[16,2048]{1,0:T(8,128)} %ld_ref.2), custom_call_target="tpu_custom_call" | custom-call | flops 196608000 | bytes 2048000 | tf_op jit(solution)/shard_map/factors/pallas_call | solution.py:189
  13.0 0.8 fusion
  13.7 1.2 %broadcast_select_fusion = (f32[64,1024]{1,0:T(8,128)S(1)}, f32[64,1024]{1,0:T(8,128)S(1)}, f32[64,1024]{1,0:T(8,128)S(1)}) fusion(pred[]{:T(512)S(6)} %lt.22, f32[1024]{0:T(1024)S(1)} %bitcast.12, f32[264,1024]{1,0:T(8,128)S(1)} %collective-permute-done.other_ref, s32[]{:T(128)S(6)} %select_n.145, f32[264,1024]{1,0:T(8,128)} %totals.1, pred[]{:T(512)S(6)} %eq.14, ...), kind=kLoop, calls=%fused_computation.7 | loop fusion | flops 589824 | bytes 1843210 | tf_op jit(solution)/shard_map/jit(_where)/select_n | solution.py:702
  15.1 2.6 %collective-permute-start.1 = (f32[72,1024]{1,0:T(8,128)S(1)}, f32[72,1024]{1,0:T(8,128)S(1)}, u32[]{:S(2)}, u32[]{:S(2)}) collective-permute-start(f32[72,1024]{1,0:T(8,128)S(1)} %get-tuple-element.128), channel_id=1, source_target_pairs={{0,8},{4,12},{8,0},{12,4},{16,24},{20,28},{24,16},{28,20},{1,9},{5... | collective-permute-start | bytes 884744 | tf_op jit(solution)/shard_map/ppermute | solution.py:703
  17.6 1.5 %collective-permute-start.2 = (f32[72,1024]{1,0:T(8,128)S(1)}, f32[72,1024]{1,0:T(8,128)S(1)}, u32[]{:S(2)}, u32[]{:S(2)}) collective-permute-start(f32[72,1024]{1,0:T(8,128)S(1)} %get-tuple-element.127), channel_id=1, source_target_pairs={{0,16},{4,20},{8,24},{12,28},{16,0},{20,4},{24,8},{28,12},{1,17},{... | collective-permute-start | bytes 884744 | tf_op jit(solution)/shard_map/ppermute | solution.py:703
  19.2 17.9 %local.1 = (bf16[512,1024]{1,0:T(8,128)(2,1)}, bf16[512,1024]{1,0:T(8,128)(2,1)}, f32[1024,128]{1,0:T(8,128)}, f32[1024,128]{1,0:T(8,128)}, bf16[1024,1024]{1,0:T(8,128)(2,1)}, /*index=5*/bf16[1024,1024]{1,0:T(8,128)(2,1)}) custom-call(s32[6]{0:T(128)} %stack.31.plan_ref, bf16[2048,1024]{1,0:T(8,128)(2,1)} %inputs_ref.9, bf16[2048,1024]{1,0:T(8,128)(2,1)} %grad_ref.9, ...), custom_call_target="tpu_custom_call" | custom-call | flops 6442450944 | bytes 16777216 | tf_op jit(solution)/shard_map/local/pallas_call | solution.py:351
  37.2 0.7 copy-done.4
  38.0 0.1 copy-done.6
  38.1 2.1 %combine.1.own_ref = f32[128,1024]{1,0:T(8,128)} custom-call(s32[1]{0:T(128)} %bitcast.9.place_ref, f32[72,1024]{1,0:T(8,128)} %copy-done.4, f32[72,1024]{1,0:T(8,128)} %copy-done.5, f32[72,1024]{1,0:T(8,128)} %copy-done.6), custom_call_target="tpu_custom_call" | custom-call | flops 884736 | bytes 1474560 | tf_op jit(solution)/shard_map/combine/pallas_call | solution.py:505
  40.2 2.1 %collective-permute-done.4.others_ref = f32[128,1024]{1,0:T(8,128)S(1)} collective-permute-done((f32[128,1024]{1,0:T(8,128)}, f32[128,1024]{1,0:T(8,128)S(1)}, u32[]{:S(2)}, u32[]{:S(2)}) %collective-permute-start.4) | collective-permute-done | bytes 524320 | tf_op jit(solution)/shard_map/ppermute | solution.py:706
  42.3 0.8 copy-done.3
  43.1 6.4 %early_grads.1 = (f32[128,1024]{1,0:T(8,128)}, f32[128,1024]{1,0:T(8,128)}, f32[512,256]{1,0:T(8,128)}, f32[512,256]{1,0:T(8,128)}) custom-call(s32[6]{0:T(128)} %stack.31.plan_ref, bf16[1024,1024]{1,0:T(8,128)(2,1)} %get-tuple-element.82.lead_ref, bf16[1024,1024]{1,0:T(8,128)(2,1)} %get-tuple-element.83.tail_ref, ...), custom_call_target="tpu_custom_call" | custom-call | flops 536870912 | bytes 4194304 | tf_op jit(solution)/shard_map/early_grads/pallas_call | solution.py:457
  49.6 3.0 %collective-permute-start.5 = (f32[512,256]{1,0:T(8,128)}, f32[512,256]{1,0:T(8,128)S(1)}, u32[]{:S(2)}, u32[]{:S(2)}) collective-permute-start(f32[512,256]{1,0:T(8,128)} %get-tuple-element.100), channel_id=1, source_target_pairs={{0,1},{1,0},{2,3},{3,2},{4,5},{5,4},{6,7},{7,6},{8,9},{9,8},{10,11... | collective-permute-start | bytes 1572872 | tf_op jit(solution)/shard_map/ppermute | solution.py:763
  52.6 0.9 collective-permute-start.6
  53.4 10.4 %outputs_and_terms.2 = (bf16[2048,1024]{1,0:T(8,128)(2,1)}, bf16[2048,1024]{1,0:T(8,128)(2,1)}, f32[512,256]{1,0:T(8,128)}) custom-call(s32[6]{0:T(128)} %stack.31.plan_ref, bf16[2048,1024]{1,0:T(8,128)(2,1)} %inputs_ref.9, bf16[2048,1024]{1,0:T(8,128)(2,1)} %grad_ref.9, bf16[2048,128]{1,0:T(8,128)(2,1)} %write_ref.9, bf16[2048,128]{1,0:T(8,128)(2,1)} %read_ref.9, ...), custom_call_target="tpu_custom_call" | custom-call | flops 1073741824 | bytes 6291456 | tf_op jit(solution)/shard_map/outputs_and_terms/pallas_call | solution.py:635
  63.8 5.2 %collective-permute-start.8 = (f32[512,256]{1,0:T(8,128)}, f32[512,256]{1,0:T(8,128)S(1)}, u32[]{:S(2)}, u32[]{:S(2)}) collective-permute-start(f32[512,256]{1,0:T(8,128)} %get-tuple-element.108), channel_id=1, source_target_pairs={{0,2},{3,1},{4,6},{7,5},{8,10},{11,9},{12,14},{15,13},{16,18},{19,... | collective-permute-start | bytes 1572872 | tf_op jit(solution)/shard_map/ppermute | solution.py:766
  69.0 10.4 %outputs_and_terms.3 = (bf16[2048,1024]{1,0:T(8,128)(2,1)}, bf16[2048,1024]{1,0:T(8,128)(2,1)}, f32[512,256]{1,0:T(8,128)}) custom-call(s32[6]{0:T(128)} %stack.31.plan_ref, bf16[2048,1024]{1,0:T(8,128)(2,1)} %inputs_ref.9, bf16[2048,1024]{1,0:T(8,128)(2,1)} %grad_ref.9, ...), custom_call_target="tpu_custom_call", output_to_operand_aliasing={{0}: (14, {}), {1}: (15, {})} | custom-call | flops 1073741824 | bytes 6291456 | tf_op jit(solution)/shard_map/outputs_and_terms/pallas_call | solution.py:635
  79.5 1.3 %collective-permute-start.7 = (f32[512,256]{1,0:T(8,128)S(1)}, f32[512,256]{1,0:T(8,128)S(1)}, u32[]{:S(2)}, u32[]{:S(2)}) collective-permute-start(f32[512,256]{1,0:T(8,128)S(1)} %add.103), channel_id=1, source_target_pairs={{1,3},{2,0},{5,7},{6,4},{9,11},{10,8},{13,15},{14,12},{17,19},{18,... | collective-permute-start | bytes 1572872 | tf_op jit(solution)/shard_map/ppermute | solution.py:770
  80.8 6.8 %collective-permute-start.9 = (f32[512,256]{1,0:T(8,128)S(1)}, f32[512,256]{1,0:T(8,128)}, u32[]{:S(2)}, u32[]{:S(2)}) collective-permute-start(f32[512,256]{1,0:T(8,128)S(1)} %copy-done.1), channel_id=1, source_target_pairs={{0,1},{3,2},{4,5},{7,6},{8,9},{11,10},{12,13},{15,14},{16,17},{19,... | collective-permute-start | bytes 1572872 | tf_op jit(solution)/shard_map/ppermute | solution.py:771
  87.6 13.7 %outputs.1 = (bf16[2048,1024]{1,0:T(8,128)(2,1)}, bf16[2048,1024]{1,0:T(8,128)(2,1)}) custom-call(s32[6]{0:T(128)} %stack.31.plan_ref, bf16[2048,1024]{1,0:T(8,128)(2,1)} %inputs_ref.9, bf16[2048,1024]{1,0:T(8,128)(2,1)} %grad_ref.9, bf16[2048,128]{1,0:T(8,128)(2,1)} %write_ref.9, ...), custom_call_target="tpu_custom_call", output_to_operand_aliasing={{0}: (14, {}), {1}: (15, {})} | custom-call | flops 2147483648 | bytes 12582912 | tf_op jit(solution)/shard_map/outputs/pallas_call | solution.py:635
  101.4 2.0 %add_add_fusion = (f32[512,128]{1,0:T(8,128)}, f32[512,128]{1,0:T(8,128)}) fusion(f32[512,256]{1,0:T(8,128)S(1)} %collective-permute-done.7, f32[512,256]{1,0:T(8,128)S(1)} %collective-permute-done.8, f32[512,256]{1,0:T(8,128)S(1)} %collective-permute-done.6, f32[512,256]{1,0:T(8,128)} %collective-permute-done.9, f32[512,256]{1,0:T(8,128)S(1)} %collective-permute-done.5, ...), kind=kLoop, calls=%fused_computation.3 | loop fusion | flops 655360 | bytes 3670017 | tf_op jit(solution)/shard_map/add | solution.py:778
  (26 shorter events, 0.4 us)
Async XLA Ops:
  9.4 3.6 %collective-permute-start = (f32[264,1024]{1,0:T(8,128)}, f32[264,1024]{1,0:T(8,128)S(1)}, u32[]{:S(2)}, u32[]{:S(2)}) collective-permute-start(f32[264,1024]{1,0:T(8,128)} %totals.1), channel_id=1, source_target_pairs={{0,4},{4,0},{8,12},{12,8},{16,20},{20,16},{24,28},{28,24},{1,5},{5... | collective-permute-start | bytes 3244040 | tf_op jit(solution)/shard_map/ppermute | solution.py:684
  13.0 24.2 %copy-start = (f32[264,1024]{1,0:T(8,128)}, f32[264,1024]{1,0:T(8,128)S(1)}, u32[]{:S(2)}) copy-start(f32[264,1024]{1,0:T(8,128)S(1)} %collective-permute-done.other_ref) | copy-start | bytes 3244036
  15.1 22.1 %collective-permute-start.1 = (f32[72,1024]{1,0:T(8,128)S(1)}, f32[72,1024]{1,0:T(8,128)S(1)}, u32[]{:S(2)}, u32[]{:S(2)}) collective-permute-start(f32[72,1024]{1,0:T(8,128)S(1)} %get-tuple-element.128), channel_id=1, source_target_pairs={{0,8},{4,12},{8,0},{12,4},{16,24},{20,28},{24,16},{28,20},{1,9},{5... | collective-permute-start | bytes 884744 | tf_op jit(solution)/shard_map/ppermute | solution.py:703
  17.6 19.5 %collective-permute-start.2 = (f32[72,1024]{1,0:T(8,128)S(1)}, f32[72,1024]{1,0:T(8,128)S(1)}, u32[]{:S(2)}, u32[]{:S(2)}) collective-permute-start(f32[72,1024]{1,0:T(8,128)S(1)} %get-tuple-element.127), channel_id=1, source_target_pairs={{0,16},{4,20},{8,24},{12,28},{16,0},{20,4},{24,8},{28,12},{1,17},{... | collective-permute-start | bytes 884744 | tf_op jit(solution)/shard_map/ppermute | solution.py:703
  19.1 18.0 %collective-permute-start.3 = (f32[72,1024]{1,0:T(8,128)S(1)}, f32[72,1024]{1,0:T(8,128)S(1)}, u32[]{:S(2)}, u32[]{:S(2)}) collective-permute-start(f32[72,1024]{1,0:T(8,128)S(1)} %get-tuple-element.126), channel_id=1, source_target_pairs={{0,24},{4,28},{8,16},{12,20},{16,8},{20,12},{24,0},{28,4},{1,25},{... | collective-permute-start | bytes 884744 | tf_op jit(solution)/shard_map/ppermute | solution.py:703
  37.1 0.7 copy-start.4
  37.2 0.8 copy-start.5
  37.2 0.9 copy-start.6
  40.2 2.1 %collective-permute-start.4 = (f32[128,1024]{1,0:T(8,128)}, f32[128,1024]{1,0:T(8,128)S(1)}, u32[]{:S(2)}, u32[]{:S(2)}) collective-permute-start(f32[128,1024]{1,0:T(8,128)} %combine.1.own_ref), channel_id=1, source_target_pairs={{0,4},{4,0},{8,12},{12,8},{16,20},{20,16},{24,28},{28,24},{1,5},{5... | collective-permute-start | bytes 1572872 | tf_op jit(solution)/shard_map/ppermute | solution.py:706
  42.3 0.8 copy-start.3
  49.6 29.8 %collective-permute-start.5 = (f32[512,256]{1,0:T(8,128)}, f32[512,256]{1,0:T(8,128)S(1)}, u32[]{:S(2)}, u32[]{:S(2)}) collective-permute-start(f32[512,256]{1,0:T(8,128)} %get-tuple-element.100), channel_id=1, source_target_pairs={{0,1},{1,0},{2,3},{3,2},{4,5},{5,4},{6,7},{7,6},{8,9},{9,8},{10,11... | collective-permute-start | bytes 1572872 | tf_op jit(solution)/shard_map/ppermute | solution.py:763
  52.6 48.8 %collective-permute-start.6 = (f32[512,256]{1,0:T(8,128)}, f32[512,256]{1,0:T(8,128)S(1)}, u32[]{:S(2)}, u32[]{:S(2)}) collective-permute-start(f32[512,256]{1,0:T(8,128)} %get-tuple-element.108), channel_id=1, source_target_pairs={{1,2},{2,1},{5,6},{6,5},{9,10},{10,9},{13,14},{14,13},{17,18},{18,... | collective-permute-start | bytes 1572872 | tf_op jit(solution)/shard_map/ppermute | solution.py:764
  63.8 15.6 %copy-start.1 = (f32[512,256]{1,0:T(8,128)S(1)}, f32[512,256]{1,0:T(8,128)}, u32[]{:S(2)}) copy-start(f32[512,256]{1,0:T(8,128)} %get-tuple-element.106) | copy-start | bytes 1572868
  63.8 37.6 %collective-permute-start.8 = (f32[512,256]{1,0:T(8,128)}, f32[512,256]{1,0:T(8,128)S(1)}, u32[]{:S(2)}, u32[]{:S(2)}) collective-permute-start(f32[512,256]{1,0:T(8,128)} %get-tuple-element.108), channel_id=1, source_target_pairs={{0,2},{3,1},{4,6},{7,5},{8,10},{11,9},{12,14},{15,13},{16,18},{19,... | collective-permute-start | bytes 1572872 | tf_op jit(solution)/shard_map/ppermute | solution.py:766
  79.5 21.9 %collective-permute-start.7 = (f32[512,256]{1,0:T(8,128)S(1)}, f32[512,256]{1,0:T(8,128)S(1)}, u32[]{:S(2)}, u32[]{:S(2)}) collective-permute-start(f32[512,256]{1,0:T(8,128)S(1)} %add.103), channel_id=1, source_target_pairs={{1,3},{2,0},{5,7},{6,4},{9,11},{10,8},{13,15},{14,12},{17,19},{18,... | collective-permute-start | bytes 1572872 | tf_op jit(solution)/shard_map/ppermute | solution.py:770
  80.8 20.6 %collective-permute-start.9 = (f32[512,256]{1,0:T(8,128)S(1)}, f32[512,256]{1,0:T(8,128)}, u32[]{:S(2)}, u32[]{:S(2)}) collective-permute-start(f32[512,256]{1,0:T(8,128)S(1)} %copy-done.1), channel_id=1, source_target_pairs={{0,1},{3,2},{4,5},{7,6},{8,9},{11,10},{12,13},{15,14},{16,17},{19,... | collective-permute-start | bytes 1572872 | tf_op jit(solution)/shard_map/ppermute | solution.py:771
  87.6 13.8 %copy-start.2 = (f32[512,256]{1,0:T(8,128)S(1)}, f32[512,256]{1,0:T(8,128)}, u32[]{:S(2)}) copy-start(f32[512,256]{1,0:T(8,128)} %get-tuple-element.111) | copy-start | bytes 1572868

commit v4 on v3

--- a/solution.py
+++ b/solution.py
@@ -609,15 +609,18 @@
                     dot(tail[at], after, 1, 1) + dot(high, read, 0, 0) + dot(low, read, 0, 0),
                 )
             )
-    for k, (for_read, for_write) in enumerate(found):
-        terms[0][k * BLOCK : k * BLOCK + BLOCK, :states] = for_read
-        terms[0][k * BLOCK : k * BLOCK + BLOCK, states:] = for_write
+    for n, out in enumerate(terms):
+
+        @pl.when(step == n)
+        def _():
+            for k, (for_read, for_write) in enumerate(found):
+                out[k * BLOCK : k * BLOCK + BLOCK, :states] = for_read
+                out[k * BLOCK : k * BLOCK + BLOCK, states:] = for_write
 
 
 def outputs(
     plan, offset, steps, with_terms, earlier, inputs, grad_out, write_keys, read_keys, made, entry, after, skip
 ):
-    assert steps == 1 or not with_terms
     length, lanes = inputs.shape
     states = write_keys.shape[1]
     entries, afters, parts, rows, decays, ranges = made
@@ -631,7 +634,7 @@
 
     wide = tokens(STEP, lanes)
     shape = jax.ShapeDtypeStruct((length, lanes), BF16)
-    terms = (jax.ShapeDtypeStruct((STEP, 2 * states), F32),) * with_terms
+    terms = (jax.ShapeDtypeStruct((STEP, 2 * states), F32),) * (steps * with_terms)
     return pl.pallas_call(
         functools.partial(outputs_kernel, offset, with_terms, len(earlier)),
         out_shape=(shape, shape, *terms),
@@ -753,31 +756,24 @@
         )
 
     if not line:
-        *results, third = part(2, 1, True, ())
-        *results, own = part(3, 1, True, results)
+        *results, third, own = part(2, 2, True, ())
         results = part(0, 2, False, results)
         terms = jnp.concatenate([own, third, crossed, far], axis=0)
         own = lax.psum_scatter(terms, "mp", scatter_dimension=0, tiled=True)
         return *results, own[:, states:], own[:, :states]
 
+    two_away = lax.ppermute(crossed, "mp", [(0, 2), (3, 1)])
     far_sum = lax.ppermute(far, "mp", [(0, 1), (1, 0), (2, 3), (3, 2)])
     middle = lax.ppermute(crossed, "mp", [(1, 2), (2, 1)])
-    (*results, third), crossed = lax.optimization_barrier((part(2, 1, True, ()), crossed))
-    two_away = lax.ppermute(crossed, "mp", [(0, 2), (3, 1)])
-    (*results, own), far_sum, third = lax.optimization_barrier(
-        (part(3, 1, True, results), far_sum, third)
+    (*results, third, own), far_sum, two_away, middle = lax.optimization_barrier(
+        (part(2, 2, True, ()), far_sum, two_away, middle)
     )
-    last = lax.ppermute(third + far_sum, "mp", [(1, 3), (2, 0)])
-    near_terms = lax.ppermute(third, "mp", [(0, 1), (3, 2)])
-    results, middle, last, two_away, near_terms = lax.optimization_barrier(
-        (part(0, 2, False, results), middle, last, two_away, near_terms)
-    )
-
-    def summed_up(lanes):
-        came = jnp.where(ends, far_sum[:, lanes], near_terms[:, lanes])
-        return own[:, lanes] + came + (middle[:, lanes] + two_away[:, lanes] + last[:, lanes])
-
-    return *results, summed_up(slice(states, None)), summed_up(slice(0, states))
+    came = jnp.where(ends, 0.0, far_sum)
+    last = lax.ppermute(third + came, "mp", [(0, 1), (1, 3), (3, 2), (2, 0)])
+    own = own + (far_sum - came) + middle + two_away
+    results, own, last = lax.optimization_barrier((part(0, 2, False, results), own, last))
+    total = own + last
+    return *results, total[:, states:], total[:, :states]
 
 
 def solution(mesh):

time: 104 us -> 97.7 us (0.939)
  starting transfers between devices: 21.7 us -> 17.7 us
  Pallas kernels: 72.2 us -> 69.1 us
    pallas_call x3 -> x2, Pallas kernels: 34.5 us -> 31.3 us  [outputs(): pl.pallas_call(functools.partial(outputs_kernel, offset, with_terms, len(...]
    ppermute x2 -> x1, starting transfers between devices: 8.14 us -> 5.76 us  [on_device(): last = lax.ppermute(third + came, 'mp', [(0, 1), (1, 3), (3, 2), (2, 0)])]
    ppermute x1, starting transfers between devices: 5.17 us -> 3.57 us  [on_device(): two_away = lax.ppermute(crossed, 'mp', [(0, 2), (3, 1)])]
  transfers between devices with their start and end apart: 10 -> 9, of which waited for: 1 -> 2; matrix products, arithmetic and copies ran while one was open for 1% -> 1% of each run, Pallas kernels for 53% -> 53%
where the time goes in v4:
time: 97.7 us; the launch traced here: 97.2 us
  Pallas kernels  69.1 us (71%)
  starting transfers between devices  17.7 us (18%)
  other arithmetic  3.5 us (4%)
  local copies, waits for them, and re-layouts  3.17 us (3%)
  waiting for transfers between devices  3 us (3%)
    pallas_call x2, Pallas kernels, outputs(): pl.pallas_call(functools.partial(outputs_kernel, offset, with_terms, len(...  31.3 us
    pallas_call x1, Pallas kernels, local(): pl.pallas_call(local_kernel, out_shape=(jax.ShapeDtypeStruct((steps * sta...  18 us
    pallas_call x1, Pallas kernels, totals(): pl.pallas_call(totals_kernel, out_shape=jax.ShapeDtypeStruct((2 * states...  8.78 us
    pallas_call x1, Pallas kernels, early_grads(): pl.pallas_call(early_grads_kernel, out_shape=shapes, grid_spec=pltpu.Pref...  6.4 us
    ppermute x1, starting transfers between devices, on_device(): last = lax.ppermute(third + came, 'mp', [(0, 1), (1, 3), (3, 2), (2, 0)])  5.76 us
    ppermute x3, starting transfers between devices, carried_states(): lax.ppermute(sent, axes, [(d, d ^ 2 * m) for d in range(devices)])  4.1 us
    ppermute x1, starting transfers between devices, on_device(): two_away = lax.ppermute(crossed, 'mp', [(0, 2), (3, 1)])  3.57 us
    ppermute x1, starting transfers between devices, on_device(): far_sum = lax.ppermute(far, 'mp', [(0, 1), (1, 0), (2, 3), (3, 2)])  2.97 us
  transfers between devices with their start and end apart: 9, of which 2 were waited for; matrix products, arithmetic and copies ran while one was open for 1% of the time, Pallas kernels for 53%

profile of v4, /device:TPU:0, one launch (start us, length us, event | category | flops | bytes accessed | tf_op | source)
XLA Modules:
  0.0 97.2 jit_solution(364784984429082122)
XLA Ops:
  0.6 8.8 %totals.1 = f32[264,1024]{1,0:T(8,128)} custom-call(bf16[2048,1024]{1,0:T(8,128)(2,1)} %inputs_ref.7, bf16[2048,1024]{1,0:T(8,128)(2,1)} %grad_ref.7, f32[16,2048]{1,0:T(8,128)} %ld_ref.2, bf16[2048,128]{1,0:T(8,128)(2,1)} %write_ref.7, bf16[2048,128]{1,0:T(8,128)(2,1)} %read_ref.7), custom_call_target="tpu_custom_call" | custom-call | flops 1610612736 | bytes 8388608 | tf_op jit(solution)/shard_map/totals/pallas_call | solution.py:143
  9.4 0.5 collective-permute-start
  9.9 0.7 stack.31.plan_ref
  10.5 2.5 %factors.1 = (bf16[2048,128]{1,0:T(8,128)(2,1)}, f32[256,128]{1,0:T(8,128)}, f32[16,1024]{1,0:T(8,128)}, f32[32,1024]{1,0:T(8,128)}) custom-call(f32[16,2048]{1,0:T(8,128)} %ld_ref.2), custom_call_target="tpu_custom_call" | custom-call | flops 196608000 | bytes 2048000 | tf_op jit(solution)/shard_map/factors/pallas_call | solution.py:189
  13.0 0.8 fusion.3
  13.8 1.2 %broadcast_select_fusion = (f32[64,1024]{1,0:T(8,128)S(1)}, f32[64,1024]{1,0:T(8,128)S(1)}, f32[64,1024]{1,0:T(8,128)S(1)}) fusion(pred[]{:T(512)S(6)} %lt.22, f32[1024]{0:T(1024)S(1)} %bitcast.12, f32[264,1024]{1,0:T(8,128)S(1)} %collective-permute-done.other_ref, s32[]{:T(128)S(6)} %select_n.141, f32[264,1024]{1,0:T(8,128)} %totals.1, pred[]{:T(512)S(6)} %eq.14, ...), kind=kLoop, calls=%fused_computation.10 | loop fusion | flops 589824 | bytes 1843210 | tf_op jit(solution)/shard_map/jit(_where)/select_n | solution.py:705
  15.1 2.6 %collective-permute-start.1 = (f32[72,1024]{1,0:T(8,128)S(1)}, f32[72,1024]{1,0:T(8,128)S(1)}, u32[]{:S(2)}, u32[]{:S(2)}) collective-permute-start(f32[72,1024]{1,0:T(8,128)S(1)} %get-tuple-element.118), channel_id=1, source_target_pairs={{0,8},{4,12},{8,0},{12,4},{16,24},{20,28},{24,16},{28,20},{1,9},{5... | collective-permute-start | bytes 884744 | tf_op jit(solution)/shard_map/ppermute | solution.py:706
  17.7 1.5 %collective-permute-start.2 = (f32[72,1024]{1,0:T(8,128)S(1)}, f32[72,1024]{1,0:T(8,128)S(1)}, u32[]{:S(2)}, u32[]{:S(2)}) collective-permute-start(f32[72,1024]{1,0:T(8,128)S(1)} %get-tuple-element.117), channel_id=1, source_target_pairs={{0,16},{4,20},{8,24},{12,28},{16,0},{20,4},{24,8},{28,12},{1,17},{... | collective-permute-start | bytes 884744 | tf_op jit(solution)/shard_map/ppermute | solution.py:706
  19.2 18.0 %local.1 = (bf16[512,1024]{1,0:T(8,128)(2,1)}, bf16[512,1024]{1,0:T(8,128)(2,1)}, f32[1024,128]{1,0:T(8,128)}, f32[1024,128]{1,0:T(8,128)}, bf16[1024,1024]{1,0:T(8,128)(2,1)}, /*index=5*/bf16[1024,1024]{1,0:T(8,128)(2,1)}) custom-call(s32[6]{0:T(128)} %stack.31.plan_ref, bf16[2048,1024]{1,0:T(8,128)(2,1)} %inputs_ref.7, bf16[2048,1024]{1,0:T(8,128)(2,1)} %grad_ref.7, ...), custom_call_target="tpu_custom_call" | custom-call | flops 6442450944 | bytes 16777216 | tf_op jit(solution)/shard_map/local/pallas_call | solution.py:351
  37.3 0.7 copy-done.2
  37.9 0.1 copy-done.3
  38.1 2.1 %combine.1.own_ref = f32[128,1024]{1,0:T(8,128)} custom-call(s32[1]{0:T(128)} %bitcast.9.place_ref, f32[72,1024]{1,0:T(8,128)} %copy-done.2, f32[72,1024]{1,0:T(8,128)} %copy-done.3, f32[72,1024]{1,0:T(8,128)} %copy-done.4), custom_call_target="tpu_custom_call" | custom-call | flops 884736 | bytes 1474560 | tf_op jit(solution)/shard_map/combine/pallas_call | solution.py:505
  40.2 2.1 %collective-permute-done.4.others_ref = f32[128,1024]{1,0:T(8,128)S(1)} collective-permute-done((f32[128,1024]{1,0:T(8,128)}, f32[128,1024]{1,0:T(8,128)S(1)}, u32[]{:S(2)}, u32[]{:S(2)}) %collective-permute-start.4) | collective-permute-done | bytes 524320 | tf_op jit(solution)/shard_map/ppermute | solution.py:709
  42.3 0.8 copy-done.1
  43.1 6.4 %early_grads.1 = (f32[128,1024]{1,0:T(8,128)}, f32[128,1024]{1,0:T(8,128)}, f32[512,256]{1,0:T(8,128)}, f32[512,256]{1,0:T(8,128)}) custom-call(s32[6]{0:T(128)} %stack.31.plan_ref, bf16[1024,1024]{1,0:T(8,128)(2,1)} %get-tuple-element.76.lead_ref, bf16[1024,1024]{1,0:T(8,128)(2,1)} %get-tuple-element.77.tail_ref, ...), custom_call_target="tpu_custom_call" | custom-call | flops 536870912 | bytes 4194304 | tf_op jit(solution)/shard_map/early_grads/pallas_call | solution.py:457
  49.5 3.0 %collective-permute-start.5 = (f32[512,256]{1,0:T(8,128)}, f32[512,256]{1,0:T(8,128)S(1)}, u32[]{:S(2)}, u32[]{:S(2)}) collective-permute-start(f32[512,256]{1,0:T(8,128)} %get-tuple-element.89), channel_id=1, source_target_pairs={{0,1},{1,0},{2,3},{3,2},{4,5},{5,4},{6,7},{7,6},{8,9},{9,8},{10,11... | collective-permute-start | bytes 1572872 | tf_op jit(solution)/shard_map/ppermute | solution.py:766
  52.5 3.6 %collective-permute-start.6 = (f32[512,256]{1,0:T(8,128)}, f32[512,256]{1,0:T(8,128)S(1)}, u32[]{:S(2)}, u32[]{:S(2)}) collective-permute-start(f32[512,256]{1,0:T(8,128)} %get-tuple-element.90), channel_id=1, source_target_pairs={{0,2},{3,1},{4,6},{7,5},{8,10},{11,9},{12,14},{15,13},{16,18},{19,... | collective-permute-start | bytes 1572872 | tf_op jit(solution)/shard_map/ppermute | solution.py:765
  56.1 0.9 collective-permute-start.7
  57.0 17.7 %outputs_and_terms.1 = (bf16[2048,1024]{1,0:T(8,128)(2,1)}, bf16[2048,1024]{1,0:T(8,128)(2,1)}, f32[512,256]{1,0:T(8,128)}, f32[512,256]{1,0:T(8,128)}) custom-call(s32[6]{0:T(128)} %stack.31.plan_ref, bf16[2048,1024]{1,0:T(8,128)(2,1)} %inputs_ref.7, bf16[2048,1024]{1,0:T(8,128)(2,1)} %grad_ref.7, bf16[2048,128]{1,0:T(8,128)(2,1)} %write_ref.7, ...), custom_call_target="tpu_custom_call" | custom-call | flops 2147483648 | bytes 12582912 | tf_op jit(solution)/shard_map/outputs_and_terms/pallas_call | solution.py:638
  74.7 0.9 collective-permute-done.6
  75.6 1.4 %select_add_fusion = (f32[512,256]{1,0:T(8,128)S(1)}, f32[512,256]{1,0:T(8,128)S(1)}) fusion(f32[512,256]{1,0:T(8,128)} %get-tuple-element.99, f32[512,256]{1,0:T(8,128)S(1)} %collective-permute-done.5, pred[]{:T(512)S(6)} %or.3, f32[512,256]{1,0:T(8,128)S(1)} %collective-permute-done.6, f32[512,256]{1,0:T(8,128)S(1)} %collective-permute-done.7, ...), kind=kLoop, calls=%fused_computation | loop fusion | flops 786432 | bytes 3670017 | tf_op jit(solution)/shard_map/add | solution.py:772
  77.0 5.8 %collective-permute-start.8 = (f32[512,256]{1,0:T(8,128)S(1)}, f32[512,256]{1,0:T(8,128)S(1)}, u32[]{:S(2)}, u32[]{:S(2)}) collective-permute-start(f32[512,256]{1,0:T(8,128)S(1)} %get-tuple-element.112), channel_id=1, source_target_pairs={{0,1},{1,3},{3,2},{2,0},{4,5},{5,7},{7,6},{6,4},{8,9},{9,11},{11,1... | collective-permute-start | bytes 1572872 | tf_op jit(solution)/shard_map/ppermute | solution.py:772
  82.7 13.6 %outputs.1 = (bf16[2048,1024]{1,0:T(8,128)(2,1)}, bf16[2048,1024]{1,0:T(8,128)(2,1)}) custom-call(s32[6]{0:T(128)} %stack.31.plan_ref, bf16[2048,1024]{1,0:T(8,128)(2,1)} %inputs_ref.7, bf16[2048,1024]{1,0:T(8,128)(2,1)} %grad_ref.7, bf16[2048,128]{1,0:T(8,128)(2,1)} %write_ref.7, ...), custom_call_target="tpu_custom_call", output_to_operand_aliasing={{0}: (14, {}), {1}: (15, {})} | custom-call | flops 2147483648 | bytes 12582912 | tf_op jit(solution)/shard_map/outputs/pallas_call | solution.py:638
  96.4 0.8 fusion.4
  (20 shorter events, 0.4 us)
Async XLA Ops:
  9.4 3.6 %collective-permute-start = (f32[264,1024]{1,0:T(8,128)}, f32[264,1024]{1,0:T(8,128)S(1)}, u32[]{:S(2)}, u32[]{:S(2)}) collective-permute-start(f32[264,1024]{1,0:T(8,128)} %totals.1), channel_id=1, source_target_pairs={{0,4},{4,0},{8,12},{12,8},{16,20},{20,16},{24,28},{28,24},{1,5},{5... | collective-permute-start | bytes 3244040 | tf_op jit(solution)/shard_map/ppermute | solution.py:687
  13.0 2.1 %copy-start = (f32[264,1024]{1,0:T(8,128)}, f32[264,1024]{1,0:T(8,128)S(1)}, u32[]{:S(2)}) copy-start(f32[264,1024]{1,0:T(8,128)S(1)} %collective-permute-done.other_ref) | copy-start | bytes 3244036
  15.1 22.1 %collective-permute-start.1 = (f32[72,1024]{1,0:T(8,128)S(1)}, f32[72,1024]{1,0:T(8,128)S(1)}, u32[]{:S(2)}, u32[]{:S(2)}) collective-permute-start(f32[72,1024]{1,0:T(8,128)S(1)} %get-tuple-element.118), channel_id=1, source_target_pairs={{0,8},{4,12},{8,0},{12,4},{16,24},{20,28},{24,16},{28,20},{1,9},{5... | collective-permute-start | bytes 884744 | tf_op jit(solution)/shard_map/ppermute | solution.py:706
  17.7 19.5 %collective-permute-start.2 = (f32[72,1024]{1,0:T(8,128)S(1)}, f32[72,1024]{1,0:T(8,128)S(1)}, u32[]{:S(2)}, u32[]{:S(2)}) collective-permute-start(f32[72,1024]{1,0:T(8,128)S(1)} %get-tuple-element.117), channel_id=1, source_target_pairs={{0,16},{4,20},{8,24},{12,28},{16,0},{20,4},{24,8},{28,12},{1,17},{... | collective-permute-start | bytes 884744 | tf_op jit(solution)/shard_map/ppermute | solution.py:706
  19.2 18.0 %collective-permute-start.3 = (f32[72,1024]{1,0:T(8,128)S(1)}, f32[72,1024]{1,0:T(8,128)S(1)}, u32[]{:S(2)}, u32[]{:S(2)}) collective-permute-start(f32[72,1024]{1,0:T(8,128)S(1)} %get-tuple-element.116), channel_id=1, source_target_pairs={{0,24},{4,28},{8,16},{12,20},{16,8},{20,12},{24,0},{28,4},{1,25},{... | collective-permute-start | bytes 884744 | tf_op jit(solution)/shard_map/ppermute | solution.py:706
  37.2 0.7 copy-start.2
  37.2 0.8 copy-start.3
  37.2 0.9 copy-start.4
  40.2 2.1 %collective-permute-start.4 = (f32[128,1024]{1,0:T(8,128)}, f32[128,1024]{1,0:T(8,128)S(1)}, u32[]{:S(2)}, u32[]{:S(2)}) collective-permute-start(f32[128,1024]{1,0:T(8,128)} %combine.1.own_ref), channel_id=1, source_target_pairs={{0,4},{4,0},{8,12},{12,8},{16,20},{20,16},{24,28},{28,24},{1,5},{5... | collective-permute-start | bytes 1572872 | tf_op jit(solution)/shard_map/ppermute | solution.py:709
  42.3 0.8 copy-start.1
  49.5 25.2 %collective-permute-start.5 = (f32[512,256]{1,0:T(8,128)}, f32[512,256]{1,0:T(8,128)S(1)}, u32[]{:S(2)}, u32[]{:S(2)}) collective-permute-start(f32[512,256]{1,0:T(8,128)} %get-tuple-element.89), channel_id=1, source_target_pairs={{0,1},{1,0},{2,3},{3,2},{4,5},{5,4},{6,7},{7,6},{8,9},{9,8},{10,11... | collective-permute-start | bytes 1572872 | tf_op jit(solution)/shard_map/ppermute | solution.py:766
  52.5 23.1 %collective-permute-start.6 = (f32[512,256]{1,0:T(8,128)}, f32[512,256]{1,0:T(8,128)S(1)}, u32[]{:S(2)}, u32[]{:S(2)}) collective-permute-start(f32[512,256]{1,0:T(8,128)} %get-tuple-element.90), channel_id=1, source_target_pairs={{0,2},{3,1},{4,6},{7,5},{8,10},{11,9},{12,14},{15,13},{16,18},{19,... | collective-permute-start | bytes 1572872 | tf_op jit(solution)/shard_map/ppermute | solution.py:765
  56.1 19.5 %collective-permute-start.7 = (f32[512,256]{1,0:T(8,128)}, f32[512,256]{1,0:T(8,128)S(1)}, u32[]{:S(2)}, u32[]{:S(2)}) collective-permute-start(f32[512,256]{1,0:T(8,128)} %get-tuple-element.90), channel_id=1, source_target_pairs={{1,2},{2,1},{5,6},{6,5},{9,10},{10,9},{13,14},{14,13},{17,18},{18,... | collective-permute-start | bytes 1572872 | tf_op jit(solution)/shard_map/ppermute | solution.py:767
  77.0 19.4 %collective-permute-start.8 = (f32[512,256]{1,0:T(8,128)S(1)}, f32[512,256]{1,0:T(8,128)S(1)}, u32[]{:S(2)}, u32[]{:S(2)}) collective-permute-start(f32[512,256]{1,0:T(8,128)S(1)} %get-tuple-element.112), channel_id=1, source_target_pairs={{0,1},{1,3},{3,2},{2,0},{4,5},{5,7},{7,6},{6,4},{8,9},{9,11},{11,1... | collective-permute-start | bytes 1572872 | tf_op jit(solution)/shard_map/ppermute | solution.py:772

commit v5 on v4

--- a/solution.py
+++ b/solution.py
@@ -150,7 +150,7 @@
             pltpu.VMEM((length, 128), BF16),
             pltpu.VMEM((2, 128, lanes), BF16),
         ],
-        compiler_params=pltpu.CompilerParams(vmem_limit_bytes=VMEM_BYTES),
+        compiler_params=pltpu.CompilerParams(vmem_limit_bytes=48 * 1024 * 1024),
         cost_estimate=pl.CostEstimate(
             flops=6 * length * lanes * states, bytes_accessed=4 * length * lanes, transcendentals=0
         ),
@@ -194,7 +194,7 @@
             jax.ShapeDtypeStruct((count, lanes), F32),
             jax.ShapeDtypeStruct((2 * count, lanes), F32),
         ),
-        compiler_params=pltpu.CompilerParams(vmem_limit_bytes=VMEM_BYTES),
+        compiler_params=pltpu.CompilerParams(vmem_limit_bytes=48 * 1024 * 1024),
         cost_estimate=pl.CostEstimate(
             flops=heads * length * 6000, bytes_accessed=1000 * length, transcendentals=0
         ),
@@ -389,7 +389,7 @@
                 pltpu.VMEM((3, 128, lanes), BF16),
             ],
         ),
-        compiler_params=pltpu.CompilerParams(vmem_limit_bytes=VMEM_BYTES),
+        compiler_params=pltpu.CompilerParams(vmem_limit_bytes=44 * 1024 * 1024),
         cost_estimate=pl.CostEstimate(
             flops=24 * length * lanes * states, bytes_accessed=8 * length * lanes, transcendentals=0
         ),
@@ -472,7 +472,7 @@
             out_specs=tuple(whole(x) for x in shapes),
             scratch_shapes=[pltpu.VMEM((2, states, lanes), BF16)],
         ),
-        compiler_params=pltpu.CompilerParams(vmem_limit_bytes=VMEM_BYTES),
+        compiler_params=pltpu.CompilerParams(vmem_limit_bytes=24 * 1024 * 1024),
         cost_estimate=pl.CostEstimate(
             flops=8 * STEP * lanes * states, bytes_accessed=8 * STEP * lanes, transcendentals=0
         ),
@@ -508,7 +508,7 @@
         in_specs=[pl.BlockSpec(memory_space=pltpu.SMEM)]
         + [pl.BlockSpec(memory_space=pltpu.VMEM)] * len(got),
         out_specs=pl.BlockSpec(memory_space=pltpu.VMEM),
-        compiler_params=pltpu.CompilerParams(vmem_limit_bytes=VMEM_BYTES),
+        compiler_params=pltpu.CompilerParams(vmem_limit_bytes=16 * 1024 * 1024),
         cost_estimate=pl.CostEstimate(
             flops=4 * len(got) * rows * lanes,
             bytes_accessed=4 * (len(got) + 2) * rows * lanes,

time: 97.7 us -> 87.6 us (0.90)
  Pallas kernels: 69.1 us -> 56.9 us
  local copies, waits for them, and re-layouts: 3.17 us -> 5.53 us
  other arithmetic: 3.5 us -> 1.73 us
  starting transfers between devices: 17.7 us -> 18.8 us
    pallas_call x1, Pallas kernels: 6.4 us -> 2.29 us  [early_grads(): pl.pallas_call(early_grads_kernel, out_shape=shapes, grid_spec=pltpu.Pref...]
    pallas_call x1, Pallas kernels: 18 us -> 14.9 us  [local(): pl.pallas_call(local_kernel, out_shape=(jax.ShapeDtypeStruct((steps * sta...]
    unnamed x10 -> x30, local copies, waits for them, and re-layouts: 1.69 us -> 4.61 us
    pallas_call x1, Pallas kernels: 2.07 us -> 0.14 us  [combine(): pl.pallas_call(combine_kernel, out_shape=jax.ShapeDtypeStruct((2 * (rows...]
    pallas_call x1, Pallas kernels: 2.49 us -> 0.77 us  [factors(): pl.pallas_call(factors_kernel, out_shape=(jax.ShapeDtypeStruct((length, 1...]
    ppermute x1, waiting for transfers between devices: 0.01 us -> 1.42 us  [carried_states(): other = lax.ppermute(summed, axes, [(d, d ^ 1) for d in range(devices)])]
    pallas_call x1, Pallas kernels: 8.78 us -> 7.38 us  [totals(): pl.pallas_call(totals_kernel, out_shape=jax.ShapeDtypeStruct((2 * states...]
    select_n x2, other arithmetic: 1.2 us -> 0.18 us  [carried_states(): jnp.where(place < place ^ m, push, pull)]
  transfers between devices with their start and end apart: 9 -> 9, of which waited for: 2 -> 2; matrix products, arithmetic and copies ran while one was open for 1% -> 0% of each run, Pallas kernels for 53% -> 54%
where the time goes in v5:
time: 87.6 us; the launch traced here: 87.2 us
  Pallas kernels  56.9 us (65%)
  starting transfers between devices  18.8 us (21%)
  local copies, waits for them, and re-layouts  5.53 us (6%)
  waiting for transfers between devices  3.34 us (4%)
  other arithmetic  1.73 us (2%)
  between operations  0.93 us (1%)
    pallas_call x2, Pallas kernels, outputs(): pl.pallas_call(functools.partial(outputs_kernel, offset, with_terms, len(...  31.4 us
    pallas_call x1, Pallas kernels, local(): pl.pallas_call(local_kernel, out_shape=(jax.ShapeDtypeStruct((steps * sta...  14.9 us
    pallas_call x1, Pallas kernels, totals(): pl.pallas_call(totals_kernel, out_shape=jax.ShapeDtypeStruct((2 * states...  7.38 us
    ppermute x1, starting transfers between devices, on_device(): last = lax.ppermute(third + came, 'mp', [(0, 1), (1, 3), (3, 2), (2, 0)])  6.34 us
    unnamed x30, local copies, waits for them, and re-layouts  4.61 us
    ppermute x1, starting transfers between devices, on_device(): two_away = lax.ppermute(crossed, 'mp', [(0, 2), (3, 1)])  4.5 us
    ppermute x3, starting transfers between devices, carried_states(): lax.ppermute(sent, axes, [(d, d ^ 2 * m) for d in range(devices)])  4.47 us
    pallas_call x1, Pallas kernels, early_grads(): pl.pallas_call(early_grads_kernel, out_shape=shapes, grid_spec=pltpu.Pref...  2.29 us
  transfers between devices with their start and end apart: 9, of which 2 were waited for; matrix products, arithmetic and copies ran while one was open for 0% of the time, Pallas kernels for 54%

profile of v5, /device:TPU:0, one launch (start us, length us, event | category | flops | bytes accessed | tf_op | source)
XLA Modules:
  0.0 87.2 jit_solution(17884785122432925681)
XLA Ops:
  0.6 1.0 %copy-done = bf16[2048,128]{1,0:T(8,128)(2,1)S(1)} copy-done((bf16[2048,128]{1,0:T(8,128)(2,1)S(1)}, bf16[2048,128]{1,0:T(8,128)(2,1)}, u32[]{:S(2)}) %copy-start) | copy-done | bytes 524312
  1.7 1.0 %copy-done.2 = bf16[2048,128]{1,0:T(8,128)(2,1)S(1)} copy-done((bf16[2048,128]{1,0:T(8,128)(2,1)S(1)}, bf16[2048,128]{1,0:T(8,128)(2,1)}, u32[]{:S(2)}) %copy-start.2) | copy-done | bytes 524312
  2.7 0.9 %copy-done.12 = f32[16,2048]{1,0:T(8,128)S(1)} copy-done((f32[16,2048]{1,0:T(8,128)S(1)}, f32[16,2048]{1,0:T(8,128)}, u32[]{:S(2)}) %copy-start.12) | copy-done | bytes 131096
  3.6 7.4 %totals.1 = f32[264,1024]{1,0:T(8,128)S(1)} custom-call(bf16[2048,1024]{1,0:T(8,128)(2,1)} %inputs_ref.7, bf16[2048,1024]{1,0:T(8,128)(2,1)} %grad_ref.7, f32[16,2048]{1,0:T(8,128)S(1)} %copy-done.12, bf16[2048,128]{1,0:T(8,128)(2,1)S(1)} %copy-done, bf16[2048,128]{1,0:T(8,128)(2,1)S(1)} %copy-done.2), custom_call_target="tpu_custom_call" | custom-call | flops 1610612736 | bytes 8388608 | tf_op jit(solution)/shard_map/totals/pallas_call | solution.py:143
  11.0 0.5 collective-permute-start
  11.6 0.8 factors.1
  12.4 1.4 %collective-permute-done.other_ref = f32[264,1024]{1,0:T(8,128)S(1)} collective-permute-done((f32[264,1024]{1,0:T(8,128)S(1)}, f32[264,1024]{1,0:T(8,128)S(1)}, u32[]{:S(2)}, u32[]{:S(2)}) %collective-permute-start) | collective-permute-done | bytes 1081376 | tf_op jit(solution)/shard_map/ppermute | solution.py:687
  13.9 0.1 broadcast_select_fusion
  14.2 2.9 %collective-permute-start.1 = (f32[72,1024]{1,0:T(8,128)S(1)}, f32[72,1024]{1,0:T(8,128)S(1)}, u32[]{:S(2)}, u32[]{:S(2)}) collective-permute-start(f32[72,1024]{1,0:T(8,128)S(1)} %get-tuple-element.118), channel_id=1, source_target_pairs={{0,8},{4,12},{8,0},{12,4},{16,24},{20,28},{24,16},{28,20},{1,9},{5... | collective-permute-start | bytes 884744 | tf_op jit(solution)/shard_map/ppermute | solution.py:706
  17.1 1.5 %collective-permute-start.2 = (f32[72,1024]{1,0:T(8,128)S(1)}, f32[72,1024]{1,0:T(8,128)S(1)}, u32[]{:S(2)}, u32[]{:S(2)}) collective-permute-start(f32[72,1024]{1,0:T(8,128)S(1)} %get-tuple-element.117), channel_id=1, source_target_pairs={{0,16},{4,20},{8,24},{12,28},{16,0},{20,4},{24,8},{28,12},{1,17},{... | collective-permute-start | bytes 884744 | tf_op jit(solution)/shard_map/ppermute | solution.py:706
  18.7 14.9 %local.1 = (bf16[512,1024]{1,0:T(8,128)(2,1)S(1)}, bf16[512,1024]{1,0:T(8,128)(2,1)S(1)}, f32[1024,128]{1,0:T(8,128)S(1)}, f32[1024,128]{1,0:T(8,128)S(1)}, bf16...) custom-call(s32[6]{0:T(128)S(1)} %stack.31.plan_ref, bf16[2048,1024]{1,0:T(8,128)(2,1)} %inputs_ref.7, ...), custom_call_target="tpu_custom_call" | custom-call | flops 6442450944 | bytes 16777216 | tf_op jit(solution)/shard_map/local/pallas_call | solution.py:351
  33.7 0.1 combine.1.own_ref
  33.9 1.9 %collective-permute-done.4.others_ref = f32[128,1024]{1,0:T(8,128)S(1)} collective-permute-done((f32[128,1024]{1,0:T(8,128)S(1)}, f32[128,1024]{1,0:T(8,128)S(1)}, u32[]{:S(2)}, u32[]{:S(2)}) %collective-permute-start.4) | collective-permute-done | bytes 524320 | tf_op jit(solution)/shard_map/ppermute | solution.py:709
  35.8 2.3 %early_grads.1 = (f32[128,1024]{1,0:T(8,128)S(1)}, f32[128,1024]{1,0:T(8,128)S(1)}, f32[512,256]{1,0:T(8,128)S(1)}, f32[512,256]{1,0:T(8,128)S(1)}) custom-call(s32[6]{0:T(128)S(1)} %stack.31.plan_ref, bf16[1024,1024]{1,0:T(8,128)(2,1)S(1)} %get-tuple-element.76.lead_ref, bf16[1024,1024]{1,0:T(8,128)(2,1)S(1)} %get-tuple-element.77.tail_ref, ...), custom_call_target="tpu_custom_call" | custom-call | flops 536870912 | bytes 4194304 | tf_op jit(solution)/shard_map/early_grads/pallas_call | solution.py:457
  38.1 0.8 copy-done.7
  38.9 0.8 copy-done.8
  39.7 2.0 %collective-permute-start.5 = (f32[512,256]{1,0:T(8,128)S(1)}, f32[512,256]{1,0:T(8,128)S(1)}, u32[]{:S(2)}, u32[]{:S(2)}) collective-permute-start(f32[512,256]{1,0:T(8,128)S(1)} %get-tuple-element.89), channel_id=1, source_target_pairs={{0,1},{1,0},{2,3},{3,2},{4,5},{5,4},{6,7},{7,6},{8,9},{9,8},{10,11... | collective-permute-start | bytes 1572872 | tf_op jit(solution)/shard_map/ppermute | solution.py:766
  41.7 4.5 %collective-permute-start.6 = (f32[512,256]{1,0:T(8,128)S(1)}, f32[512,256]{1,0:T(8,128)S(1)}, u32[]{:S(2)}, u32[]{:S(2)}) collective-permute-start(f32[512,256]{1,0:T(8,128)S(1)} %get-tuple-element.90), channel_id=1, source_target_pairs={{0,2},{3,1},{4,6},{7,5},{8,10},{11,9},{12,14},{15,13},{16,18},{19,... | collective-permute-start | bytes 1572872 | tf_op jit(solution)/shard_map/ppermute | solution.py:765
  46.2 0.9 %collective-permute-start.7 = (f32[512,256]{1,0:T(8,128)S(1)}, f32[512,256]{1,0:T(8,128)S(1)}, u32[]{:S(2)}, u32[]{:S(2)}) collective-permute-start(f32[512,256]{1,0:T(8,128)S(1)} %get-tuple-element.90), channel_id=1, source_target_pairs={{1,2},{2,1},{5,6},{6,5},{9,10},{10,9},{13,14},{14,13},{17,18},{18,... | collective-permute-start | bytes 1572872 | tf_op jit(solution)/shard_map/ppermute | solution.py:767
  47.1 17.8 %outputs_and_terms.1 = (bf16[2048,1024]{1,0:T(8,128)(2,1)}, bf16[2048,1024]{1,0:T(8,128)(2,1)}, f32[512,256]{1,0:T(8,128)}, f32[512,256]{1,0:T(8,128)}) custom-call(s32[6]{0:T(128)} %copy-done.14, bf16[2048,1024]{1,0:T(8,128)(2,1)} %inputs_ref.7, bf16[2048,1024]{1,0:T(8,128)(2,1)} %grad_ref.7, bf16[2048,128]{1,0:T(8,128)(2,1)} %write_ref.7, ...), custom_call_target="tpu_custom_call" | custom-call | flops 2147483648 | bytes 12582912 | tf_op jit(solution)/shard_map/outputs_and_terms/pallas_call | solution.py:638
  65.0 1.4 %select_add_fusion = (f32[512,256]{1,0:T(8,128)S(1)}, f32[512,256]{1,0:T(8,128)S(1)}) fusion(f32[512,256]{1,0:T(8,128)} %get-tuple-element.99, f32[512,256]{1,0:T(8,128)S(1)} %collective-permute-done.5, pred[]{:T(512)S(6)} %or.3, f32[512,256]{1,0:T(8,128)S(1)} %collective-permute-done.6, f32[512,256]{1,0:T(8,128)S(1)} %collective-permute-done.7, ...), kind=kLoop, calls=%fused_computation | loop fusion | flops 786432 | bytes 3670017 | tf_op jit(solution)/shard_map/add | solution.py:772
  66.3 6.3 %collective-permute-start.8 = (f32[512,256]{1,0:T(8,128)S(1)}, f32[512,256]{1,0:T(8,128)S(1)}, u32[]{:S(2)}, u32[]{:S(2)}) collective-permute-start(f32[512,256]{1,0:T(8,128)S(1)} %get-tuple-element.112), channel_id=1, source_target_pairs={{0,1},{1,3},{3,2},{2,0},{4,5},{5,7},{7,6},{6,4},{8,9},{9,11},{11,1... | collective-permute-start | bytes 1572872 | tf_op jit(solution)/shard_map/ppermute | solution.py:772
  72.7 13.6 %outputs.1 = (bf16[2048,1024]{1,0:T(8,128)(2,1)}, bf16[2048,1024]{1,0:T(8,128)(2,1)}) custom-call(s32[6]{0:T(128)} %copy-done.14, bf16[2048,1024]{1,0:T(8,128)(2,1)} %inputs_ref.7, bf16[2048,1024]{1,0:T(8,128)(2,1)} %grad_ref.7, bf16[2048,128]{1,0:T(8,128)(2,1)} %write_ref.7, ...), custom_call_target="tpu_custom_call", output_to_operand_aliasing={{0}: (14, {}), {1}: (15, {})} | custom-call | flops 2147483648 | bytes 12582912 | tf_op jit(solution)/shard_map/outputs/pallas_call | solution.py:638
  86.4 0.8 fusion.4
  (40 shorter events, 0.5 us)
Async XLA Ops:
  0.6 1.0 %copy-start = (bf16[2048,128]{1,0:T(8,128)(2,1)S(1)}, bf16[2048,128]{1,0:T(8,128)(2,1)}, u32[]{:S(2)}) copy-start(bf16[2048,128]{1,0:T(8,128)(2,1)} %write_ref.7) | copy-start | bytes 1572868
  1.7 1.0 %copy-start.2 = (bf16[2048,128]{1,0:T(8,128)(2,1)S(1)}, bf16[2048,128]{1,0:T(8,128)(2,1)}, u32[]{:S(2)}) copy-start(bf16[2048,128]{1,0:T(8,128)(2,1)} %read_ref.7) | copy-start | bytes 1572868
  2.7 0.9 %copy-start.12 = (f32[16,2048]{1,0:T(8,128)S(1)}, f32[16,2048]{1,0:T(8,128)}, u32[]{:S(2)}) copy-start(f32[16,2048]{1,0:T(8,128)} %ld_ref.2) | copy-start | bytes 393220
  3.6 8.0 %copy-start.13 = (f32[16,2048]{1,0:T(8,128)S(1)}, f32[16,2048]{1,0:T(8,128)}, u32[]{:S(2)}) copy-start(f32[16,2048]{1,0:T(8,128)} %ld_ref.2) | copy-start | bytes 393220
  11.0 2.8 %collective-permute-start = (f32[264,1024]{1,0:T(8,128)S(1)}, f32[264,1024]{1,0:T(8,128)S(1)}, u32[]{:S(2)}, u32[]{:S(2)}) collective-permute-start(f32[264,1024]{1,0:T(8,128)S(1)} %totals.1), channel_id=1, source_target_pairs={{0,4},{4,0},{8,12},{12,8},{16,20},{20,16},{24,28},{28,24},{1,5},{5... | collective-permute-start | bytes 3244040 | tf_op jit(solution)/shard_map/ppermute | solution.py:687
  11.6 24.2 %copy-start.14 = (s32[6]{0:T(128)}, s32[6]{0:T(128)S(1)}, u32[]{:S(2)}) copy-start(s32[6]{0:T(128)S(1)} %stack.31.plan_ref) | copy-start | bytes 76
  12.4 6.3 %copy-start.6 = (bf16[2048,128]{1,0:T(8,128)(2,1)}, bf16[2048,128]{1,0:T(8,128)(2,1)S(1)}, u32[]{:S(2)}) copy-start(bf16[2048,128]{1,0:T(8,128)(2,1)S(1)} %get-tuple-element.72.parts_ref) | copy-start | bytes 1572868
  12.4 6.3 %copy-start.9 = (f32[256,128]{1,0:T(8,128)}, f32[256,128]{1,0:T(8,128)S(1)}, u32[]{:S(2)}) copy-start(f32[256,128]{1,0:T(8,128)S(1)} %get-tuple-element.73.rows_ref) | copy-start | bytes 393220
  12.4 6.3 %copy-start.10 = (f32[32,1024]{1,0:T(8,128)}, f32[32,1024]{1,0:T(8,128)S(1)}, u32[]{:S(2)}) copy-start(f32[32,1024]{1,0:T(8,128)S(1)} %get-tuple-element.75.ranges_ref) | copy-start | bytes 393220
  12.4 6.3 %copy-start.11 = (f32[16,1024]{1,0:T(8,128)}, f32[16,1024]{1,0:T(8,128)S(1)}, u32[]{:S(2)}) copy-start(f32[16,1024]{1,0:T(8,128)S(1)} %get-tuple-element.74.decays_ref) | copy-start | bytes 196612
  13.9 4.8 %copy-start.1 = (bf16[2048,128]{1,0:T(8,128)(2,1)S(1)}, bf16[2048,128]{1,0:T(8,128)(2,1)}, u32[]{:S(2)}) copy-start(bf16[2048,128]{1,0:T(8,128)(2,1)} %write_ref.7) | copy-start | bytes 1572868
  13.9 4.8 %copy-start.3 = (bf16[2048,128]{1,0:T(8,128)(2,1)S(1)}, bf16[2048,128]{1,0:T(8,128)(2,1)}, u32[]{:S(2)}) copy-start(bf16[2048,128]{1,0:T(8,128)(2,1)} %read_ref.7) | copy-start | bytes 1572868
  14.2 19.4 %collective-permute-start.1 = (f32[72,1024]{1,0:T(8,128)S(1)}, f32[72,1024]{1,0:T(8,128)S(1)}, u32[]{:S(2)}, u32[]{:S(2)}) collective-permute-start(f32[72,1024]{1,0:T(8,128)S(1)} %get-tuple-element.118), channel_id=1, source_target_pairs={{0,8},{4,12},{8,0},{12,4},{16,24},{20,28},{24,16},{28,20},{1,9},{5... | collective-permute-start | bytes 884744 | tf_op jit(solution)/shard_map/ppermute | solution.py:706
  17.1 16.5 %collective-permute-start.2 = (f32[72,1024]{1,0:T(8,128)S(1)}, f32[72,1024]{1,0:T(8,128)S(1)}, u32[]{:S(2)}, u32[]{:S(2)}) collective-permute-start(f32[72,1024]{1,0:T(8,128)S(1)} %get-tuple-element.117), channel_id=1, source_target_pairs={{0,16},{4,20},{8,24},{12,28},{16,0},{20,4},{24,8},{28,12},{1,17},{... | collective-permute-start | bytes 884744 | tf_op jit(solution)/shard_map/ppermute | solution.py:706
  18.7 15.0 %collective-permute-start.3 = (f32[72,1024]{1,0:T(8,128)S(1)}, f32[72,1024]{1,0:T(8,128)S(1)}, u32[]{:S(2)}, u32[]{:S(2)}) collective-permute-start(f32[72,1024]{1,0:T(8,128)S(1)} %get-tuple-element.116), channel_id=1, source_target_pairs={{0,24},{4,28},{8,16},{12,20},{16,8},{20,12},{24,0},{28,4},{1,25},{... | collective-permute-start | bytes 884744 | tf_op jit(solution)/shard_map/ppermute | solution.py:706
  33.6 4.5 %copy-start.4 = (bf16[512,1024]{1,0:T(8,128)(2,1)}, bf16[512,1024]{1,0:T(8,128)(2,1)S(1)}, u32[]{:S(2)}) copy-start(bf16[512,1024]{1,0:T(8,128)(2,1)S(1)} %get-tuple-element.70.entries_ref) | copy-start | bytes 3145732
  33.6 4.5 %copy-start.5 = (bf16[512,1024]{1,0:T(8,128)(2,1)}, bf16[512,1024]{1,0:T(8,128)(2,1)S(1)}, u32[]{:S(2)}) copy-start(bf16[512,1024]{1,0:T(8,128)(2,1)S(1)} %get-tuple-element.71.afters_ref) | copy-start | bytes 3145732
  33.8 2.0 %collective-permute-start.4 = (f32[128,1024]{1,0:T(8,128)S(1)}, f32[128,1024]{1,0:T(8,128)S(1)}, u32[]{:S(2)}, u32[]{:S(2)}) collective-permute-start(f32[128,1024]{1,0:T(8,128)S(1)} %combine.1.own_ref), channel_id=1, source_target_pairs={{0,4},{4,0},{8,12},{12,8},{16,20},{20,16},{24,28},{28,24},{1,5},{5... | collective-permute-start | bytes 1572872 | tf_op jit(solution)/shard_map/ppermute | solution.py:709
  38.1 0.8 copy-start.7
  38.9 0.8 copy-start.8
  39.7 25.2 %collective-permute-start.5 = (f32[512,256]{1,0:T(8,128)S(1)}, f32[512,256]{1,0:T(8,128)S(1)}, u32[]{:S(2)}, u32[]{:S(2)}) collective-permute-start(f32[512,256]{1,0:T(8,128)S(1)} %get-tuple-element.89), channel_id=1, source_target_pairs={{0,1},{1,0},{2,3},{3,2},{4,5},{5,4},{6,7},{7,6},{8,9},{9,8},{10,11... | collective-permute-start | bytes 1572872 | tf_op jit(solution)/shard_map/ppermute | solution.py:766
  41.7 23.2 %collective-permute-start.6 = (f32[512,256]{1,0:T(8,128)S(1)}, f32[512,256]{1,0:T(8,128)S(1)}, u32[]{:S(2)}, u32[]{:S(2)}) collective-permute-start(f32[512,256]{1,0:T(8,128)S(1)} %get-tuple-element.90), channel_id=1, source_target_pairs={{0,2},{3,1},{4,6},{7,5},{8,10},{11,9},{12,14},{15,13},{16,18},{19,... | collective-permute-start | bytes 1572872 | tf_op jit(solution)/shard_map/ppermute | solution.py:765
  46.2 18.7 %collective-permute-start.7 = (f32[512,256]{1,0:T(8,128)S(1)}, f32[512,256]{1,0:T(8,128)S(1)}, u32[]{:S(2)}, u32[]{:S(2)}) collective-permute-start(f32[512,256]{1,0:T(8,128)S(1)} %get-tuple-element.90), channel_id=1, source_target_pairs={{1,2},{2,1},{5,6},{6,5},{9,10},{10,9},{13,14},{14,13},{17,18},{18,... | collective-permute-start | bytes 1572872 | tf_op jit(solution)/shard_map/ppermute | solution.py:767
  66.3 20.0 %collective-permute-start.8 = (f32[512,256]{1,0:T(8,128)S(1)}, f32[512,256]{1,0:T(8,128)S(1)}, u32[]{:S(2)}, u32[]{:S(2)}) collective-permute-start(f32[512,256]{1,0:T(8,128)S(1)} %get-tuple-element.112), channel_id=1, source_target_pairs={{0,1},{1,3},{3,2},{2,0},{4,5},{5,7},{7,6},{6,4},{8,9},{9,11},{11,1... | collective-permute-start | bytes 1572872 | tf_op jit(solution)/shard_map/ppermute | solution.py:772

commit v6 on v5

--- a/solution.py
+++ b/solution.py
@@ -406,14 +406,13 @@
     own_ref,
     others_ref,
     other_ref,
-    entry_ref,
-    after_ref,
+    ends_ref,
     far_ref,
     crossed_ref,
     halved,
 ):
     step = pl.program_id(0)
-    states, lanes = entry_ref.shape
+    states = ends_ref.shape[0] // 2
     part = states // 2
 
     @pl.when(step == 0)
@@ -426,8 +425,8 @@
         decay = other_ref[2 * states : 2 * states + 1]
         entry = jnp.where(first, entry, other_ref[:states] + decay * entry)
         after = jnp.where(first, other_ref[states : 2 * states] + decay * after, after)
-        entry_ref[...] = entry
-        after_ref[...] = after
+        ends_ref[:states] = entry
+        ends_ref[states:] = after
         halved[0] = entry.astype(BF16)
         halved[1] = after.astype(BF16)
 
@@ -451,9 +450,9 @@
     def whole(x):
         return pl.BlockSpec(x.shape, lambda c, plan: (0, 0))
 
-    state = jax.ShapeDtypeStruct((states, lanes), F32)
+    ends = jax.ShapeDtypeStruct((2 * states, lanes), F32)
     terms = jax.ShapeDtypeStruct((STEP, 2 * states), F32)
-    shapes = (state, state, terms, terms)
+    shapes = (ends, terms, terms)
     return pl.pallas_call(
         early_grads_kernel,
         out_shape=shapes,
@@ -533,8 +532,7 @@
     rows_ref,
     decays_ref,
     ranges_ref,
-    entry_ref,
-    after_ref,
+    ends_ref,
     skip_ref,
     *rest,
 ):
@@ -557,14 +555,14 @@
     lead = (leads * grad_ref[...].astype(F32)).astype(BF16)
     tail = (tails * inputs_ref[...].astype(F32)).astype(BF16)
     start = plan_ref[offset + step] * inner
-    state = entries_ref[...].astype(F32) + ranges_ref[pl.ds(start, 1), :] * entry_ref[...]
+    state = entries_ref[...].astype(F32) + ranges_ref[pl.ds(start, 1), :] * ends_ref[:states]
     for k in range(inner):
         at = slice(k * BLOCK, k * BLOCK + BLOCK)
         states_in[at] = state.astype(BF16)
         if k < inner - 1:
             state = state * decays_ref[pl.ds(start + k, 1), :] + dot(write_ref[at, :], tail[at], 0, 0)
     end = start + inner - 1
-    state = afters_ref[...].astype(F32) + ranges_ref[pl.ds(count + end, 1), :] * after_ref[...]
+    state = afters_ref[...].astype(F32) + ranges_ref[pl.ds(count + end, 1), :] * ends_ref[states:]
     for k in reversed(range(inner)):
         at = slice(k * BLOCK, k * BLOCK + BLOCK)
         states_out[at] = state.astype(BF16)
@@ -619,7 +617,7 @@
 
 
 def outputs(
-    plan, offset, steps, with_terms, earlier, inputs, grad_out, write_keys, read_keys, made, entry, after, skip
+    plan, offset, steps, with_terms, earlier, inputs, grad_out, write_keys, read_keys, made, ends, skip
 ):
     length, lanes = inputs.shape
     states = write_keys.shape[1]
@@ -652,8 +650,7 @@
                 tokens(STEP // BLOCK * heads, BLOCK),
                 whole(decays),
                 whole(ranges),
-                whole(entry),
-                whole(after),
+                whole(ends),
                 whole(skip),
                 *[pl.BlockSpec(memory_space=pl.ANY) for _ in earlier],
             ],
@@ -665,7 +662,7 @@
                 pltpu.VMEM((8, lanes), F32),
             ],
         ),
-        input_output_aliases={14 + k: k for k in range(len(earlier))},
+        input_output_aliases={13 + k: k for k in range(len(earlier))},
         compiler_params=pltpu.CompilerParams(vmem_limit_bytes=VMEM_BYTES),
         cost_estimate=pl.CostEstimate(
             flops=16 * steps * STEP * lanes * states, bytes_accessed=12 * steps * STEP * lanes, transcendentals=0
@@ -673,7 +670,7 @@
         name="outputs_and_terms" if with_terms else "outputs",
     )(
         plan, inputs, grad_out, write_keys, read_keys, entries, afters, parts, rows, decays, ranges,
-        entry, after, skip, *earlier,
+        ends, skip, *earlier,
     )
 
 
@@ -747,12 +744,12 @@
 
     given, made = carried_states(summed, states, first_window, second_window)
     (entries, afters, read_terms, write_terms, lead, tail), made = made
-    entry, after, far, crossed = early_grads(plan, lead, tail, read_terms, write_terms, *given)
+    states_at_ends, far, crossed = early_grads(plan, lead, tail, read_terms, write_terms, *given)
 
     def part(offset, steps, with_terms, earlier):
         return outputs(
             plan, offset, steps, with_terms, earlier, inputs, grad_out, write_keys, read_keys,
-            (entries, afters, *made), entry, after, skip_gain[None],
+            (entries, afters, *made), states_at_ends, skip_gain[None],
         )
 
     if not line:

time: 87.6 us -> 87 us (level)
    unnamed x30 -> x28, local copies, waits for them, and re-layouts: 4.61 us -> 4.01 us
where the time goes in v6:
time: 87 us; the launch traced here: 86.6 us
  Pallas kernels  56.9 us (65%)
  starting transfers between devices  18.8 us (22%)
  local copies, waits for them, and re-layouts  4.92 us (6%)
  waiting for transfers between devices  3.34 us (4%)
  other arithmetic  1.73 us (2%)
  between operations  0.93 us (1%)
    pallas_call x2, Pallas kernels, outputs(): pl.pallas_call(functools.partial(outputs_kernel, offset, with_terms, len(...  31.4 us
    pallas_call x1, Pallas kernels, local(): pl.pallas_call(local_kernel, out_shape=(jax.ShapeDtypeStruct((steps * sta...  14.9 us
    pallas_call x1, Pallas kernels, totals(): pl.pallas_call(totals_kernel, out_shape=jax.ShapeDtypeStruct((2 * states...  7.38 us
    ppermute x1, starting transfers between devices, on_device(): last = lax.ppermute(third + came, 'mp', [(0, 1), (1, 3), (3, 2), (2, 0)])  6.31 us
    ppermute x1, starting transfers between devices, on_device(): two_away = lax.ppermute(crossed, 'mp', [(0, 2), (3, 1)])  4.5 us
    ppermute x3, starting transfers between devices, carried_states(): lax.ppermute(sent, axes, [(d, d ^ 2 * m) for d in range(devices)])  4.47 us
    unnamed x28, local copies, waits for them, and re-layouts  4.01 us
    pallas_call x1, Pallas kernels, early_grads(): pl.pallas_call(early_grads_kernel, out_shape=shapes, grid_spec=pltpu.Pref...  2.29 us
  transfers between devices with their start and end apart: 9, of which 2 were waited for; matrix products, arithmetic and copies ran while one was open for 0% of the time, Pallas kernels for 54%

profile of v6, /device:TPU:0, one launch (start us, length us, event | category | flops | bytes accessed | tf_op | source)
XLA Modules:
  0.0 86.6 jit_solution(1560332116055621697)
XLA Ops:
  0.6 1.0 %copy-done = bf16[2048,128]{1,0:T(8,128)(2,1)S(1)} copy-done((bf16[2048,128]{1,0:T(8,128)(2,1)S(1)}, bf16[2048,128]{1,0:T(8,128)(2,1)}, u32[]{:S(2)}) %copy-start) | copy-done | bytes 524312
  1.7 1.0 %copy-done.2 = bf16[2048,128]{1,0:T(8,128)(2,1)S(1)} copy-done((bf16[2048,128]{1,0:T(8,128)(2,1)S(1)}, bf16[2048,128]{1,0:T(8,128)(2,1)}, u32[]{:S(2)}) %copy-start.2) | copy-done | bytes 524312
  2.7 0.9 %copy-done.11 = f32[16,2048]{1,0:T(8,128)S(1)} copy-done((f32[16,2048]{1,0:T(8,128)S(1)}, f32[16,2048]{1,0:T(8,128)}, u32[]{:S(2)}) %copy-start.11) | copy-done | bytes 131096
  3.6 7.4 %totals.1 = f32[264,1024]{1,0:T(8,128)S(1)} custom-call(bf16[2048,1024]{1,0:T(8,128)(2,1)} %inputs_ref.7, bf16[2048,1024]{1,0:T(8,128)(2,1)} %grad_ref.7, f32[16,2048]{1,0:T(8,128)S(1)} %copy-done.11, bf16[2048,128]{1,0:T(8,128)(2,1)S(1)} %copy-done, bf16[2048,128]{1,0:T(8,128)(2,1)S(1)} %copy-done.2), custom_call_target="tpu_custom_call" | custom-call | flops 1610612736 | bytes 8388608 | tf_op jit(solution)/shard_map/totals/pallas_call | solution.py:143
  11.0 0.5 collective-permute-start
  11.6 0.8 factors.1
  12.4 1.4 %collective-permute-done.other_ref = f32[264,1024]{1,0:T(8,128)S(1)} collective-permute-done((f32[264,1024]{1,0:T(8,128)S(1)}, f32[264,1024]{1,0:T(8,128)S(1)}, u32[]{:S(2)}, u32[]{:S(2)}) %collective-permute-start) | collective-permute-done | bytes 1081376 | tf_op jit(solution)/shard_map/ppermute | solution.py:684
  13.9 0.1 broadcast_select_fusion
  14.1 0.1 pad_maximum_fusion
  14.2 2.9 %collective-permute-start.1 = (f32[72,1024]{1,0:T(8,128)S(1)}, f32[72,1024]{1,0:T(8,128)S(1)}, u32[]{:S(2)}, u32[]{:S(2)}) collective-permute-start(f32[72,1024]{1,0:T(8,128)S(1)} %get-tuple-element.116), channel_id=1, source_target_pairs={{0,8},{4,12},{8,0},{12,4},{16,24},{20,28},{24,16},{28,20},{1,9},{5... | collective-permute-start | bytes 884744 | tf_op jit(solution)/shard_map/ppermute | solution.py:703
  17.1 1.5 %collective-permute-start.2 = (f32[72,1024]{1,0:T(8,128)S(1)}, f32[72,1024]{1,0:T(8,128)S(1)}, u32[]{:S(2)}, u32[]{:S(2)}) collective-permute-start(f32[72,1024]{1,0:T(8,128)S(1)} %get-tuple-element.115), channel_id=1, source_target_pairs={{0,16},{4,20},{8,24},{12,28},{16,0},{20,4},{24,8},{28,12},{1,17},{... | collective-permute-start | bytes 884744 | tf_op jit(solution)/shard_map/ppermute | solution.py:703
  18.7 14.9 %local.1 = (bf16[512,1024]{1,0:T(8,128)(2,1)S(1)}, bf16[512,1024]{1,0:T(8,128)(2,1)S(1)}, f32[1024,128]{1,0:T(8,128)S(1)}, f32[1024,128]{1,0:T(8,128)S(1)}, bf16...) custom-call(s32[6]{0:T(128)S(1)} %stack.31.plan_ref, bf16[2048,1024]{1,0:T(8,128)(2,1)} %inputs_ref.7, ...), custom_call_target="tpu_custom_call" | custom-call | flops 6442450944 | bytes 16777216 | tf_op jit(solution)/shard_map/local/pallas_call | solution.py:351
  33.7 0.1 combine.1.own_ref
  33.9 1.9 %collective-permute-done.4.others_ref = f32[128,1024]{1,0:T(8,128)S(1)} collective-permute-done((f32[128,1024]{1,0:T(8,128)S(1)}, f32[128,1024]{1,0:T(8,128)S(1)}, u32[]{:S(2)}, u32[]{:S(2)}) %collective-permute-start.4) | collective-permute-done | bytes 524320 | tf_op jit(solution)/shard_map/ppermute | solution.py:706
  35.8 2.3 %early_grads.1 = (f32[256,1024]{1,0:T(8,128)S(1)}, f32[512,256]{1,0:T(8,128)S(1)}, f32[512,256]{1,0:T(8,128)S(1)}) custom-call(s32[6]{0:T(128)S(1)} %stack.31.plan_ref, bf16[1024,1024]{1,0:T(8,128)(2,1)S(1)} %get-tuple-element.75.lead_ref, bf16[1024,1024]{1,0:T(8,128)(2,1)S(1)} %get-tuple-element.76.tail_ref, ...), custom_call_target="tpu_custom_call" | custom-call | flops 536870912 | bytes 4194304 | tf_op jit(solution)/shard_map/early_grads/pallas_call | solution.py:456
  38.1 1.0 %copy-done.6 = f32[256,1024]{1,0:T(8,128)} copy-done((f32[256,1024]{1,0:T(8,128)}, f32[256,1024]{1,0:T(8,128)S(1)}, u32[]{:S(2)}) %copy-start.6) | copy-done | bytes 1048600
  39.1 2.0 %collective-permute-start.5 = (f32[512,256]{1,0:T(8,128)S(1)}, f32[512,256]{1,0:T(8,128)S(1)}, u32[]{:S(2)}, u32[]{:S(2)}) collective-permute-start(f32[512,256]{1,0:T(8,128)S(1)} %get-tuple-element.87), channel_id=1, source_target_pairs={{0,1},{1,0},{2,3},{3,2},{4,5},{5,4},{6,7},{7,6},{8,9},{9,8},{10,11... | collective-permute-start | bytes 1572872 | tf_op jit(solution)/shard_map/ppermute | solution.py:763
  41.1 4.5 %collective-permute-start.6 = (f32[512,256]{1,0:T(8,128)S(1)}, f32[512,256]{1,0:T(8,128)S(1)}, u32[]{:S(2)}, u32[]{:S(2)}) collective-permute-start(f32[512,256]{1,0:T(8,128)S(1)} %get-tuple-element.88), channel_id=1, source_target_pairs={{0,2},{3,1},{4,6},{7,5},{8,10},{11,9},{12,14},{15,13},{16,18},{19,... | collective-permute-start | bytes 1572872 | tf_op jit(solution)/shard_map/ppermute | solution.py:762
  45.6 0.9 %collective-permute-start.7 = (f32[512,256]{1,0:T(8,128)S(1)}, f32[512,256]{1,0:T(8,128)S(1)}, u32[]{:S(2)}, u32[]{:S(2)}) collective-permute-start(f32[512,256]{1,0:T(8,128)S(1)} %get-tuple-element.88), channel_id=1, source_target_pairs={{1,2},{2,1},{5,6},{6,5},{9,10},{10,9},{13,14},{14,13},{17,18},{18,... | collective-permute-start | bytes 1572872 | tf_op jit(solution)/shard_map/ppermute | solution.py:764
  46.5 17.8 %outputs_and_terms.1 = (bf16[2048,1024]{1,0:T(8,128)(2,1)}, bf16[2048,1024]{1,0:T(8,128)(2,1)}, f32[512,256]{1,0:T(8,128)}, f32[512,256]{1,0:T(8,128)}) custom-call(s32[6]{0:T(128)} %copy-done.13, bf16[2048,1024]{1,0:T(8,128)(2,1)} %inputs_ref.7, bf16[2048,1024]{1,0:T(8,128)(2,1)} %grad_ref.7, bf16[2048,128]{1,0:T(8,128)(2,1)} %write_ref.7, ...), custom_call_target="tpu_custom_call" | custom-call | flops 2147483648 | bytes 12582912 | tf_op jit(solution)/shard_map/outputs_and_terms/pallas_call | solution.py:636
  64.4 1.4 %select_add_fusion = (f32[512,256]{1,0:T(8,128)S(1)}, f32[512,256]{1,0:T(8,128)S(1)}) fusion(f32[512,256]{1,0:T(8,128)} %get-tuple-element.97, f32[512,256]{1,0:T(8,128)S(1)} %collective-permute-done.5, pred[]{:T(512)S(6)} %or.3, f32[512,256]{1,0:T(8,128)S(1)} %collective-permute-done.6, f32[512,256]{1,0:T(8,128)S(1)} %collective-permute-done.7, ...), kind=kLoop, calls=%fused_computation | loop fusion | flops 786432 | bytes 3670017 | tf_op jit(solution)/shard_map/add | solution.py:769
  65.8 6.3 %collective-permute-start.8 = (f32[512,256]{1,0:T(8,128)S(1)}, f32[512,256]{1,0:T(8,128)S(1)}, u32[]{:S(2)}, u32[]{:S(2)}) collective-permute-start(f32[512,256]{1,0:T(8,128)S(1)} %get-tuple-element.110), channel_id=1, source_target_pairs={{0,1},{1,3},{3,2},{2,0},{4,5},{5,7},{7,6},{6,4},{8,9},{9,11},{11,1... | collective-permute-start | bytes 1572872 | tf_op jit(solution)/shard_map/ppermute | solution.py:769
  72.1 13.6 %outputs.1 = (bf16[2048,1024]{1,0:T(8,128)(2,1)}, bf16[2048,1024]{1,0:T(8,128)(2,1)}) custom-call(s32[6]{0:T(128)} %copy-done.13, bf16[2048,1024]{1,0:T(8,128)(2,1)} %inputs_ref.7, bf16[2048,1024]{1,0:T(8,128)(2,1)} %grad_ref.7, bf16[2048,128]{1,0:T(8,128)(2,1)} %write_ref.7, ...), custom_call_target="tpu_custom_call", output_to_operand_aliasing={{0}: (13, {}), {1}: (14, {})} | custom-call | flops 2147483648 | bytes 12582912 | tf_op jit(solution)/shard_map/outputs/pallas_call | solution.py:636
  85.8 0.8 fusion.4
  (38 shorter events, 0.4 us)
Async XLA Ops:
  0.6 1.0 %copy-start = (bf16[2048,128]{1,0:T(8,128)(2,1)S(1)}, bf16[2048,128]{1,0:T(8,128)(2,1)}, u32[]{:S(2)}) copy-start(bf16[2048,128]{1,0:T(8,128)(2,1)} %write_ref.7) | copy-start | bytes 1572868
  1.7 1.0 %copy-start.2 = (bf16[2048,128]{1,0:T(8,128)(2,1)S(1)}, bf16[2048,128]{1,0:T(8,128)(2,1)}, u32[]{:S(2)}) copy-start(bf16[2048,128]{1,0:T(8,128)(2,1)} %read_ref.7) | copy-start | bytes 1572868
  2.7 0.9 %copy-start.11 = (f32[16,2048]{1,0:T(8,128)S(1)}, f32[16,2048]{1,0:T(8,128)}, u32[]{:S(2)}) copy-start(f32[16,2048]{1,0:T(8,128)} %ld_ref.2) | copy-start | bytes 393220
  3.6 8.0 %copy-start.12 = (f32[16,2048]{1,0:T(8,128)S(1)}, f32[16,2048]{1,0:T(8,128)}, u32[]{:S(2)}) copy-start(f32[16,2048]{1,0:T(8,128)} %ld_ref.2) | copy-start | bytes 393220
  11.0 2.8 %collective-permute-start = (f32[264,1024]{1,0:T(8,128)S(1)}, f32[264,1024]{1,0:T(8,128)S(1)}, u32[]{:S(2)}, u32[]{:S(2)}) collective-permute-start(f32[264,1024]{1,0:T(8,128)S(1)} %totals.1), channel_id=1, source_target_pairs={{0,4},{4,0},{8,12},{12,8},{16,20},{20,16},{24,28},{28,24},{1,5},{5... | collective-permute-start | bytes 3244040 | tf_op jit(solution)/shard_map/ppermute | solution.py:684
  11.6 24.2 %copy-start.13 = (s32[6]{0:T(128)}, s32[6]{0:T(128)S(1)}, u32[]{:S(2)}) copy-start(s32[6]{0:T(128)S(1)} %stack.31.plan_ref) | copy-start | bytes 76
  12.4 6.3 %copy-start.7 = (bf16[2048,128]{1,0:T(8,128)(2,1)}, bf16[2048,128]{1,0:T(8,128)(2,1)S(1)}, u32[]{:S(2)}) copy-start(bf16[2048,128]{1,0:T(8,128)(2,1)S(1)} %get-tuple-element.71.parts_ref) | copy-start | bytes 1572868
  12.4 6.3 %copy-start.8 = (f32[256,128]{1,0:T(8,128)}, f32[256,128]{1,0:T(8,128)S(1)}, u32[]{:S(2)}) copy-start(f32[256,128]{1,0:T(8,128)S(1)} %get-tuple-element.72.rows_ref) | copy-start | bytes 393220
  12.4 6.3 %copy-start.9 = (f32[32,1024]{1,0:T(8,128)}, f32[32,1024]{1,0:T(8,128)S(1)}, u32[]{:S(2)}) copy-start(f32[32,1024]{1,0:T(8,128)S(1)} %get-tuple-element.74.ranges_ref) | copy-start | bytes 393220
  12.4 6.3 %copy-start.10 = (f32[16,1024]{1,0:T(8,128)}, f32[16,1024]{1,0:T(8,128)S(1)}, u32[]{:S(2)}) copy-start(f32[16,1024]{1,0:T(8,128)S(1)} %get-tuple-element.73.decays_ref) | copy-start | bytes 196612
  13.9 4.8 %copy-start.1 = (bf16[2048,128]{1,0:T(8,128)(2,1)S(1)}, bf16[2048,128]{1,0:T(8,128)(2,1)}, u32[]{:S(2)}) copy-start(bf16[2048,128]{1,0:T(8,128)(2,1)} %write_ref.7) | copy-start | bytes 1572868
  13.9 4.8 %copy-start.3 = (bf16[2048,128]{1,0:T(8,128)(2,1)S(1)}, bf16[2048,128]{1,0:T(8,128)(2,1)}, u32[]{:S(2)}) copy-start(bf16[2048,128]{1,0:T(8,128)(2,1)} %read_ref.7) | copy-start | bytes 1572868
  14.2 19.4 %collective-permute-start.1 = (f32[72,1024]{1,0:T(8,128)S(1)}, f32[72,1024]{1,0:T(8,128)S(1)}, u32[]{:S(2)}, u32[]{:S(2)}) collective-permute-start(f32[72,1024]{1,0:T(8,128)S(1)} %get-tuple-element.116), channel_id=1, source_target_pairs={{0,8},{4,12},{8,0},{12,4},{16,24},{20,28},{24,16},{28,20},{1,9},{5... | collective-permute-start | bytes 884744 | tf_op jit(solution)/shard_map/ppermute | solution.py:703
  17.1 16.5 %collective-permute-start.2 = (f32[72,1024]{1,0:T(8,128)S(1)}, f32[72,1024]{1,0:T(8,128)S(1)}, u32[]{:S(2)}, u32[]{:S(2)}) collective-permute-start(f32[72,1024]{1,0:T(8,128)S(1)} %get-tuple-element.115), channel_id=1, source_target_pairs={{0,16},{4,20},{8,24},{12,28},{16,0},{20,4},{24,8},{28,12},{1,17},{... | collective-permute-start | bytes 884744 | tf_op jit(solution)/shard_map/ppermute | solution.py:703
  18.7 15.0 %collective-permute-start.3 = (f32[72,1024]{1,0:T(8,128)S(1)}, f32[72,1024]{1,0:T(8,128)S(1)}, u32[]{:S(2)}, u32[]{:S(2)}) collective-permute-start(f32[72,1024]{1,0:T(8,128)S(1)} %get-tuple-element.114), channel_id=1, source_target_pairs={{0,24},{4,28},{8,16},{12,20},{16,8},{20,12},{24,0},{28,4},{1,25},{... | collective-permute-start | bytes 884744 | tf_op jit(solution)/shard_map/ppermute | solution.py:703
  33.6 4.5 %copy-start.4 = (bf16[512,1024]{1,0:T(8,128)(2,1)}, bf16[512,1024]{1,0:T(8,128)(2,1)S(1)}, u32[]{:S(2)}) copy-start(bf16[512,1024]{1,0:T(8,128)(2,1)S(1)} %get-tuple-element.69.entries_ref) | copy-start | bytes 3145732
  33.6 4.5 %copy-start.5 = (bf16[512,1024]{1,0:T(8,128)(2,1)}, bf16[512,1024]{1,0:T(8,128)(2,1)S(1)}, u32[]{:S(2)}) copy-start(bf16[512,1024]{1,0:T(8,128)(2,1)S(1)} %get-tuple-element.70.afters_ref) | copy-start | bytes 3145732
  33.8 2.0 %collective-permute-start.4 = (f32[128,1024]{1,0:T(8,128)S(1)}, f32[128,1024]{1,0:T(8,128)S(1)}, u32[]{:S(2)}, u32[]{:S(2)}) collective-permute-start(f32[128,1024]{1,0:T(8,128)S(1)} %combine.1.own_ref), channel_id=1, source_target_pairs={{0,4},{4,0},{8,12},{12,8},{16,20},{20,16},{24,28},{28,24},{1,5},{5... | collective-permute-start | bytes 1572872 | tf_op jit(solution)/shard_map/ppermute | solution.py:706
  38.1 1.0 %copy-start.6 = (f32[256,1024]{1,0:T(8,128)}, f32[256,1024]{1,0:T(8,128)S(1)}, u32[]{:S(2)}) copy-start(f32[256,1024]{1,0:T(8,128)S(1)} %get-tuple-element.82.ends_ref) | copy-start | bytes 3145732
  39.1 25.2 %collective-permute-start.5 = (f32[512,256]{1,0:T(8,128)S(1)}, f32[512,256]{1,0:T(8,128)S(1)}, u32[]{:S(2)}, u32[]{:S(2)}) collective-permute-start(f32[512,256]{1,0:T(8,128)S(1)} %get-tuple-element.87), channel_id=1, source_target_pairs={{0,1},{1,0},{2,3},{3,2},{4,5},{5,4},{6,7},{7,6},{8,9},{9,8},{10,11... | collective-permute-start | bytes 1572872 | tf_op jit(solution)/shard_map/ppermute | solution.py:763
  41.1 23.2 %collective-permute-start.6 = (f32[512,256]{1,0:T(8,128)S(1)}, f32[512,256]{1,0:T(8,128)S(1)}, u32[]{:S(2)}, u32[]{:S(2)}) collective-permute-start(f32[512,256]{1,0:T(8,128)S(1)} %get-tuple-element.88), channel_id=1, source_target_pairs={{0,2},{3,1},{4,6},{7,5},{8,10},{11,9},{12,14},{15,13},{16,18},{19,... | collective-permute-start | bytes 1572872 | tf_op jit(solution)/shard_map/ppermute | solution.py:762
  45.6 18.7 %collective-permute-start.7 = (f32[512,256]{1,0:T(8,128)S(1)}, f32[512,256]{1,0:T(8,128)S(1)}, u32[]{:S(2)}, u32[]{:S(2)}) collective-permute-start(f32[512,256]{1,0:T(8,128)S(1)} %get-tuple-element.88), channel_id=1, source_target_pairs={{1,2},{2,1},{5,6},{6,5},{9,10},{10,9},{13,14},{14,13},{17,18},{18,... | collective-permute-start | bytes 1572872 | tf_op jit(solution)/shard_map/ppermute | solution.py:764
  65.8 20.0 %collective-permute-start.8 = (f32[512,256]{1,0:T(8,128)S(1)}, f32[512,256]{1,0:T(8,128)S(1)}, u32[]{:S(2)}, u32[]{:S(2)}) collective-permute-start(f32[512,256]{1,0:T(8,128)S(1)} %get-tuple-element.110), channel_id=1, source_target_pairs={{0,1},{1,3},{3,2},{2,0},{4,5},{5,7},{7,6},{6,4},{8,9},{9,11},{11,1... | collective-permute-start | bytes 1572872 | tf_op jit(solution)/shard_map/ppermute | solution.py:769

commit v7 on v6

--- a/solution.py
+++ b/solution.py
@@ -389,7 +389,7 @@
                 pltpu.VMEM((3, 128, lanes), BF16),
             ],
         ),
-        compiler_params=pltpu.CompilerParams(vmem_limit_bytes=44 * 1024 * 1024),
+        compiler_params=pltpu.CompilerParams(vmem_limit_bytes=40 * 1024 * 1024),
         cost_estimate=pl.CostEstimate(
             flops=24 * length * lanes * states, bytes_accessed=8 * length * lanes, transcendentals=0
         ),

time: 87 us -> 86.4 us (level)
  local copies, waits for them, and re-layouts: 4.92 us -> 5.84 us
  waiting for transfers between devices: 3.34 us -> 2.44 us
    unnamed x28 -> x30, local copies, waits for them, and re-layouts: 4.01 us -> 4.93 us
    ppermute x1, waiting for transfers between devices: 1.42 us -> 0.52 us  [carried_states(): other = lax.ppermute(summed, axes, [(d, d ^ 1) for d in range(devices)])]
where the time goes in v7:
time: 86.4 us; the launch traced here: 86 us
  Pallas kernels  56.3 us (65%)
  starting transfers between devices  18.8 us (22%)
  local copies, waits for them, and re-layouts  5.84 us (7%)
  waiting for transfers between devices  2.44 us (3%)
  other arithmetic  1.73 us (2%)
  between operations  0.93 us (1%)
    pallas_call x2, Pallas kernels, outputs(): pl.pallas_call(functools.partial(outputs_kernel, offset, with_terms, len(...  31.5 us
    pallas_call x1, Pallas kernels, local(): pl.pallas_call(local_kernel, out_shape=(jax.ShapeDtypeStruct((steps * sta...  14.3 us
    pallas_call x1, Pallas kernels, totals(): pl.pallas_call(totals_kernel, out_shape=jax.ShapeDtypeStruct((2 * states...  7.33 us
    ppermute x1, starting transfers between devices, on_device(): last = lax.ppermute(third + came, 'mp', [(0, 1), (1, 3), (3, 2), (2, 0)])  6.3 us
    unnamed x30, local copies, waits for them, and re-layouts  4.93 us
    ppermute x1, starting transfers between devices, on_device(): two_away = lax.ppermute(crossed, 'mp', [(0, 2), (3, 1)])  4.52 us
    ppermute x3, starting transfers between devices, carried_states(): lax.ppermute(sent, axes, [(d, d ^ 2 * m) for d in range(devices)])  4.47 us
    pallas_call x1, Pallas kernels, early_grads(): pl.pallas_call(early_grads_kernel, out_shape=shapes, grid_spec=pltpu.Pref...  2.28 us
  transfers between devices with their start and end apart: 9, of which 2 were waited for; matrix products, arithmetic and copies ran while one was open for 0% of the time, Pallas kernels for 54%

profile of v7, /device:TPU:0, one launch (start us, length us, event | category | flops | bytes accessed | tf_op | source)
XLA Modules:
  0.0 86.0 jit_solution(17965395242246557091)
XLA Ops:
  0.6 1.0 %copy-done.1 = bf16[2048,128]{1,0:T(8,128)(2,1)S(1)} copy-done((bf16[2048,128]{1,0:T(8,128)(2,1)S(1)}, bf16[2048,128]{1,0:T(8,128)(2,1)}, u32[]{:S(2)}) %copy-start.1) | copy-done | bytes 524312
  1.7 1.0 %copy-done.3 = bf16[2048,128]{1,0:T(8,128)(2,1)S(1)} copy-done((bf16[2048,128]{1,0:T(8,128)(2,1)S(1)}, bf16[2048,128]{1,0:T(8,128)(2,1)}, u32[]{:S(2)}) %copy-start.3) | copy-done | bytes 524312
  2.7 0.9 %copy-done.12 = f32[16,2048]{1,0:T(8,128)S(1)} copy-done((f32[16,2048]{1,0:T(8,128)S(1)}, f32[16,2048]{1,0:T(8,128)}, u32[]{:S(2)}) %copy-start.12) | copy-done | bytes 131096
  3.6 7.3 %totals.1 = f32[264,1024]{1,0:T(8,128)S(1)} custom-call(bf16[2048,1024]{1,0:T(8,128)(2,1)} %inputs_ref.7, bf16[2048,1024]{1,0:T(8,128)(2,1)} %grad_ref.7, f32[16,2048]{1,0:T(8,128)S(1)} %copy-done.12, bf16[2048,128]{1,0:T(8,128)(2,1)S(1)} %copy-done.1, bf16[2048,128]{1,0:T(8,128)(2,1)S(1)} %copy-done.3), custom_call_target="tpu_custom_call" | custom-call | flops 1610612736 | bytes 8388608 | tf_op jit(solution)/shard_map/totals/pallas_call | solution.py:143
  11.0 0.5 collective-permute-start
  11.6 0.9 %copy-done.13 = f32[16,2048]{1,0:T(8,128)S(1)} copy-done((f32[16,2048]{1,0:T(8,128)S(1)}, f32[16,2048]{1,0:T(8,128)}, u32[]{:S(2)}) %copy-start.13) | copy-done | bytes 131096
  12.5 0.8 factors.1
  13.3 0.5 collective-permute-done.other_ref
  13.8 0.1 broadcast_select_fusion
  14.2 2.9 %collective-permute-start.1 = (f32[72,1024]{1,0:T(8,128)S(1)}, f32[72,1024]{1,0:T(8,128)S(1)}, u32[]{:S(2)}, u32[]{:S(2)}) collective-permute-start(f32[72,1024]{1,0:T(8,128)S(1)} %get-tuple-element.116), channel_id=1, source_target_pairs={{0,8},{4,12},{8,0},{12,4},{16,24},{20,28},{24,16},{28,20},{1,9},{5... | collective-permute-start | bytes 884744 | tf_op jit(solution)/shard_map/ppermute | solution.py:703
  17.1 1.5 %collective-permute-start.2 = (f32[72,1024]{1,0:T(8,128)S(1)}, f32[72,1024]{1,0:T(8,128)S(1)}, u32[]{:S(2)}, u32[]{:S(2)}) collective-permute-start(f32[72,1024]{1,0:T(8,128)S(1)} %get-tuple-element.115), channel_id=1, source_target_pairs={{0,16},{4,20},{8,24},{12,28},{16,0},{20,4},{24,8},{28,12},{1,17},{... | collective-permute-start | bytes 884744 | tf_op jit(solution)/shard_map/ppermute | solution.py:703
  18.7 14.3 %local.1 = (bf16[512,1024]{1,0:T(8,128)(2,1)S(1)}, bf16[512,1024]{1,0:T(8,128)(2,1)S(1)}, f32[1024,128]{1,0:T(8,128)S(1)}, f32[1024,128]{1,0:T(8,128)S(1)}, bf16...) custom-call(s32[6]{0:T(128)S(1)} %stack.31.plan_ref, bf16[2048,1024]{1,0:T(8,128)(2,1)S(1)} %copy-done, ...), custom_call_target="tpu_custom_call" | custom-call | flops 6442450944 | bytes 16777216 | tf_op jit(solution)/shard_map/local/pallas_call | solution.py:351
  33.0 0.1 combine.1.own_ref
  33.2 1.9 %collective-permute-done.4.others_ref = f32[128,1024]{1,0:T(8,128)S(1)} collective-permute-done((f32[128,1024]{1,0:T(8,128)S(1)}, f32[128,1024]{1,0:T(8,128)S(1)}, u32[]{:S(2)}, u32[]{:S(2)}) %collective-permute-start.4) | collective-permute-done | bytes 524320 | tf_op jit(solution)/shard_map/ppermute | solution.py:706
  35.1 2.3 %early_grads.1 = (f32[256,1024]{1,0:T(8,128)S(1)}, f32[512,256]{1,0:T(8,128)S(1)}, f32[512,256]{1,0:T(8,128)S(1)}) custom-call(s32[6]{0:T(128)S(1)} %stack.31.plan_ref, bf16[1024,1024]{1,0:T(8,128)(2,1)S(1)} %get-tuple-element.75.lead_ref, bf16[1024,1024]{1,0:T(8,128)(2,1)S(1)} %get-tuple-element.76.tail_ref, ...), custom_call_target="tpu_custom_call" | custom-call | flops 536870912 | bytes 4194304 | tf_op jit(solution)/shard_map/early_grads/pallas_call | solution.py:456
  37.5 1.0 %copy-done.7 = f32[256,1024]{1,0:T(8,128)} copy-done((f32[256,1024]{1,0:T(8,128)}, f32[256,1024]{1,0:T(8,128)S(1)}, u32[]{:S(2)}) %copy-start.7) | copy-done | bytes 1048600
  38.5 2.0 %collective-permute-start.5 = (f32[512,256]{1,0:T(8,128)S(1)}, f32[512,256]{1,0:T(8,128)S(1)}, u32[]{:S(2)}, u32[]{:S(2)}) collective-permute-start(f32[512,256]{1,0:T(8,128)S(1)} %get-tuple-element.87), channel_id=1, source_target_pairs={{0,1},{1,0},{2,3},{3,2},{4,5},{5,4},{6,7},{7,6},{8,9},{9,8},{10,11... | collective-permute-start | bytes 1572872 | tf_op jit(solution)/shard_map/ppermute | solution.py:763
  40.5 4.5 %collective-permute-start.6 = (f32[512,256]{1,0:T(8,128)S(1)}, f32[512,256]{1,0:T(8,128)S(1)}, u32[]{:S(2)}, u32[]{:S(2)}) collective-permute-start(f32[512,256]{1,0:T(8,128)S(1)} %get-tuple-element.88), channel_id=1, source_target_pairs={{0,2},{3,1},{4,6},{7,5},{8,10},{11,9},{12,14},{15,13},{16,18},{19,... | collective-permute-start | bytes 1572872 | tf_op jit(solution)/shard_map/ppermute | solution.py:762
  45.0 0.9 %collective-permute-start.7 = (f32[512,256]{1,0:T(8,128)S(1)}, f32[512,256]{1,0:T(8,128)S(1)}, u32[]{:S(2)}, u32[]{:S(2)}) collective-permute-start(f32[512,256]{1,0:T(8,128)S(1)} %get-tuple-element.88), channel_id=1, source_target_pairs={{1,2},{2,1},{5,6},{6,5},{9,10},{10,9},{13,14},{14,13},{17,18},{18,... | collective-permute-start | bytes 1572872 | tf_op jit(solution)/shard_map/ppermute | solution.py:764
  45.9 17.8 %outputs_and_terms.1 = (bf16[2048,1024]{1,0:T(8,128)(2,1)}, bf16[2048,1024]{1,0:T(8,128)(2,1)}, f32[512,256]{1,0:T(8,128)}, f32[512,256]{1,0:T(8,128)}) custom-call(s32[6]{0:T(128)} %copy-done.14, bf16[2048,1024]{1,0:T(8,128)(2,1)} %inputs_ref.7, bf16[2048,1024]{1,0:T(8,128)(2,1)} %grad_ref.7, bf16[2048,128]{1,0:T(8,128)(2,1)} %write_ref.7, ...), custom_call_target="tpu_custom_call" | custom-call | flops 2147483648 | bytes 12582912 | tf_op jit(solution)/shard_map/outputs_and_terms/pallas_call | solution.py:636
  63.8 1.4 %select_add_fusion = (f32[512,256]{1,0:T(8,128)S(1)}, f32[512,256]{1,0:T(8,128)S(1)}) fusion(f32[512,256]{1,0:T(8,128)} %get-tuple-element.97, f32[512,256]{1,0:T(8,128)S(1)} %collective-permute-done.5, pred[]{:T(512)S(6)} %or.3, f32[512,256]{1,0:T(8,128)S(1)} %collective-permute-done.6, f32[512,256]{1,0:T(8,128)S(1)} %collective-permute-done.7, ...), kind=kLoop, calls=%fused_computation | loop fusion | flops 786432 | bytes 3670017 | tf_op jit(solution)/shard_map/add | solution.py:769
  65.1 6.3 %collective-permute-start.8 = (f32[512,256]{1,0:T(8,128)S(1)}, f32[512,256]{1,0:T(8,128)S(1)}, u32[]{:S(2)}, u32[]{:S(2)}) collective-permute-start(f32[512,256]{1,0:T(8,128)S(1)} %get-tuple-element.110), channel_id=1, source_target_pairs={{0,1},{1,3},{3,2},{2,0},{4,5},{5,7},{7,6},{6,4},{8,9},{9,11},{11,1... | collective-permute-start | bytes 1572872 | tf_op jit(solution)/shard_map/ppermute | solution.py:769
  71.4 13.6 %outputs.1 = (bf16[2048,1024]{1,0:T(8,128)(2,1)}, bf16[2048,1024]{1,0:T(8,128)(2,1)}) custom-call(s32[6]{0:T(128)} %copy-done.14, bf16[2048,1024]{1,0:T(8,128)(2,1)} %inputs_ref.7, bf16[2048,1024]{1,0:T(8,128)(2,1)} %grad_ref.7, bf16[2048,128]{1,0:T(8,128)(2,1)} %write_ref.7, ...), custom_call_target="tpu_custom_call", output_to_operand_aliasing={{0}: (13, {}), {1}: (14, {})} | custom-call | flops 2147483648 | bytes 12582912 | tf_op jit(solution)/shard_map/outputs/pallas_call | solution.py:636
  85.2 0.8 fusion.4
  (40 shorter events, 0.5 us)
Async XLA Ops:
  0.6 1.0 %copy-start.1 = (bf16[2048,128]{1,0:T(8,128)(2,1)S(1)}, bf16[2048,128]{1,0:T(8,128)(2,1)}, u32[]{:S(2)}) copy-start(bf16[2048,128]{1,0:T(8,128)(2,1)} %write_ref.7) | copy-start | bytes 1572868
  1.7 1.0 %copy-start.3 = (bf16[2048,128]{1,0:T(8,128)(2,1)S(1)}, bf16[2048,128]{1,0:T(8,128)(2,1)}, u32[]{:S(2)}) copy-start(bf16[2048,128]{1,0:T(8,128)(2,1)} %read_ref.7) | copy-start | bytes 1572868
  2.7 0.9 %copy-start.12 = (f32[16,2048]{1,0:T(8,128)S(1)}, f32[16,2048]{1,0:T(8,128)}, u32[]{:S(2)}) copy-start(f32[16,2048]{1,0:T(8,128)} %ld_ref.2) | copy-start | bytes 393220
  11.0 2.9 %collective-permute-start = (f32[264,1024]{1,0:T(8,128)S(1)}, f32[264,1024]{1,0:T(8,128)S(1)}, u32[]{:S(2)}, u32[]{:S(2)}) collective-permute-start(f32[264,1024]{1,0:T(8,128)S(1)} %totals.1), channel_id=1, source_target_pairs={{0,4},{4,0},{8,12},{12,8},{16,20},{20,16},{24,28},{28,24},{1,5},{5... | collective-permute-start | bytes 3244040 | tf_op jit(solution)/shard_map/ppermute | solution.py:684
  11.6 0.9 %copy-start.13 = (f32[16,2048]{1,0:T(8,128)S(1)}, f32[16,2048]{1,0:T(8,128)}, u32[]{:S(2)}) copy-start(f32[16,2048]{1,0:T(8,128)} %ld_ref.2) | copy-start | bytes 393220
  12.5 22.7 %copy-start.14 = (s32[6]{0:T(128)}, s32[6]{0:T(128)S(1)}, u32[]{:S(2)}) copy-start(s32[6]{0:T(128)S(1)} %stack.31.plan_ref) | copy-start | bytes 76
  12.5 6.2 %copy-start.2 = (bf16[2048,128]{1,0:T(8,128)(2,1)S(1)}, bf16[2048,128]{1,0:T(8,128)(2,1)}, u32[]{:S(2)}) copy-start(bf16[2048,128]{1,0:T(8,128)(2,1)} %write_ref.7) | copy-start | bytes 1572868
  12.5 6.2 %copy-start.4 = (bf16[2048,128]{1,0:T(8,128)(2,1)S(1)}, bf16[2048,128]{1,0:T(8,128)(2,1)}, u32[]{:S(2)}) copy-start(bf16[2048,128]{1,0:T(8,128)(2,1)} %read_ref.7) | copy-start | bytes 1572868
  13.2 5.4 %copy-start.8 = (bf16[2048,128]{1,0:T(8,128)(2,1)}, bf16[2048,128]{1,0:T(8,128)(2,1)S(1)}, u32[]{:S(2)}) copy-start(bf16[2048,128]{1,0:T(8,128)(2,1)S(1)} %get-tuple-element.71.parts_ref) | copy-start | bytes 1572868
  13.3 5.4 %copy-start.9 = (f32[256,128]{1,0:T(8,128)}, f32[256,128]{1,0:T(8,128)S(1)}, u32[]{:S(2)}) copy-start(f32[256,128]{1,0:T(8,128)S(1)} %get-tuple-element.72.rows_ref) | copy-start | bytes 393220
  13.3 5.4 %copy-start.10 = (f32[32,1024]{1,0:T(8,128)}, f32[32,1024]{1,0:T(8,128)S(1)}, u32[]{:S(2)}) copy-start(f32[32,1024]{1,0:T(8,128)S(1)} %get-tuple-element.74.ranges_ref) | copy-start | bytes 393220
  13.3 5.3 %copy-start.11 = (f32[16,1024]{1,0:T(8,128)}, f32[16,1024]{1,0:T(8,128)S(1)}, u32[]{:S(2)}) copy-start(f32[16,1024]{1,0:T(8,128)S(1)} %get-tuple-element.73.decays_ref) | copy-start | bytes 196612
  13.8 4.8 %copy-start = (bf16[2048,1024]{1,0:T(8,128)(2,1)S(1)}, bf16[2048,1024]{1,0:T(8,128)(2,1)}, u32[]{:S(2)}) copy-start(bf16[2048,1024]{1,0:T(8,128)(2,1)} %inputs_ref.7) | copy-start | bytes 12582916
  14.2 18.8 %collective-permute-start.1 = (f32[72,1024]{1,0:T(8,128)S(1)}, f32[72,1024]{1,0:T(8,128)S(1)}, u32[]{:S(2)}, u32[]{:S(2)}) collective-permute-start(f32[72,1024]{1,0:T(8,128)S(1)} %get-tuple-element.116), channel_id=1, source_target_pairs={{0,8},{4,12},{8,0},{12,4},{16,24},{20,28},{24,16},{28,20},{1,9},{5... | collective-permute-start | bytes 884744 | tf_op jit(solution)/shard_map/ppermute | solution.py:703
  17.1 15.9 %collective-permute-start.2 = (f32[72,1024]{1,0:T(8,128)S(1)}, f32[72,1024]{1,0:T(8,128)S(1)}, u32[]{:S(2)}, u32[]{:S(2)}) collective-permute-start(f32[72,1024]{1,0:T(8,128)S(1)} %get-tuple-element.115), channel_id=1, source_target_pairs={{0,16},{4,20},{8,24},{12,28},{16,0},{20,4},{24,8},{28,12},{1,17},{... | collective-permute-start | bytes 884744 | tf_op jit(solution)/shard_map/ppermute | solution.py:703
  18.6 14.4 %collective-permute-start.3 = (f32[72,1024]{1,0:T(8,128)S(1)}, f32[72,1024]{1,0:T(8,128)S(1)}, u32[]{:S(2)}, u32[]{:S(2)}) collective-permute-start(f32[72,1024]{1,0:T(8,128)S(1)} %get-tuple-element.114), channel_id=1, source_target_pairs={{0,24},{4,28},{8,16},{12,20},{16,8},{20,12},{24,0},{28,4},{1,25},{... | collective-permute-start | bytes 884744 | tf_op jit(solution)/shard_map/ppermute | solution.py:703
  33.0 4.5 %copy-start.5 = (bf16[512,1024]{1,0:T(8,128)(2,1)}, bf16[512,1024]{1,0:T(8,128)(2,1)S(1)}, u32[]{:S(2)}) copy-start(bf16[512,1024]{1,0:T(8,128)(2,1)S(1)} %get-tuple-element.69.entries_ref) | copy-start | bytes 3145732
  33.0 4.5 %copy-start.6 = (bf16[512,1024]{1,0:T(8,128)(2,1)}, bf16[512,1024]{1,0:T(8,128)(2,1)S(1)}, u32[]{:S(2)}) copy-start(bf16[512,1024]{1,0:T(8,128)(2,1)S(1)} %get-tuple-element.70.afters_ref) | copy-start | bytes 3145732
  33.2 2.0 %collective-permute-start.4 = (f32[128,1024]{1,0:T(8,128)S(1)}, f32[128,1024]{1,0:T(8,128)S(1)}, u32[]{:S(2)}, u32[]{:S(2)}) collective-permute-start(f32[128,1024]{1,0:T(8,128)S(1)} %combine.1.own_ref), channel_id=1, source_target_pairs={{0,4},{4,0},{8,12},{12,8},{16,20},{20,16},{24,28},{28,24},{1,5},{5... | collective-permute-start | bytes 1572872 | tf_op jit(solution)/shard_map/ppermute | solution.py:706
  37.4 1.0 %copy-start.7 = (f32[256,1024]{1,0:T(8,128)}, f32[256,1024]{1,0:T(8,128)S(1)}, u32[]{:S(2)}) copy-start(f32[256,1024]{1,0:T(8,128)S(1)} %get-tuple-element.82.ends_ref) | copy-start | bytes 3145732
  38.5 25.3 %collective-permute-start.5 = (f32[512,256]{1,0:T(8,128)S(1)}, f32[512,256]{1,0:T(8,128)S(1)}, u32[]{:S(2)}, u32[]{:S(2)}) collective-permute-start(f32[512,256]{1,0:T(8,128)S(1)} %get-tuple-element.87), channel_id=1, source_target_pairs={{0,1},{1,0},{2,3},{3,2},{4,5},{5,4},{6,7},{7,6},{8,9},{9,8},{10,11... | collective-permute-start | bytes 1572872 | tf_op jit(solution)/shard_map/ppermute | solution.py:763
  40.5 23.3 %collective-permute-start.6 = (f32[512,256]{1,0:T(8,128)S(1)}, f32[512,256]{1,0:T(8,128)S(1)}, u32[]{:S(2)}, u32[]{:S(2)}) collective-permute-start(f32[512,256]{1,0:T(8,128)S(1)} %get-tuple-element.88), channel_id=1, source_target_pairs={{0,2},{3,1},{4,6},{7,5},{8,10},{11,9},{12,14},{15,13},{16,18},{19,... | collective-permute-start | bytes 1572872 | tf_op jit(solution)/shard_map/ppermute | solution.py:762
  45.0 18.7 %collective-permute-start.7 = (f32[512,256]{1,0:T(8,128)S(1)}, f32[512,256]{1,0:T(8,128)S(1)}, u32[]{:S(2)}, u32[]{:S(2)}) collective-permute-start(f32[512,256]{1,0:T(8,128)S(1)} %get-tuple-element.88), channel_id=1, source_target_pairs={{1,2},{2,1},{5,6},{6,5},{9,10},{10,9},{13,14},{14,13},{17,18},{18,... | collective-permute-start | bytes 1572872 | tf_op jit(solution)/shard_map/ppermute | solution.py:764
  65.1 19.9 %collective-permute-start.8 = (f32[512,256]{1,0:T(8,128)S(1)}, f32[512,256]{1,0:T(8,128)S(1)}, u32[]{:S(2)}, u32[]{:S(2)}) collective-permute-start(f32[512,256]{1,0:T(8,128)S(1)} %get-tuple-element.110), channel_id=1, source_target_pairs={{0,1},{1,3},{3,2},{2,0},{4,5},{5,7},{7,6},{6,4},{8,9},{9,11},{11,1... | collective-permute-start | bytes 1572872 | tf_op jit(solution)/shard_map/ppermute | solution.py:769
